TPU v7x, 512 devices: a whole 4x8x8 slice. The times are simulated.
512 devices in a mesh: dp: 8 (over z_lo, core), seq: 64 (over z_hi, y, x).
Axes of the slice: x: 4, y: 8, z: 8 (z_hi: 2, z_lo: 4; z = z_hi * 4 + z_lo), core: 2. Of those that a mesh axis runs over, the one named last changes fastest.
Arguments:
- value_branch: bfloat16 [512, 65536], P(None, ('dp', 'seq')), parts along dimension 1, may hold values from -6 to 6
- first_gate: bfloat16 [512, 65536], P(None, ('dp', 'seq')), parts along dimension 1, may hold values from -6 to 6
- second_gate: bfloat16 [512, 65536], P(None, ('dp', 'seq')), parts along dimension 1, may hold values from -6 to 6
- out_cotangent: bfloat16 [512, 65536], P(None, ('dp', 'seq')), parts along dimension 1, may hold values from -6 to 6
- pos_weight: float32 [64, 33], replicated, may hold values from -4 to 4
- pos_bias: float32 [64], replicated, may hold values from -3.140625 to 3.140625
- mid_weight: float32 [64, 64], replicated, may hold values from -0.75 to 0.75
- mid_bias: float32 [64], replicated, may hold values from -3.140625 to 3.140625
- out_weight: float32 [1024, 64], replicated, may hold values from -0.0234375 to 0.0234375
- decay_rates: float32 [1024], replicated, may hold values from 3.07 to 15.35
Outputs:
- value_grad: bfloat16 [512, 65536], P(None, ('dp', 'seq')), parts along dimension 1
- first_gate_grad: bfloat16 [512, 65536], P(None, ('dp', 'seq')), parts along dimension 1
- second_gate_grad: bfloat16 [512, 65536], P(None, ('dp', 'seq')), parts along dimension 1
- pos_weight_grad: float32 [512, 33], P('dp'), parts along dimension 0
- pos_bias_grad: float32 [512], P('dp'), parts along dimension 0
- mid_weight_grad: float32 [512, 64], P('dp'), parts along dimension 0
- mid_bias_grad: float32 [512], P('dp'), parts along dimension 0
- out_weight_grad: float32 [1024, 512], P('seq', 'dp'), parts along dimension 1
There are 8 independent parts, one for each index of `dp`. A program takes and returns all parts, laid end to end along the dimension named above; an argument that names none is the same for every part. Nothing has to cross between parts.
All inputs are finite; a program needn't handle non-finite values.
Results may differ from a plain program's by a relative error of at most 0.017.
Values may be sent and summed in bfloat16 or wider, within the bound.
No kernel may reach another device: no remote copies, remote signals or barrier semaphores. Data moves between devices by JAX's collectives and lax.ppermute only.
A program may use at most 64 MiB of HBM per device.

v0:
```python
import math

import jax
import jax.numpy as jnp
from jax import lax
from jax.sharding import PartitionSpec as P

RADIX = 128


def make_tables(freq_rows, radix):
    length_all = freq_rows * radix
    freq_index = jnp.arange(freq_rows, dtype=jnp.int32)
    half_index = jnp.arange(freq_rows // 2, dtype=jnp.int32)
    inner_index = jnp.arange(radix, dtype=jnp.int32)
    angle_one = (freq_index[:, None] * half_index[None, :] % freq_rows).astype(jnp.float32) * (
        2.0 * math.pi / freq_rows
    )
    angle_two = (inner_index[:, None] * inner_index[None, :] % radix).astype(jnp.float32) * (
        2.0 * math.pi / radix
    )
    angle_twid = (freq_index[:, None] * inner_index[None, :] % length_all).astype(jnp.float32) * (
        2.0 * math.pi / length_all
    )
    cos_one = jnp.cos(angle_one).astype(jnp.bfloat16)
    sin_one = jnp.sin(angle_one).astype(jnp.bfloat16)
    cos_two = jnp.cos(angle_two).astype(jnp.bfloat16)
    sin_two = jnp.sin(angle_two).astype(jnp.bfloat16)
    left_table = jnp.concatenate([cos_one, -sin_one], axis=0)
    right_fwd = jnp.concatenate(
        [jnp.concatenate([cos_two, -sin_two], axis=1), jnp.concatenate([sin_two, cos_two], axis=1)],
        axis=0,
    )
    right_inv = jnp.concatenate(
        [jnp.concatenate([cos_two, sin_two], axis=1), jnp.concatenate([-sin_two, cos_two], axis=1)],
        axis=0,
    )
    return (left_table, right_fwd, right_inv, jnp.cos(angle_twid), jnp.sin(angle_twid))


def forward_spectrum(signal, tables, freq_rows, radix):
    left_table, right_fwd, right_inv, twid_cos, twid_sin = tables
    count = signal.shape[0]
    shaped = signal.reshape(count, freq_rows // 2, radix)
    stacked = jnp.einsum("kn,rnm->rkm", left_table, shaped, preferred_element_type=jnp.float32)
    real_a = stacked[:, :freq_rows]
    imag_a = stacked[:, freq_rows:]
    real_b = (real_a * twid_cos + imag_a * twid_sin).astype(jnp.bfloat16)
    imag_b = (imag_a * twid_cos - real_a * twid_sin).astype(jnp.bfloat16)
    joined = jnp.concatenate([real_b, imag_b], axis=2)
    spectrum = jnp.einsum("rkn,nm->rkm", joined, right_fwd, preferred_element_type=jnp.float32)
    return (spectrum[:, :, :radix], spectrum[:, :, radix:])


def inverse_signal(product, tables, freq_rows, radix):
    left_table, right_fwd, right_inv, twid_cos, twid_sin = tables
    real_p, imag_p = product
    joined = jnp.concatenate([real_p, imag_p], axis=2)
    section_q = jnp.einsum("rkn,nm->rkm", joined, right_inv, preferred_element_type=jnp.float32)
    real_q = section_q[:, :, :radix]
    imag_q = section_q[:, :, radix:]
    real_r = (real_q * twid_cos - imag_q * twid_sin).astype(jnp.bfloat16)
    imag_r = (imag_q * twid_cos + real_q * twid_sin).astype(jnp.bfloat16)
    rows_both = jnp.concatenate([real_r, imag_r], axis=1)
    output = jnp.einsum("kn,rkm->rnm", left_table, rows_both, preferred_element_type=jnp.float32)
    count = real_p.shape[0]
    return (output * (1.0 / (freq_rows * radix))).reshape(count, freq_rows // 2 * radix)


def spectral_product(left, right, conj_left, conj_right):
    sign_left = -1.0 if conj_left else 1.0
    sign_right = -1.0 if conj_right else 1.0
    real_part = left[0] * right[0] - sign_left * sign_right * left[1] * right[1]
    imag_part = sign_left * left[1] * right[0] + sign_right * left[0] * right[1]
    return (real_part.astype(jnp.bfloat16), imag_part.astype(jnp.bfloat16))


def positional_features(positions, seq_len, bands):
    band_index = jnp.arange(1, bands + 1, dtype=jnp.int32)
    angles = (band_index[:, None] * positions[None, :] % seq_len).astype(jnp.float32) * (
        2.0 * math.pi / seq_len
    )
    ramp = positions.astype(jnp.float32)[None, :] / seq_len
    return jnp.concatenate([ramp, jnp.cos(angles), jnp.sin(angles)], axis=0)


def filter_network(positions, seq_len, pos_weight, pos_bias, mid_weight, mid_bias):
    bands = (pos_weight.shape[1] - 1) // 2
    features = positional_features(positions, seq_len, bands)
    pre_one = jnp.dot(pos_weight, features, precision=lax.Precision.HIGHEST) + pos_bias[:, None]
    act_one = jnp.sin(pre_one)
    pre_two = jnp.dot(mid_weight, act_one, precision=lax.Precision.HIGHEST) + mid_bias[:, None]
    act_two = jnp.sin(pre_two)
    return (features, pre_one, act_one, pre_two, act_two)


def modulation(rates, positions, seq_len):
    return jnp.exp(-rates[:, None] * positions.astype(jnp.float32)[None, :] / seq_len)


def contract_last(left, right):
    return lax.dot_general(left, right, (((1,), (1,)), ((), ())), precision=lax.Precision.HIGHEST)


def network_backward(act_grad, features, pre_one, act_one, pre_two, mid_weight):
    pre_two_grad = act_grad * jnp.cos(pre_two)
    mid_weight_part = contract_last(pre_two_grad, act_one)
    mid_bias_part = jnp.sum(pre_two_grad, axis=1)
    pre_one_grad = jnp.dot(mid_weight.T, pre_two_grad, precision=lax.Precision.HIGHEST) * jnp.cos(
        pre_one
    )
    pos_weight_part = contract_last(pre_one_grad, features)
    pos_bias_part = jnp.sum(pre_one_grad, axis=1)
    return (pos_weight_part, pos_bias_part, mid_weight_part, mid_bias_part)


def on_device(
    value_branch,
    first_gate,
    second_gate,
    out_cotangent,
    pos_weight,
    pos_bias,
    mid_weight,
    mid_bias,
    out_weight,
    decay_rates,
):
    model_width, tok_dev = value_branch.shape
    devices = lax.axis_size("seq")
    seq_len = tok_dev * devices
    channels = model_width // devices
    my_rank = lax.axis_index("seq")
    freq_rows = 2 * seq_len // RADIX
    tables = make_tables(freq_rows, RADIX)
    all_positions = jnp.arange(seq_len, dtype=jnp.int32)
    own_rates = lax.dynamic_slice_in_dim(decay_rates, my_rank * 2 * channels, 2 * channels)
    window_own = modulation(own_rates, all_positions, seq_len)
    value_ch, first_ch = (
        lax.all_to_all(value_branch, "seq", split_axis=0, concat_axis=1, tiled=True),
        lax.all_to_all(first_gate, "seq", split_axis=0, concat_axis=1, tiled=True),
    )
    local_positions = my_rank * tok_dev + jnp.arange(tok_dev, dtype=jnp.int32)
    features, pre_one, act_one, pre_two, act_two = filter_network(
        local_positions, seq_len, pos_weight, pos_bias, mid_weight, mid_bias
    )
    window_local = modulation(decay_rates, local_positions, seq_len)
    local_filters = (
        jnp.dot(out_weight, act_two, precision=lax.Precision.HIGHEST) * window_local
    ).astype(jnp.bfloat16)
    filt_ch = lax.all_to_all(local_filters, "seq", split_axis=0, concat_axis=1, tiled=True)
    filt_real, filt_imag = forward_spectrum(filt_ch, tables, freq_rows, RADIX)
    filt_real = filt_real.reshape(channels, 2, freq_rows, RADIX)
    filt_imag = filt_imag.reshape(channels, 2, freq_rows, RADIX)
    spec_one = (filt_real[:, 0], filt_imag[:, 0])
    spec_two = (filt_real[:, 1], filt_imag[:, 1])
    spec_val = forward_spectrum(value_ch, tables, freq_rows, RADIX)
    conv_one = inverse_signal(
        spectral_product(spec_one, spec_val, False, False), tables, freq_rows, RADIX
    )
    gated = (first_ch.astype(jnp.float32) * conv_one).astype(jnp.bfloat16)
    spec_gated = forward_spectrum(gated, tables, freq_rows, RADIX)
    conv_two = inverse_signal(
        spectral_product(spec_two, spec_gated, False, False), tables, freq_rows, RADIX
    )
    second_ch, cot_ch = (
        lax.all_to_all(second_gate, "seq", split_axis=0, concat_axis=1, tiled=True),
        lax.all_to_all(out_cotangent, "seq", split_axis=0, concat_axis=1, tiled=True),
    )
    cot_wide = cot_ch.astype(jnp.float32)
    second_grad_ch = (cot_wide * conv_two).astype(jnp.bfloat16)
    second_out = lax.all_to_all(second_grad_ch, "seq", split_axis=1, concat_axis=0, tiled=True)
    grad_two = (cot_wide * second_ch.astype(jnp.float32)).astype(jnp.bfloat16)
    spec_gtwo = forward_spectrum(grad_two, tables, freq_rows, RADIX)
    gated_grad = inverse_signal(
        spectral_product(spec_two, spec_gtwo, True, False), tables, freq_rows, RADIX
    )
    filt_grad_two = inverse_signal(
        spectral_product(spec_gtwo, spec_gated, False, True), tables, freq_rows, RADIX
    )
    first_grad_ch = (gated_grad * conv_one).astype(jnp.bfloat16)
    grad_one = (gated_grad * first_ch.astype(jnp.float32)).astype(jnp.bfloat16)
    spec_gone = forward_spectrum(grad_one, tables, freq_rows, RADIX)
    value_grad_ch = inverse_signal(
        spectral_product(spec_one, spec_gone, True, False), tables, freq_rows, RADIX
    ).astype(jnp.bfloat16)
    filt_grad_one = inverse_signal(
        spectral_product(spec_gone, spec_val, False, True), tables, freq_rows, RADIX
    )
    value_out, first_out = (
        lax.all_to_all(value_grad_ch, "seq", split_axis=1, concat_axis=0, tiled=True),
        lax.all_to_all(first_grad_ch, "seq", split_axis=1, concat_axis=0, tiled=True),
    )
    filt_grads = jnp.stack([filt_grad_one, filt_grad_two], axis=1).reshape(2 * channels, seq_len)
    filter_grad_ch = filt_grads * window_own / seq_len
    filter_grad_seq = lax.all_to_all(
        filter_grad_ch.astype(jnp.bfloat16), "seq", split_axis=1, concat_axis=0, tiled=True
    ).astype(filter_grad_ch.dtype)
    out_weight_grad = lax.psum_scatter(
        contract_last(filter_grad_seq, act_two), "seq", scatter_dimension=0, tiled=True
    )
    act_grad = jnp.dot(out_weight.T, filter_grad_seq, precision=lax.Precision.HIGHEST)
    partials = network_backward(act_grad, features, pre_one, act_one, pre_two, mid_weight)
    pos_weight_grad, pos_bias_grad, mid_weight_grad, mid_bias_grad = lax.psum(
        (partials[0], partials[1], partials[2], partials[3]), "seq"
    )
    return (
        value_out,
        first_out,
        second_out,
        pos_weight_grad,
        pos_bias_grad,
        mid_weight_grad,
        mid_bias_grad,
        out_weight_grad,
    )


def solution(mesh):
    in_specs = (
        P(None, ("dp", "seq")),
        P(None, ("dp", "seq")),
        P(None, ("dp", "seq")),
        P(None, ("dp", "seq")),
        P(),
        P(),
        P(),
        P(),
        P(),
        P(),
    )
    out_specs = (
        P(None, ("dp", "seq")),
        P(None, ("dp", "seq")),
        P(None, ("dp", "seq")),
        P("dp", None),
        P("dp"),
        P("dp", None),
        P("dp"),
        P("seq", "dp"),
    )
    return jax.shard_map(
        on_device, mesh=mesh, in_specs=in_specs, out_specs=out_specs, check_vma=False
    )
```

profile of v0, /device:TPU:64, one launch (start us, length us, event | category | flops | bytes accessed | tf_op | source)
XLA Modules:
  0.0 657.4 jit_solution(1359038051351091509)
XLA Ops:
  7.2 18.3 %all-to-all-start.1 = ((bf16[64,8,128]{2,1,0:T(8,128)(2,1)}), bf16[64,8,128]{2,1,0:T(8,128)(2,1)S(1)}, u32[]{:S(2)}, u32[]{:S(2)}) async-start(bf16[64,8,128]{2,1,0:T(8,128)(2,1)} %bitcast.181), calls=%async_computation.1 | async-start | bytes 262144 | tf_op jit(solution)/shard_map/all_to_all | solution.py:168
  26.4 1.6 fusion.148
  28.7 1.6 fusion.149
  30.3 10.2 %all-to-all-done.1 = bf16[64,8,128]{2,1,0:T(8,128)(2,1)S(1)} async-done(((bf16[64,8,128]{2,1,0:T(8,128)(2,1)}), bf16[64,8,128]{2,1,0:T(8,128)(2,1)S(1)}, u32[]{:S(2)}, u32[]{:S(2)}) %all-to-all-start.1) | async-done | bytes 131104 | tf_op jit(solution)/shard_map/all_to_all | solution.py:168
  40.5 5.0 all-to-all-start.5
  47.0 13.6 %all-to-all-done.5 = bf16[64,8,128]{2,1,0:T(8,128)(2,1)S(1)} async-done(((bf16[64,8,128]{2,1,0:T(8,128)(2,1)}), bf16[64,8,128]{2,1,0:T(8,128)(2,1)S(1)}, u32[]{:S(2)}, u32[]{:S(2)}) %all-to-all-start.5) | async-done | bytes 131104 | tf_op jit(solution)/shard_map/all_to_all | solution.py:140
  60.6 4.6 all-to-all-start.2
  65.6 0.8 copy.93
  66.8 13.5 %all-to-all-done.2 = bf16[64,8,128]{2,1,0:T(8,128)(2,1)S(1)} async-done(((bf16[64,8,128]{2,1,0:T(8,128)(2,1)}), bf16[64,8,128]{2,1,0:T(8,128)(2,1)S(1)}, u32[]{:S(2)}, u32[]{:S(2)}) %all-to-all-start.2) | async-done | bytes 131104 | tf_op jit(solution)/shard_map/all_to_all | solution.py:167
  80.3 4.6 all-to-all-start
  86.3 14.5 %all-to-all-done = bf16[64,16,128]{2,1,0:T(8,128)(2,1)S(1)} async-done(((bf16[64,16,128]{2,1,0:T(8,128)(2,1)}), bf16[64,16,128]{2,1,0:T(8,128)(2,1)S(1)}, u32[]{:S(2)}, u32[]{:S(2)}) %all-to-all-start) | async-done | bytes 262176 | tf_op jit(solution)/shard_map/all_to_all | solution.py:151
  100.8 5.6 all-to-all-start.3
  109.4 1.0 fusion.4
  110.5 1.3 fusion.17
  111.8 9.3 %all-to-all-done.3 = bf16[64,8,128]{2,1,0:T(8,128)(2,1)} async-done(((bf16[64,8,128]{2,1,0:T(8,128)(2,1)}), bf16[64,8,128]{2,1,0:T(8,128)(2,1)}, u32[]{:S(2)}, u32[]{:S(2)}) %all-to-all-start.3) | async-done | bytes 131104 | tf_op jit(solution)/shard_map/all_to_all | solution.py:141
  121.1 1.4 convolution_bitcast_fusion.1
  122.6 1.2 add_convert_fusion.7
  124.7 0.9 multiply_convert_fusion.1
  125.6 1.3 convolution_bitcast_fusion.3
  131.4 5.6 all-to-all-start.7
  138.1 14.0 %all-to-all-done.7 = bf16[8,64,128]{2,0,1:T(8,128)(2,1)S(1)} async-done(((bf16[8,64,128]{2,0,1:T(8,128)(2,1)}), bf16[8,64,128]{2,0,1:T(8,128)(2,1)S(1)}, u32[]{:S(2)}, u32[]{:S(2)}) %all-to-all-start.7) | async-done | bytes 131104 | tf_op jit(solution)/shard_map/all_to_all | solution.py:172
  152.1 4.6 all-to-all-start.4
  156.7 0.8 dynamic-slice_negate_fusion
  158.8 12.9 %all-to-all-done.4 = bf16[8,64,128]{2,0,1:T(8,128)(2,1)S(1)} async-done(((bf16[8,64,128]{2,0,1:T(8,128)(2,1)}), bf16[8,64,128]{2,0,1:T(8,128)(2,1)S(1)}, u32[]{:S(2)}, u32[]{:S(2)}) %all-to-all-start.4) | async-done | bytes 131104 | tf_op jit(solution)/shard_map/all_to_all | solution.py:191
  171.7 4.6 all-to-all-start.6
  177.5 0.9 copy.135
  178.4 13.0 %all-to-all-done.6 = bf16[8,64,128]{2,0,1:T(8,128)(2,1)S(1)} async-done(((bf16[8,64,128]{2,0,1:T(8,128)(2,1)}), bf16[8,64,128]{2,0,1:T(8,128)(2,1)S(1)}, u32[]{:S(2)}, u32[]{:S(2)}) %all-to-all-start.6) | async-done | bytes 131104 | tf_op jit(solution)/shard_map/all_to_all | solution.py:192
  191.4 4.6 all-to-all-start.8
  196.1 15.7 %all-to-all-done.8 = bf16[16,64,128]{2,0,1:T(8,128)(2,1)S(1)} async-done(((bf16[16,64,128]{2,0,1:T(8,128)(2,1)}), bf16[16,64,128]{2,0,1:T(8,128)(2,1)S(1)}, u32[]{:S(2)}, u32[]{:S(2)}) %all-to-all-start.8) | async-done | bytes 262176 | tf_op jit(solution)/shard_map/all_to_all | solution.py:196
  211.8 1.2 fusion.153
  214.1 429.3 %all-reduce = (f32[64,33]{0,1:T(8,128)}, f32[64]{0:T(128)}, f32[64,64]{1,0:T(8,128)}, f32[64]{0:T(128)}) all-reduce(f32[64,33]{0,1:T(8,128)S(1)} %fusion.109, f32[64]{0:T(128)S(1)} %get-tuple-element.70, f32[64,64]{1,0:T(8,128)S(1)} %fusion.152, f32[64]{0:T(128)S(1)} %get-tuple-element.72), channel_id=1, replica_groups=mesh['dp'=8,'seq'=64] {'seq'}, use_global_device_ids=true, to_apply=%region_0.1 | all-reduce | flops 6336 | bytes 50688 | tf_op jit(solution)/shard_map/psum | solution.py:204
  643.4 5.2 reduce-scatter.2.cloned.1.call-done
  (103 shorter events, 19.9 us)
Async XLA Ops:
  7.2 39.2 %copy-start = (f32[1024,64]{0,1:T(8,128)S(1)}, f32[1024,64]{0,1:T(8,128)}, u32[]{:S(2)}) copy-start(f32[1024,64]{0,1:T(8,128)} %param.18) | copy-start | bytes 786436
  7.2 33.3 %all-to-all-start.1 = ((bf16[64,8,128]{2,1,0:T(8,128)(2,1)}), bf16[64,8,128]{2,1,0:T(8,128)(2,1)S(1)}, u32[]{:S(2)}, u32[]{:S(2)}) async-start(bf16[64,8,128]{2,1,0:T(8,128)(2,1)} %bitcast.181), calls=%async_computation.1 | async-start | bytes 262144 | tf_op jit(solution)/shard_map/all_to_all | solution.py:168
  26.3 14.2 %copy-start.21 = (f32[1,128]{1,0:T(1,128)}, f32[1,128]{1,0:T(1,128)S(1)}, u32[]{:S(2)}) copy-start(f32[1,128]{1,0:T(1,128)S(1)} %convert_multiply_fusion) | copy-start | bytes 1540
  30.3 30.3 %copy-start.16 = (f32[128,64]{0,1:T(8,128)}, f32[128,64]{0,1:T(8,128)S(1)}, u32[]{:S(2)}) copy-start(f32[128,64]{0,1:T(8,128)S(1)} %get-tuple-element.66) | copy-start | bytes 98308
  40.5 44.8 %copy-start.12 = (bf16[64,8,128]{2,1,0:T(8,128)(2,1)}, bf16[64,8,128]{2,1,0:T(8,128)(2,1)S(1)}, u32[]{:S(2)}) copy-start(bf16[64,8,128]{2,1,0:T(8,128)(2,1)S(1)} %all-to-all-done.1) | copy-start | bytes 393220
  40.5 20.1 %all-to-all-start.5 = ((bf16[64,8,128]{2,1,0:T(8,128)(2,1)}), bf16[64,8,128]{2,1,0:T(8,128)(2,1)S(1)}, u32[]{:S(2)}, u32[]{:S(2)}) async-start(bf16[64,8,128]{2,1,0:T(8,128)(2,1)} %bitcast.182), calls=%async_computation.5 | async-start | bytes 262144 | tf_op jit(solution)/shard_map/all_to_all | solution.py:140
  60.6 19.7 %all-to-all-start.2 = ((bf16[64,8,128]{2,1,0:T(8,128)(2,1)}), bf16[64,8,128]{2,1,0:T(8,128)(2,1)S(1)}, u32[]{:S(2)}, u32[]{:S(2)}) async-start(bf16[64,8,128]{2,1,0:T(8,128)(2,1)} %bitcast.183), calls=%async_computation.2 | async-start | bytes 262144 | tf_op jit(solution)/shard_map/all_to_all | solution.py:167
  65.5 41.4 %copy-start.4 = (f32[128,128]{0,1:T(8,128)}, f32[128,128]{0,1:T(8,128)S(1)}, u32[]{:S(2)}) copy-start(f32[128,128]{0,1:T(8,128)S(1)} %copy.95) | copy-start | bytes 196612
  65.6 41.3 %copy-start.7 = (f32[128,128]{0,1:T(8,128)}, f32[128,128]{0,1:T(8,128)S(1)}, u32[]{:S(2)}) copy-start(f32[128,128]{0,1:T(8,128)S(1)} %copy.96) | copy-start | bytes 196612
  80.3 20.5 %all-to-all-start = ((bf16[64,16,128]{2,1,0:T(8,128)(2,1)}), bf16[64,16,128]{2,1,0:T(8,128)(2,1)S(1)}, u32[]{:S(2)}, u32[]{:S(2)}) async-start(bf16[64,16,128]{2,1,0:T(8,128)(2,1)} %bitcast.4), calls=%async_computation | async-start | bytes 524288 | tf_op jit(solution)/shard_map/all_to_all | solution.py:151
  100.8 20.3 %all-to-all-start.3 = ((bf16[64,8,128]{2,1,0:T(8,128)(2,1)}), bf16[64,8,128]{2,1,0:T(8,128)(2,1)}, u32[]{:S(2)}, u32[]{:S(2)}) async-start(bf16[64,8,128]{2,1,0:T(8,128)(2,1)} %bitcast.21), calls=%async_computation.3 | async-start | bytes 262144 | tf_op jit(solution)/shard_map/all_to_all | solution.py:141
  107.9 1.0 copy-start.1
  107.9 1.3 copy-start.5
  107.9 1.3 copy-start.8
  121.1 1.4 copy-start.3
  123.7 1.0 copy-start.10
  124.1 2.9 copy-start.6
  124.1 2.9 copy-start.9
  125.6 1.9 copy-start.2
  129.5 0.9 copy-start.13
  130.1 27.3 %copy-start.11 = (bf16[8,64,128]{2,1,0:T(8,128)(2,1)S(1)}, bf16[8,64,128]{2,1,0:T(8,128)(2,1)}, u32[]{:S(2)}) copy-start(bf16[8,64,128]{2,1,0:T(8,128)(2,1)} %get-tuple-element.68) | copy-start | bytes 393220
  131.4 20.6 %all-to-all-start.7 = ((bf16[8,64,128]{2,0,1:T(8,128)(2,1)}), bf16[8,64,128]{2,0,1:T(8,128)(2,1)S(1)}, u32[]{:S(2)}, u32[]{:S(2)}) async-start(bf16[8,64,128]{2,0,1:T(8,128)(2,1)} %copy.126), calls=%async_computation.7 | async-start | bytes 262144 | tf_op jit(solution)/shard_map/all_to_all | solution.py:172
  152.1 19.7 %all-to-all-start.4 = ((bf16[8,64,128]{2,0,1:T(8,128)(2,1)}), bf16[8,64,128]{2,0,1:T(8,128)(2,1)S(1)}, u32[]{:S(2)}, u32[]{:S(2)}) async-start(bf16[8,64,128]{2,0,1:T(8,128)(2,1)} %copy.115), calls=%async_computation.4 | async-start | bytes 262144 | tf_op jit(solution)/shard_map/all_to_all | solution.py:191
  158.8 53.0 %copy-start.17 = (f32[128,64]{0,1:T(8,128)S(1)}, f32[128,64]{0,1:T(8,128)}, u32[]{:S(2)}) copy-start(f32[128,64]{0,1:T(8,128)} %copy-done.16) | copy-start | bytes 98308
  171.7 19.7 %all-to-all-start.6 = ((bf16[8,64,128]{2,0,1:T(8,128)(2,1)}), bf16[8,64,128]{2,0,1:T(8,128)(2,1)S(1)}, u32[]{:S(2)}, u32[]{:S(2)}) async-start(bf16[8,64,128]{2,0,1:T(8,128)(2,1)} %copy.121), calls=%async_computation.6 | async-start | bytes 262144 | tf_op jit(solution)/shard_map/all_to_all | solution.py:192
  176.8 36.1 %copy-start.19 = (f32[128,64]{0,1:T(8,128)S(1)}, f32[128,64]{0,1:T(8,128)}, u32[]{:S(2)}) copy-start(f32[128,64]{0,1:T(8,128)} %get-tuple-element.67) | copy-start | bytes 98308
  177.3 36.1 %copy-start.18 = (f32[64,64]{1,0:T(8,128)S(1)}, f32[64,64]{1,0:T(8,128)}, u32[]{:S(2)}) copy-start(f32[64,64]{1,0:T(8,128)} %param.16) | copy-start | bytes 49156
  177.3 36.1 %copy-start.20 = (f32[128,64]{0,1:T(8,128)S(1)}, f32[128,64]{0,1:T(8,128)}, u32[]{:S(2)}) copy-start(f32[128,64]{0,1:T(8,128)} %get-tuple-element.65) | copy-start | bytes 98308
  177.3 36.4 %copy-start.22 = (f32[1,128]{1,0:T(1,128)S(1)}, f32[1,128]{1,0:T(1,128)}, u32[]{:S(2)}) copy-start(f32[1,128]{1,0:T(1,128)} %copy-done.21) | copy-start | bytes 1540
  177.3 36.6 %copy-start.15 = (f32[128,64]{0,1:T(8,128)S(1)}, f32[128,64]{0,1:T(8,128)}, u32[]{:S(2)}) copy-start(f32[128,64]{0,1:T(8,128)} %copy-done.14) | copy-start | bytes 98308
  191.4 20.4 %all-to-all-start.8 = ((bf16[16,64,128]{2,0,1:T(8,128)(2,1)}), bf16[16,64,128]{2,0,1:T(8,128)(2,1)S(1)}, u32[]{:S(2)}, u32[]{:S(2)}) async-start(bf16[16,64,128]{2,0,1:T(8,128)(2,1)} %copy.135), calls=%async_computation.8 | async-start | bytes 524288 | tf_op jit(solution)/shard_map/all_to_all | solution.py:196
  196.0 452.6 %reduce-scatter.2.cloned.1.call-start = ((), (), s32[]{:S(2)}) async-start(), calls=%async_computation.10 | async-start | bytes 532480 | tf_op jit(solution)/shard_map/reduce_scatter | solution.py:199
  (1 other events, 0.6 us)
Sparse Core Ops, SparseCore 0:
  213.1 435.4 reduce-scatter.1
where the time goes:
time: 658 us; the launch traced here: 657 us
  blocking collectives  429 us (65%)
  waiting for transfers between devices  122 us (19%)
  starting transfers between devices  57.7 us (9%)
  matrix products  18.1 us (3%)
  between operations  14.6 us (2%)
  local copies, waits for them, and re-layouts  8.39 us (1%)
  other arithmetic  7.39 us (1%)
    psum x1, blocking collectives, on_device(): lax.psum((partials[0], partials[1], partials[2], partials[3]), 'seq')  429 us
    all_to_all x1, starting transfers between devices, on_device(): lax.all_to_all(out_cotangent, 'seq', split_axis=0, concat_axis=1, tiled=T...  18.3 us
    all_to_all x1, waiting for transfers between devices, on_device(): lax.all_to_all(filter_grad_ch.astype(jnp.bfloat16), 'seq', split_axis=1,...  15.7 us
    all_to_all x1, waiting for transfers between devices, on_device(): lax.all_to_all(local_filters, 'seq', split_axis=0, concat_axis=1, tiled=T...  14.5 us
    all_to_all x1, waiting for transfers between devices, on_device(): lax.all_to_all(second_grad_ch, 'seq', split_axis=1, concat_axis=0, tiled=...  14 us
    all_to_all x1, waiting for transfers between devices, on_device(): lax.all_to_all(value_branch, 'seq', split_axis=0, concat_axis=1, tiled=True)  13.6 us
    all_to_all x1, waiting for transfers between devices, on_device(): lax.all_to_all(second_gate, 'seq', split_axis=0, concat_axis=1, tiled=True)  13.5 us
  transfers between devices with their start and end apart: 10, of which 10 were waited for; matrix products, arithmetic and copies ran while one was open for 3% of the time, Pallas kernels for 0%

commit v1 on v0

v1 whole, which is shorter than its diff:
```python
import math

import jax
import jax.numpy as jnp
import numpy as np
from jax import lax
from jax.experimental import pallas as pl
from jax.experimental.pallas import tpu as pltpu
from jax.sharding import Mesh
from jax.sharding import PartitionSpec as P

F32 = jnp.float32
BF16 = jnp.bfloat16
RADIX = 128
HALF_ROWS = 64
SEQLEN = HALF_ROWS * RADIX
KROWS = 80
WIDTH = 64
PE = 33
PE_PAD = 208
CHUNK = 1024
CHANNELS = 8
ROWS = 2 * CHANNELS


def dft_tables():
    n1, n2 = 2 * HALF_ROWS, RADIX
    k1 = np.arange(KROWS)[:, None]
    live = (k1 <= n1 // 2).astype(np.float64)
    angle_one = 2.0 * np.pi * ((k1 * np.arange(n1 // 2)[None, :]) % n1) / n1
    cos_one = np.cos(angle_one) * live
    sin_one = np.sin(angle_one) * live
    left = np.concatenate([cos_one, -sin_one], axis=0)
    weight = np.where((k1 == 0) | (k1 == n1 // 2), 1.0, 2.0) / (n1 * n2)
    back = np.concatenate([cos_one * weight, -sin_one * weight], axis=0).T
    grid = np.arange(n2)
    angle_two = 2.0 * np.pi * ((grid[:, None] * grid[None, :]) % n2) / n2
    cos_two, sin_two = np.cos(angle_two), np.sin(angle_two)
    right = np.block([[cos_two, -sin_two], [sin_two, cos_two]])
    right_inv = np.block([[cos_two, sin_two], [-sin_two, cos_two]])
    angle_tw = 2.0 * np.pi * ((k1 * grid[None, :]) % (n1 * n2)) / (n1 * n2)
    bf = lambda a: np.asarray(a, np.float32).astype(jnp.bfloat16)
    return (
        bf(left),
        bf(back),
        bf(right),
        bf(right_inv),
        np.cos(angle_tw).astype(np.float32),
        np.sin(angle_tw).astype(np.float32),
    )


def features():
    positions = np.arange(SEQLEN)
    bands = np.arange(1, (PE - 1) // 2 + 1)
    angles = 2.0 * np.pi * ((bands[:, None] * positions[None, :]) % SEQLEN) / SEQLEN
    ramp = positions[None, :] / SEQLEN
    return np.concatenate([ramp, np.cos(angles), np.sin(angles)], axis=0).astype(np.float32)


def np_split(value, parts):
    pieces = []
    for _ in range(parts):
        piece = value.astype(jnp.bfloat16)
        pieces.append(piece)
        value = value - piece.astype(np.float32)
    return pieces


def feature_tables():
    table = features()
    hi, mid, lo = np_split(table, 3)
    pad = np.zeros((PE_PAD - 6 * PE, SEQLEN), jnp.bfloat16)
    stack = np.concatenate([hi, mid, lo, hi, mid, hi, pad], axis=0)
    tail = np.zeros((64, SEQLEN), jnp.bfloat16)
    tail[:PE] = hi
    tail[PE] = 1.0
    return stack, tail


def poly_tables():
    top = (math.pi / 2) ** 2 * 1.0001
    nodes = (np.cos(np.pi * (np.arange(64) + 0.5) / 64) + 1) * top / 2
    root = np.sqrt(nodes)
    cheb = np.polynomial.chebyshev.Chebyshev
    sin_fit = cheb.fit(nodes, np.sin(root) / root, 4, domain=[0, top])
    cos_fit = cheb.fit(nodes, np.cos(root), 5, domain=[0, top])
    to_poly = lambda c: [float(x) for x in c.convert(kind=np.polynomial.Polynomial).coef]
    return to_poly(sin_fit), to_poly(cos_fit)


SIN_COEF, COS_COEF = poly_tables()
PI_HI = 3.140625
PI_MID = float(np.float32(int((math.pi - PI_HI) * 2**22) / 2**22))
PI_LO = float(np.float32(math.pi - PI_HI - PI_MID))


def sin_cos(value):
    turns = jnp.round(value * (1.0 / math.pi))
    rest = ((value - turns * PI_HI) - turns * PI_MID) - turns * PI_LO
    half = turns * 0.5
    sign = 1.0 - 4.0 * (half - jnp.floor(half))
    square = rest * rest

    def horner(coefs):
        total = jnp.full_like(square, coefs[-1])
        for coef in coefs[-2::-1]:
            total = total * square + coef
        return total

    return (rest * sign) * horner(SIN_COEF), sign * horner(COS_COEF)


def dot(left, right):
    return lax.dot_general(left, right, (((1,), (0,)), ((), ())), preferred_element_type=F32)


def dot_last(left, right):
    return lax.dot_general(left, right, (((1,), (1,)), ((), ())), preferred_element_type=F32)


def split_four(value):
    high = value.astype(BF16)
    low = (value - high.astype(F32)).astype(BF16)
    return high, jnp.concatenate([high, low, high, low], axis=0)


def forward_pair(signal, left, right, twid_cos, twid_sin):
    stacked = dot(left, signal)
    rows = []
    for j in range(2):
        cols = slice(j * RADIX, (j + 1) * RADIX)
        real_a, imag_a = stacked[:KROWS, cols], stacked[KROWS:, cols]
        real_b = (real_a * twid_cos + imag_a * twid_sin).astype(BF16)
        imag_b = (imag_a * twid_cos - real_a * twid_sin).astype(BF16)
        rows.append(jnp.concatenate([real_b, imag_b], axis=1))
    return dot(jnp.concatenate(rows, axis=0), right)


def inverse_pair(product, back, right_inv, twid_cos, twid_sin):
    section = dot(product, right_inv)
    cols = []
    for j in range(2):
        real_q = section[j * KROWS : (j + 1) * KROWS, :RADIX]
        imag_q = section[j * KROWS : (j + 1) * KROWS, RADIX:]
        real_r = (real_q * twid_cos - imag_q * twid_sin).astype(BF16)
        imag_r = (imag_q * twid_cos + real_q * twid_sin).astype(BF16)
        cols.append(jnp.concatenate([real_r, imag_r], axis=0))
    return dot(back, jnp.concatenate(cols, axis=1))


def spectral_product(left, right, sign_left, sign_right):
    left_re, left_im = left[:, :RADIX], left[:, RADIX:]
    right_re, right_im = right[:, :RADIX], right[:, RADIX:]
    cross = left_im * right_im
    real = left_re * right_re + cross if sign_left * sign_right < 0 else left_re * right_re - cross
    one, two = left_im * right_re, left_re * right_im
    if sign_left > 0:
        imag = one + two if sign_right > 0 else one - two
    else:
        imag = two - one
    return jnp.concatenate([real.astype(BF16), imag.astype(BF16)], axis=1)


def network_kernel(
    pe_ref, wp_ref, bp_ref, wm_ref, bm_ref, wo_ref, rate_ref, left_ref, right_ref, tc_ref, ts_ref,
    a1_ref, a2_ref, c1_ref, c2_ref, spec_ref, filt,
):
    step = pl.program_id(0)
    span = 256
    for part in range(CHUNK // span):
        cols = slice(part * span, (part + 1) * span)
        pre_one = dot(wp_ref[...], pe_ref[:, cols]) + bp_ref[...]
        act_one, cos_one = sin_cos(pre_one)
        high, stack = split_four(act_one)
        a1_ref[:, cols] = high
        c1_ref[:, cols] = cos_one.astype(BF16)
        pre_two = dot(wm_ref[...], stack) + bm_ref[...]
        act_two, cos_two = sin_cos(pre_two)
        high, stack = split_four(act_two)
        a2_ref[:, cols] = high
        c2_ref[:, cols] = cos_two.astype(BF16)
        start = (step * CHUNK + part * span).astype(F32)
        times = (lax.broadcasted_iota(jnp.int32, (ROWS, span), 1).astype(F32) + start) * (1.0 / SEQLEN)
        rows = dot(wo_ref[...], stack) * jnp.exp(-rate_ref[...] * times)
        for j in range(span // RADIX):
            base = pl.multiple_of(step * (CHUNK // RADIX * ROWS) + (part * (span // RADIX) + j) * ROWS, ROWS)
            filt[pl.ds(base, ROWS), :] = rows[:, j * RADIX : (j + 1) * RADIX]

    @pl.when(step == SEQLEN // CHUNK - 1)
    def _():
        for o in range(2):
            for pair in range(CHANNELS // 2):
                signal = jnp.concatenate(
                    [filt[pl.ds(2 * (2 * pair + j) + o, HALF_ROWS, stride=ROWS), :] for j in range(2)], axis=1
                ).astype(BF16)
                spec_ref[o, pair * 2 * KROWS : (pair + 1) * 2 * KROWS, :] = forward_pair(
                    signal, left_ref[...], right_ref[...], tc_ref[...], ts_ref[...]
                )


def spectral_kernel(
    x_ref, spec_ref, left_ref, back_ref, right_ref, inv_ref, tc_ref, ts_ref,
    y_ref, dh_ref,
    xs, ys, sv, sg2, sz, sg1, conv, dz,
):
    xs[...] = x_ref[...].astype(F32)
    tables_f = (left_ref[...], right_ref[...], tc_ref[...], ts_ref[...])
    tables_i = (back_ref[...], inv_ref[...], tc_ref[...], ts_ref[...])
    stride = 3 * CHANNELS
    pairs = range(CHANNELS // 2)

    def signal(kind, pair):
        return jnp.concatenate(
            [xs[pl.ds(kind * CHANNELS + 2 * pair + j, HALF_ROWS, stride=stride), :] for j in range(2)], axis=1
        )

    def rows(pair):
        return slice(pair * 2 * KROWS, (pair + 1) * 2 * KROWS)

    def lanes(pair):
        return slice(pair * 2 * RADIX, (pair + 1) * 2 * RADIX)

    def emit(kind, pair, value):
        for j in range(2):
            ys[pl.ds(kind * CHANNELS + 2 * pair + j, HALF_ROWS, stride=stride), :] = value[
                :, j * RADIX : (j + 1) * RADIX
            ]

    def emit_filter(o, pair, value):
        for j in range(2):
            dh_ref[pl.ds(2 * (2 * pair + j) + o, HALF_ROWS, stride=ROWS), :] = value[:, j * RADIX : (j + 1) * RADIX]

    def product(left, right, sign_left, sign_right):
        return spectral_product(left, right, sign_left, sign_right)

    for p in pairs:
        sv[rows(p), :] = forward_pair(signal(0, p).astype(BF16), *tables_f)
    for p in pairs:
        sg2[rows(p), :] = forward_pair(signal(2, p).astype(BF16), *tables_f)
    for p in pairs:
        conv[:, lanes(p)] = inverse_pair(product(spec_ref[0, rows(p), :], sv[rows(p), :], 1, 1), *tables_i)
    for p in pairs:
        dz[:, lanes(p)] = inverse_pair(product(spec_ref[1, rows(p), :], sg2[rows(p), :], -1, 1), *tables_i)
    for p in pairs:
        gated = (signal(1, p) * conv[:, lanes(p)]).astype(BF16)
        sz[rows(p), :] = forward_pair(gated, *tables_f)
    for p in pairs:
        emit(1, p, dz[:, lanes(p)] * conv[:, lanes(p)])
        grad = (dz[:, lanes(p)] * signal(1, p)).astype(BF16)
        sg1[rows(p), :] = forward_pair(grad, *tables_f)
    for p in pairs:
        emit(0, p, inverse_pair(product(spec_ref[1, rows(p), :], sz[rows(p), :], 1, 1), *tables_i))
    for p in pairs:
        emit_filter(1, p, inverse_pair(product(sg2[rows(p), :], sz[rows(p), :], 1, -1), *tables_i))
    for p in pairs:
        emit(2, p, inverse_pair(product(spec_ref[0, rows(p), :], sg1[rows(p), :], -1, 1), *tables_i))
    for p in pairs:
        emit_filter(0, p, inverse_pair(product(sg1[rows(p), :], sv[rows(p), :], 1, -1), *tables_i))
    y_ref[...] = ys[...].astype(BF16)


def gradient_kernel(
    dh_ref, a1_ref, a2_ref, c1_ref, c2_ref, tail_ref, wo_ref, wm_ref, rate_ref, out_ref, inner_ref
):
    step = pl.program_id(0)

    @pl.when(step == 0)
    def _():
        out_ref[...] = jnp.zeros_like(out_ref)
        inner_ref[...] = jnp.zeros_like(inner_ref)

    per = CHUNK // RADIX
    wide = jnp.concatenate([dh_ref[i * ROWS : (i + 1) * ROWS, :] for i in range(per)], axis=1)
    start = (step * CHUNK).astype(F32)
    times = (lax.broadcasted_iota(jnp.int32, (ROWS, CHUNK), 1).astype(F32) + start) * (1.0 / SEQLEN)
    grad = (wide * jnp.exp(-rate_ref[...] * times) * (1.0 / SEQLEN)).astype(BF16)
    out_ref[...] += dot_last(grad, a2_ref[...])
    grad_two = dot(wo_ref[...], grad) * c2_ref[...].astype(F32)
    low_two = grad_two.astype(BF16)
    grad_one = dot(wm_ref[...], low_two) * c1_ref[...].astype(F32)
    low_one = grad_one.astype(BF16)
    inner_ref[:, :WIDTH] += dot_last(low_two, a1_ref[...])
    inner_ref[:, WIDTH:] += dot_last(low_one, tail_ref[...])
    lane = lax.broadcasted_iota(jnp.int32, (WIDTH, WIDTH), 1)
    bias = jnp.sum(grad_two, axis=1, keepdims=True)
    inner_ref[:, WIDTH:] += jnp.where(lane == PE + 1, bias, 0.0)


def full(shape):
    return pl.BlockSpec(shape, lambda i: (0,) * len(shape))


def network_forward(pos_weight, pos_bias, mid_weight, mid_bias, own_weight, own_rates, tables, stack):
    left, back, right, right_inv, twid_cos, twid_sin = tables
    ph = pos_weight.astype(BF16)
    pm = (pos_weight - ph.astype(F32)).astype(BF16)
    plo = (pos_weight - ph.astype(F32) - pm.astype(F32)).astype(BF16)
    wp = jnp.concatenate([ph, ph, ph, pm, pm, plo, jnp.zeros((WIDTH, PE_PAD - 6 * PE), BF16)], axis=1)

    def doubled(weight):
        high = weight.astype(BF16)
        low = (weight - high.astype(F32)).astype(BF16)
        return jnp.concatenate([high, high, low, low], axis=1)

    block = pl.BlockSpec((WIDTH, CHUNK), lambda i: (0, i))
    args = (
        stack, wp, pos_bias[:, None], doubled(mid_weight), mid_bias[:, None], doubled(own_weight),
        own_rates[:, None], left, right, twid_cos, twid_sin,
    )
    act = jax.ShapeDtypeStruct((WIDTH, SEQLEN), BF16)
    return pl.pallas_call(
        network_kernel,
        grid=(SEQLEN // CHUNK,),
        in_specs=[pl.BlockSpec((PE_PAD, CHUNK), lambda i: (0, i))] + [full(a.shape) for a in args[1:]],
        out_specs=[block] * 4 + [full((2, CHANNELS * KROWS, 2 * RADIX))],
        out_shape=[act] * 4 + [jax.ShapeDtypeStruct((2, CHANNELS * KROWS, 2 * RADIX), F32)],
        scratch_shapes=[pltpu.VMEM((HALF_ROWS * ROWS, RADIX), F32)],
        compiler_params=pltpu.CompilerParams(vmem_limit_bytes=12 << 20),
        cost_estimate=pl.CostEstimate(flops=1 << 30, bytes_accessed=10 << 20, transcendentals=1 << 20),
    )(*args)


def spectral_chain(x, spec, tables):
    left, back, right, right_inv, twid_cos, twid_sin = tables
    spectrum = pltpu.VMEM((CHANNELS * KROWS, 2 * RADIX), F32)
    wide = pltpu.VMEM((HALF_ROWS, CHANNELS * RADIX), F32)
    return pl.pallas_call(
        spectral_kernel,
        out_shape=[
            jax.ShapeDtypeStruct(x.shape, BF16),
            jax.ShapeDtypeStruct((HALF_ROWS * ROWS, RADIX), F32),
        ],
        scratch_shapes=[pltpu.VMEM(x.shape, F32)] * 2 + [spectrum] * 4 + [wide] * 2,
        compiler_params=pltpu.CompilerParams(vmem_limit_bytes=16 << 20),
        cost_estimate=pl.CostEstimate(flops=2 << 30, bytes_accessed=4 << 20, transcendentals=0),
    )(x, spec, left, back, right, right_inv, twid_cos, twid_sin)


def network_gradient(dh, acts, tail, own_weight, mid_weight, own_rates):
    block = pl.BlockSpec((WIDTH, CHUNK), lambda i: (0, i))
    args = (own_weight.T.astype(BF16), mid_weight.T.astype(BF16), own_rates[:, None])
    return pl.pallas_call(
        gradient_kernel,
        grid=(SEQLEN // CHUNK,),
        in_specs=[pl.BlockSpec((CHUNK // RADIX * ROWS, RADIX), lambda i: (i, 0))]
        + [block] * 5
        + [full(a.shape) for a in args],
        out_specs=[full((ROWS, WIDTH)), full((WIDTH, 2 * WIDTH))],
        out_shape=[jax.ShapeDtypeStruct((ROWS, WIDTH), F32), jax.ShapeDtypeStruct((WIDTH, 2 * WIDTH), F32)],
        compiler_params=pltpu.CompilerParams(vmem_limit_bytes=12 << 20),
        cost_estimate=pl.CostEstimate(flops=1 << 29, bytes_accessed=6 << 20, transcendentals=1 << 17),
    )(dh, *acts, tail, *args)


SEQ = ("z", "y", "x")


def on_device(
    value_branch, first_gate, second_gate, out_cotangent,
    pos_weight, pos_bias, mid_weight, mid_bias, out_weight, decay_rates,
):
    devices = lax.axis_size(SEQ)
    rank = lax.axis_index(SEQ)
    tables = dft_tables()
    stack, tail = feature_tables()
    grad_two = (out_cotangent.astype(F32) * second_gate.astype(F32)).astype(BF16)
    blocks = (devices, CHANNELS, RADIX)
    sent = jnp.concatenate([a.reshape(blocks) for a in (value_branch, first_gate, grad_two)], axis=1)
    x = lax.all_to_all(sent, SEQ, 0, 0, tiled=True)

    own_weight = lax.dynamic_slice_in_dim(out_weight, rank * ROWS, ROWS)
    own_rates = lax.dynamic_slice_in_dim(decay_rates, rank * ROWS, ROWS)
    a1, a2, c1, c2, spec = network_forward(
        pos_weight, pos_bias, mid_weight, mid_bias, own_weight, own_rates, tables, stack
    )
    y, dh = spectral_chain(x.reshape(HALF_ROWS * 3 * CHANNELS, RADIX), spec, tables)
    back = lax.all_to_all(y.reshape(devices, 3 * CHANNELS, RADIX), SEQ, 0, 0, tiled=True)
    out_weight_grad, inner = network_gradient(dh, (a1, a2, c1, c2), tail, own_weight, mid_weight, own_rates)
    inner = inner + lax.ppermute(inner, "z", [(0, 1), (1, 0)])
    peers = lax.axis_size(("y", "x"))
    shares = jnp.broadcast_to(inner.astype(BF16)[None], (peers,) + inner.shape)
    inner = jnp.sum(lax.all_to_all(shares, ("y", "x"), 0, 0, tiled=True).astype(F32), axis=0)

    shape = value_branch.shape
    conv_two = back[:, :CHANNELS].reshape(shape)
    return (
        back[:, 2 * CHANNELS :].reshape(shape),
        back[:, CHANNELS : 2 * CHANNELS].reshape(shape),
        (out_cotangent.astype(F32) * conv_two.astype(F32)).astype(BF16),
        inner[:, WIDTH : WIDTH + PE],
        inner[:, WIDTH + PE],
        inner[:, :WIDTH],
        inner[:, WIDTH + PE + 1],
        out_weight_grad,
    )


def solution(mesh):
    grid = Mesh(mesh.devices.reshape(mesh.shape["dp"], 2, 8, 4), ("dp",) + SEQ)
    part = P(None, ("dp",) + SEQ)
    in_specs = (part,) * 4 + (P(),) * 6
    out_specs = (part,) * 3 + (P("dp", None), P("dp"), P("dp", None), P("dp"), P(SEQ, "dp"))
    return jax.shard_map(on_device, mesh=grid, in_specs=in_specs, out_specs=out_specs, check_vma=False)
```

time: 658 us -> 126 us (0.19)
  the two profiles are of different devices: /device:TPU:64 before, /device:TPU:6 now
where the time goes in v1:
time: 126 us; the launch traced here: 124 us
  starting transfers between devices  51.7 us (41%)
  local copies, waits for them, and re-layouts  26.6 us (21%)
  Pallas kernels  25.7 us (20%)
  waiting for transfers between devices  13.6 us (11%)
  other arithmetic  5.42 us (4%)
    unnamed x50, local copies, waits for them, and re-layouts  20.4 us
    all_to_all x1, starting transfers between devices, on_device(): x = lax.all_to_all(sent, SEQ, 0, 0, tiled=True)  19.2 us
    all_to_all x1, starting transfers between devices, on_device(): lax.all_to_all(y.reshape(devices, 3 * CHANNELS, RADIX), SEQ, 0, 0, tiled=...  15.4 us
    pallas_call x1, Pallas kernels, network_forward(): pl.pallas_call(network_kernel, grid=(SEQLEN // CHUNK,), in_specs=[pl.Bloc...  14.1 us
    all_to_all x1, waiting for transfers between devices, on_device(): lax.all_to_all(shares, ('y', 'x'), 0, 0, tiled=True).astype(F32)  11.2 us
    all_to_all x1, starting transfers between devices, on_device(): lax.all_to_all(shares, ('y', 'x'), 0, 0, tiled=True).astype(F32)  9.78 us
    ppermute x1, starting transfers between devices, on_device(): inner = inner + lax.ppermute(inner, 'z', [(0, 1), (1, 0)])  7.38 us
    pallas_call x1, Pallas kernels, network_gradient(): pl.pallas_call(gradient_kernel, grid=(SEQLEN // CHUNK,), in_specs=[pl.Blo...  6.1 us
  transfers between devices with their start and end apart: 4, of which 2 were waited for; matrix products, arithmetic and copies ran while one was open for 7% of the time, Pallas kernels for 16%

profile of v1, /device:TPU:6, one launch (start us, length us, event | category | flops | bytes accessed | tf_op | source)
XLA Modules:
  0.0 123.8 jit_solution(7790578673926908881)
XLA Ops:
  0.7 1.0 fusion.2
  1.7 1.8 %pad_maximum_fusion = bf16[64,24,128]{2,1,0:T(8,128)(2,1)} fusion(bf16[64,8,128]{2,1,0:T(8,128)(2,1)S(1)} %fusion.2, bf16[64,8,128]{2,1,0:T(8,128)(2,1)} %bitcast.26, bf16[64,8,128]{2,1,0:T(8,128)(2,1)} %bitcast.27), kind=kLoop, calls=%fused_computation.1 | loop fusion | flops 1179648 | bytes 786432 | tf_op jit(solution)/shard_map/concatenate | solution.py:369
  3.5 19.2 %all-to-all-start = ((bf16[64,24,128]{2,1,0:T(8,128)(2,1)}), bf16[64,24,128]{2,1,0:T(8,128)(2,1)}, u32[]{:S(2)}, u32[]{:S(2)}) async-start(bf16[64,24,128]{2,1,0:T(8,128)(2,1)} %pad_maximum_fusion), calls=%async_computation | async-start | bytes 786432 | tf_op jit(solution)/shard_map/all_to_all | solution.py:370
  23.4 0.8 copy.77
  25.4 0.8 copy.81
  28.1 2.0 %copy-done.9 = bf16[208,8192]{1,0:T(8,128)(2,1)S(1)} copy-done((bf16[208,8192]{1,0:T(8,128)(2,1)S(1)}, bf16[208,8192]{1,0:T(8,128)(2,1)}, u32[]{:S(2)}) %copy-start.9) | copy-done | bytes 3407896
  30.0 0.9 copy-done.10
  30.9 0.8 copy-done.13
  31.7 0.8 copy-done.15
  32.5 0.8 copy-done.17
  33.3 14.1 %shard_map.233 = (bf16[64,8192]{1,0:T(8,128)(2,1)S(1)}, bf16[64,8192]{1,0:T(8,128)(2,1)S(1)}, bf16[64,8192]{1,0:T(8,128)(2,1)S(1)}, bf16[64,8192]{1,0:T(8,128)(2,1)S(1)}, f32[2,640,256]{2,1,0:T(8,128)S(1)}) custom-call(bf16[208,8192]{1,0:T(8,128)(2,1)S(1)} %copy-done.9, bf16[64,208]{1,0:T(8,128)(2,1)S(1)} %concatenate.13.wp_ref, f32[64,1]{1,0:T(8,128)S(1)} %copy.84.bp_ref, ...), custom_call_target="tpu_custom_call" | custom-call | flops 1073741824 | bytes 10485760 | tf_op jit(solution)/shard_map/pallas_call | solution.py:312
  47.4 1.0 copy-done.2
  48.3 1.0 copy-done.4
  49.3 1.1 copy-done.20
  50.4 0.9 copy-done.11
  51.3 0.9 copy-done.12
  52.2 0.8 copy-done.18
  53.8 1.3 %copy-done.21 = f32[2,640,256]{2,1,0:T(8,128)S(1)} copy-done((f32[2,640,256]{2,1,0:T(8,128)S(1)}, f32[2,640,256]{2,1,0:T(8,128)}, u32[]{:S(2)}) %copy-start.21) | copy-done | bytes 1310744
  55.1 5.5 %shard_map.234 = (bf16[1536,128]{1,0:T(8,128)(2,1)S(1)}, f32[1024,128]{1,0:T(8,128)S(1)}) custom-call(bf16[1536,128]{1,0:T(8,128)(2,1)} %bitcast.3.x_ref, f32[2,640,256]{2,1,0:T(8,128)S(1)} %copy-done.21, bf16[160,64]{1,0:T(8,128)(2,1)S(1)} %copy-done.14, bf16[64,160]{1,0:T(8,128)(2,1)S(1)} %copy-done.19, bf16[256,256]{1,0:T(8,128)(2,1)S(1)} %copy-done.11, ...), custom_call_target="tpu_custom_call" | custom-call | flops 2147483648 | bytes 4194304 | tf_op jit(solution)/shard_map/pallas_call | solution.py:328
  60.6 0.8 copy-done.6
  62.2 15.4 %all-to-all-start.1 = ((bf16[64,24,128]{2,1,0:T(8,128)(2,1)}), bf16[64,24,128]{2,1,0:T(8,128)(2,1)}, u32[]{:S(2)}, u32[]{:S(2)}) async-start(bf16[64,24,128]{2,1,0:T(8,128)(2,1)} %bitcast.22), calls=%async_computation.1 | async-start | bytes 786432 | tf_op jit(solution)/shard_map/all_to_all | solution.py:378
  77.7 1.2 copy-done.3
  78.9 1.2 copy-done.5
  80.1 1.0 copy-done.7
  81.2 6.1 %shard_map.235 = (f32[16,64]{1,0:T(8,128)}, f32[64,128]{1,0:T(8,128)S(1)}) custom-call(f32[1024,128]{1,0:T(8,128)S(1)} %copy-done.7, bf16[64,8192]{1,0:T(8,128)(2,1)S(1)} %get-tuple-element.20.a1_ref, bf16[64,8192]{1,0:T(8,128)(2,1)S(1)} %get-tuple-element.21.a2_ref, bf16[64,8192]{1,0:T(8,128)(2,1)S(1)} %copy-done.3, bf16[64,8192]{1,0:T(8,128)(2,1)S(1)} %copy-done.5, ...), custom_call_target="tpu_custom_call" | custom-call | flops 536870912 | bytes 6291456 | tf_op jit(solution)/shard_map/pallas_call | solution.py:343
  87.3 7.4 %collective-permute-start = (f32[64,128]{1,0:T(8,128)S(1)}, f32[64,128]{1,0:T(8,128)S(1)}, u32[]{:S(2)}, u32[]{:S(2)}) collective-permute-start(f32[64,128]{1,0:T(8,128)S(1)} %get-tuple-element.24), channel_id=1, source_target_pairs={{0,32},{32,0},{1,33},{33,1},{2,34},{34,2},{3,35},{35,3},{4,36},{36... | collective-permute-start | bytes 98312 | tf_op jit(solution)/shard_map/ppermute | solution.py:380
  94.7 2.3 %collective-permute-done = f32[64,128]{1,0:T(8,128)S(1)} collective-permute-done((f32[64,128]{1,0:T(8,128)S(1)}, f32[64,128]{1,0:T(8,128)S(1)}, u32[]{:S(2)}, u32[]{:S(2)}) %collective-permute-start) | collective-permute-done | bytes 32800 | tf_op jit(solution)/shard_map/ppermute | solution.py:380
  97.0 0.9 broadcast_in_dim.23
  97.9 9.8 %all-to-all-start.2 = ((bf16[32,64,128]{2,1,0:T(8,128)(2,1)}), bf16[32,64,128]{2,1,0:T(8,128)(2,1)S(1)}, u32[]{:S(2)}, u32[]{:S(2)}) async-start(bf16[32,64,128]{2,1,0:T(8,128)(2,1)} %broadcast_in_dim.23), calls=%async_computation.2 | async-start | bytes 1048576 | tf_op jit(solution)/shard_map/all_to_all | solution.py:383
  107.7 1.7 %slice_bitcast_fusion.1 = (bf16[512,128]{1,0:T(8,128)(2,1)}, bf16[512,128]{1,0:T(8,128)(2,1)}) fusion(bf16[64,24,128]{2,1,0:T(8,128)(2,1)} %all-to-all-done.1), kind=kLoop, calls=%fused_computation.8 | loop fusion | bytes 524288 | tf_op jit(solution)/shard_map/reshape | solution.py:389
  109.4 1.7 %fusion.1 = bf16[512,128]{1,0:T(8,128)(2,1)} fusion(bf16[512,128]{1,0:T(8,128)(2,1)} %param.21, bf16[64,24,128]{2,1,0:T(8,128)(2,1)} %all-to-all-done.1), kind=kLoop, calls=%fused_computation.5 | loop fusion | flops 262144 | bytes 393216 | tf_op jit(solution)/shard_map/convert_element_type | solution.py:390
  111.1 11.2 %all-to-all-done.2 = bf16[32,64,128]{2,1,0:T(8,128)(2,1)S(1)} async-done(((bf16[32,64,128]{2,1,0:T(8,128)(2,1)}), bf16[32,64,128]{2,1,0:T(8,128)(2,1)S(1)}, u32[]{:S(2)}, u32[]{:S(2)}) %all-to-all-start.2) | async-done | bytes 524320 | tf_op jit(solution)/shard_map/all_to_all | solution.py:383
  (54 shorter events, 6.9 us)
Async XLA Ops:
  0.6 23.6 %copy-start = (f32[1024,64]{0,1:T(8,128)S(1)}, f32[1024,64]{0,1:T(8,128)}, u32[]{:S(2)}) copy-start(f32[1024,64]{0,1:T(8,128)} %param.26) | copy-start | bytes 786436
  0.6 49.8 %copy-start.14 = (bf16[160,64]{1,0:T(8,128)(2,1)S(1)}, bf16[160,64]{1,0:T(8,128)(2,1)}, u32[]{:S(2)}) copy-start(bf16[160,64]{1,0:T(8,128)(2,1)} %constant.46.clone.left_ref) | copy-start | bytes 61444
  0.7 49.8 %copy-start.16 = (f32[80,128]{1,0:T(8,128)S(1)}, f32[80,128]{1,0:T(8,128)}, u32[]{:S(2)}) copy-start(f32[80,128]{1,0:T(8,128)} %constant.48.clone.tc_ref) | copy-start | bytes 122884
  3.5 46.9 %all-to-all-start = ((bf16[64,24,128]{2,1,0:T(8,128)(2,1)}), bf16[64,24,128]{2,1,0:T(8,128)(2,1)}, u32[]{:S(2)}, u32[]{:S(2)}) async-start(bf16[64,24,128]{2,1,0:T(8,128)(2,1)} %pad_maximum_fusion), calls=%async_computation | async-start | bytes 786432 | tf_op jit(solution)/shard_map/all_to_all | solution.py:370
  28.1 2.0 %copy-start.9 = (bf16[208,8192]{1,0:T(8,128)(2,1)S(1)}, bf16[208,8192]{1,0:T(8,128)(2,1)}, u32[]{:S(2)}) copy-start(bf16[208,8192]{1,0:T(8,128)(2,1)} %constant.45.clone.pe_ref) | copy-start | bytes 10223620
  30.0 0.9 copy-start.10
  30.9 0.8 copy-start.13
  31.7 0.8 copy-start.15
  32.5 0.8 copy-start.17
  47.4 1.0 copy-start.2
  48.3 1.0 copy-start.4
  49.3 1.1 copy-start.20
  50.4 0.9 copy-start.11
  51.3 0.9 copy-start.12
  52.2 0.8 copy-start.18
  53.0 0.8 copy-start.19
  53.8 1.3 %copy-start.21 = (f32[2,640,256]{2,1,0:T(8,128)S(1)}, f32[2,640,256]{2,1,0:T(8,128)}, u32[]{:S(2)}) copy-start(f32[2,640,256]{2,1,0:T(8,128)} %copy-done.20) | copy-start | bytes 3932164
  55.1 22.6 %copy-start.1 = (bf16[64,8192]{1,0:T(8,128)(2,1)S(1)}, bf16[64,8192]{1,0:T(8,128)(2,1)}, u32[]{:S(2)}) copy-start(bf16[64,8192]{1,0:T(8,128)(2,1)} %constant.52.clone.tail_ref) | copy-start | bytes 3145732
  60.6 0.8 copy-start.6
  61.4 0.8 copy-start.8
  62.2 34.8 %all-to-all-start.1 = ((bf16[64,24,128]{2,1,0:T(8,128)(2,1)}), bf16[64,24,128]{2,1,0:T(8,128)(2,1)}, u32[]{:S(2)}, u32[]{:S(2)}) async-start(bf16[64,24,128]{2,1,0:T(8,128)(2,1)} %bitcast.22), calls=%async_computation.1 | async-start | bytes 786432 | tf_op jit(solution)/shard_map/all_to_all | solution.py:378
  77.7 1.2 copy-start.3
  78.9 1.2 copy-start.5
  80.1 1.0 copy-start.7
  87.3 9.7 %collective-permute-start = (f32[64,128]{1,0:T(8,128)S(1)}, f32[64,128]{1,0:T(8,128)S(1)}, u32[]{:S(2)}, u32[]{:S(2)}) collective-permute-start(f32[64,128]{1,0:T(8,128)S(1)} %get-tuple-element.24), channel_id=1, source_target_pairs={{0,32},{32,0},{1,33},{33,1},{2,34},{34,2},{3,35},{35,3},{4,36},{36... | collective-permute-start | bytes 98312 | tf_op jit(solution)/shard_map/ppermute | solution.py:380
  97.9 24.3 %all-to-all-start.2 = ((bf16[32,64,128]{2,1,0:T(8,128)(2,1)}), bf16[32,64,128]{2,1,0:T(8,128)(2,1)S(1)}, u32[]{:S(2)}, u32[]{:S(2)}) async-start(bf16[32,64,128]{2,1,0:T(8,128)(2,1)} %broadcast_in_dim.23), calls=%async_computation.2 | async-start | bytes 1048576 | tf_op jit(solution)/shard_map/all_to_all | solution.py:383
  122.4 1.5 %copy-start.22 = (f32[64,128]{1,0:T(8,128)}, f32[64,128]{1,0:T(8,128)S(1)}, u32[]{:S(2)}) copy-start(f32[64,128]{1,0:T(8,128)S(1)} %convert_reduce_fusion) | copy-start | bytes 98308

commit v2 on v1

v2 whole, which is shorter than its diff:
```python
import math

import jax
import jax.numpy as jnp
import numpy as np
from jax import lax
from jax.experimental import pallas as pl
from jax.experimental.pallas import tpu as pltpu
from jax.sharding import Mesh
from jax.sharding import PartitionSpec as P

F32 = jnp.float32
BF16 = jnp.bfloat16
RADIX = 128
HALF_ROWS = 64
SEQLEN = HALF_ROWS * RADIX
KROWS = 80
WIDTH = 64
PE = 33
PE_BLOCK = 40
CHUNK = 1024
CHANNELS = 8
ROWS = 2 * CHANNELS
SHARE = 56
DATA = 3 * CHANNELS
SEND = DATA + SHARE
VMEM_BYTES = 60 << 20
CHAIN_BYTES = 60 << 20


def dft_tables():
    n1, n2 = 2 * HALF_ROWS, RADIX
    k1 = np.arange(KROWS)[:, None]
    live = (k1 <= n1 // 2).astype(np.float64)
    angle_one = 2.0 * np.pi * ((k1 * np.arange(n1 // 2)[None, :]) % n1) / n1
    cos_one = np.cos(angle_one) * live
    sin_one = np.sin(angle_one) * live
    left = np.concatenate([cos_one, -sin_one], axis=0)
    weight = np.where((k1 == 0) | (k1 == n1 // 2), 1.0, 2.0) / (n1 * n2)
    back = np.concatenate([cos_one * weight, -sin_one * weight], axis=0).T
    grid = np.arange(n2)
    angle_two = 2.0 * np.pi * ((grid[:, None] * grid[None, :]) % n2) / n2
    cos_two, sin_two = np.cos(angle_two), np.sin(angle_two)
    right = np.block([[cos_two, -sin_two], [sin_two, cos_two]])
    right_inv = np.block([[cos_two, sin_two], [-sin_two, cos_two]])
    angle_tw = 2.0 * np.pi * ((k1 * grid[None, :]) % (n1 * n2)) / (n1 * n2)
    bf = lambda a: np.asarray(a, np.float32).astype(jnp.bfloat16)
    return (
        bf(left),
        bf(back),
        bf(right),
        bf(right_inv),
        np.cos(angle_tw).astype(np.float32),
        np.sin(angle_tw).astype(np.float32),
    )


def features():
    positions = np.arange(SEQLEN)
    bands = np.arange(1, (PE - 1) // 2 + 1)
    angles = 2.0 * np.pi * ((bands[:, None] * positions[None, :]) % SEQLEN) / SEQLEN
    ramp = positions[None, :] / SEQLEN
    return np.concatenate([ramp, np.cos(angles), np.sin(angles)], axis=0).astype(np.float32)


def np_split(value, parts):
    pieces = []
    for _ in range(parts):
        piece = value.astype(jnp.bfloat16)
        pieces.append(piece)
        value = value - piece.astype(np.float32)
    return pieces


def feature_tables():
    table = np.zeros((PE_BLOCK, SEQLEN), np.float32)
    table[:PE] = features()
    table[PE] = 1.0
    pieces = np_split(table, 3)
    pad = np.zeros((2 * WIDTH - 3 * PE_BLOCK, SEQLEN), jnp.bfloat16)
    return np.concatenate(pieces + [pad], axis=0), pieces[0]


def poly_tables():
    top = math.pi**2 * 1.0001
    nodes = (np.cos(np.pi * (np.arange(64) + 0.5) / 64) + 1) * top / 2
    root = np.sqrt(nodes)
    cheb = np.polynomial.chebyshev.Chebyshev
    sin_fit = cheb.fit(nodes, math.sqrt(2) * np.sin(root / 2) / root, 4, domain=[0, top])
    cos_fit = cheb.fit(nodes, math.sqrt(2) * np.cos(root / 2), 4, domain=[0, top])
    to_poly = lambda c: [float(x) for x in c.convert(kind=np.polynomial.Polynomial).coef]
    return to_poly(sin_fit), to_poly(cos_fit)


SIN_COEF, COS_COEF = poly_tables()
TURN_HI = 6.28125
TURN_LO = float(np.float32(2 * math.pi - TURN_HI))


def sin_cos(value):
    turns = jnp.round(value * (0.5 / math.pi))
    rest = (value - turns * TURN_HI) - turns * TURN_LO
    square = rest * rest

    def horner(coefs):
        total = square * coefs[-1] + coefs[-2]
        for coef in coefs[-3::-1]:
            total = total * square + coef
        return total

    half = rest * horner(SIN_COEF)
    return half * horner(COS_COEF), 1.0 - half * half


def dot(left, right):
    return lax.dot_general(left, right, (((1,), (0,)), ((), ())), preferred_element_type=F32)


def dot_last(left, right):
    return lax.dot_general(left, right, (((1,), (1,)), ((), ())), preferred_element_type=F32)


def split_two(value):
    high = value.astype(BF16)
    return high, (value - high.astype(F32)).astype(BF16)


def forward_pair(signal, left, right, twid_cos, twid_sin):
    stacked = dot(left, signal)
    rows = []
    for j in range(2):
        cols = slice(j * RADIX, (j + 1) * RADIX)
        real_a, imag_a = stacked[:KROWS, cols], stacked[KROWS:, cols]
        real_b = (real_a * twid_cos + imag_a * twid_sin).astype(BF16)
        imag_b = (imag_a * twid_cos - real_a * twid_sin).astype(BF16)
        rows.append(jnp.concatenate([real_b, imag_b], axis=1))
    return dot(jnp.concatenate(rows, axis=0), right)


def inverse_pair(product, back, right_inv, twid_cos, twid_sin):
    section = dot(product, right_inv)
    cols = []
    for j in range(2):
        real_q = section[j * KROWS : (j + 1) * KROWS, :RADIX]
        imag_q = section[j * KROWS : (j + 1) * KROWS, RADIX:]
        real_r = (real_q * twid_cos - imag_q * twid_sin).astype(BF16)
        imag_r = (imag_q * twid_cos + real_q * twid_sin).astype(BF16)
        cols.append(jnp.concatenate([real_r, imag_r], axis=0))
    return dot(back, jnp.concatenate(cols, axis=1))


def spectral_product(left, right, sign_left, sign_right):
    left_re, left_im = left[:, :RADIX], left[:, RADIX:]
    right_re, right_im = right[:, :RADIX], right[:, RADIX:]
    cross = left_im * right_im
    real = left_re * right_re + cross if sign_left * sign_right < 0 else left_re * right_re - cross
    one, two = left_im * right_re, left_re * right_im
    if sign_left > 0:
        imag = one + two if sign_right > 0 else one - two
    else:
        imag = two - one
    return jnp.concatenate([real.astype(BF16), imag.astype(BF16)], axis=1)


def pack_kernel(v_hbm, x1_hbm, x2_hbm, cot_hbm, out_hbm, x2, cot, grad, sems):
    loads = [pltpu.make_async_copy(cot_hbm, cot, sems.at[0]), pltpu.make_async_copy(x2_hbm, x2, sems.at[1])]
    moves = [
        pltpu.make_async_copy(v_hbm, out_hbm.at[:, pl.ds(0, CHANNELS), :], sems.at[2]),
        pltpu.make_async_copy(x1_hbm, out_hbm.at[:, pl.ds(CHANNELS, CHANNELS), :], sems.at[3]),
    ]
    for copy in loads + moves:
        copy.start()
    for copy in loads:
        copy.wait()
    grad[...] = (cot[...].astype(F32) * x2[...].astype(F32)).astype(BF16)
    last = pltpu.make_async_copy(grad, out_hbm.at[:, pl.ds(2 * CHANNELS, CHANNELS), :], sems.at[4])
    last.start()
    for copy in moves + [last]:
        copy.wait()


def network_kernel(
    pe_ref, ramp_ref, left_ref, right_ref, tc_ref, ts_ref,
    pos_hbm, pos_bias_hbm, mid_hbm, mid_bias_hbm, out_hbm, rate_hbm,
    act_ref, cos_ref, spec_ref, own_ref, own_rate_ref,
    filt, square, wp, wm, wo, bias, decay,
    pos_ref, pos_bias_ref, mid_ref, mid_bias_ref, out_ref, rate_ref, sems,
):
    step = pl.program_id(0)

    @pl.when(step == 0)
    def _():
        sources = (pos_hbm, pos_bias_hbm, mid_hbm, mid_bias_hbm, out_hbm, rate_hbm)
        targets = (pos_ref, pos_bias_ref, mid_ref, mid_bias_ref, out_ref, rate_ref)
        copies = [pltpu.make_async_copy(src, dst, sems.at[i]) for i, (src, dst) in enumerate(zip(sources, targets))]
        for copy in copies:
            copy.start()
        for copy in copies:
            copy.wait()
        rank = lax.axis_index(SEQ)
        lane = pl.multiple_of(rank // 8 * RADIX, RADIX)
        first = pl.multiple_of(rank % 8 * ROWS, ROWS)

        square[...] = jnp.zeros_like(square)
        for i in range(3):
            square[i * PE_BLOCK : i * PE_BLOCK + PE, :WIDTH] = pos_ref[...]
            square[i * PE_BLOCK + PE : i * PE_BLOCK + PE + 1, :WIDTH] = pos_bias_ref[...]
        wp[...] = jnp.concatenate(split_two(square[...].T[:WIDTH, :]), axis=0)

        square[...] = jnp.zeros_like(square)
        square[:WIDTH, :WIDTH] = mid_ref[...]
        own_ref[WIDTH:, :] = square[...].T[:WIDTH, :].astype(BF16)
        square[:WIDTH, WIDTH:] = mid_ref[...]
        wm[...] = jnp.concatenate(split_two(square[:WIDTH, :]), axis=0)

        square[:, :WIDTH] = jnp.broadcast_to(mid_bias_ref[...], (RADIX, WIDTH))
        bias[...] = square[...].T[:WIDTH, :]

        square[...] = jnp.broadcast_to(rate_ref[:, pl.ds(lane, RADIX)], (RADIX, RADIX)).T
        decay[...] = square[pl.ds(first, ROWS), :]
        own_rate_ref[...] = decay[...]

        block = out_ref[:, pl.ds(lane, RADIX)]
        square[...] = jnp.concatenate([block, block], axis=0).T
        mine = square[pl.ds(first, ROWS), :]
        wo[...] = jnp.concatenate(split_two(mine), axis=0)
        square[...] = jnp.zeros_like(square)
        square[:ROWS, :] = mine
        own_ref[:WIDTH, :] = square[...].T[:WIDTH, :].astype(BF16)

    span = 256
    parts = [slice(p * span, (p + 1) * span) for p in range(CHUNK // span)]
    wide_bias = jnp.concatenate([bias[...]] * (span // RADIX), axis=1)
    wide_rate = jnp.concatenate([decay[...]] * (span // RADIX), axis=1)
    for part, cols in enumerate(parts):
        both = dot(wp[...], pe_ref[:, cols])
        act, slope = sin_cos(both[:WIDTH] + both[WIDTH:])
        pieces = split_two(act)
        act_ref[:WIDTH, cols] = pieces[0]
        cos_ref[:WIDTH, cols] = slope.astype(BF16)
        both = dot(wm[...], jnp.concatenate(pieces, axis=0))
        act, slope = sin_cos(both[:WIDTH] + both[WIDTH:] + wide_bias)
        pieces = split_two(act)
        act_ref[WIDTH:, cols] = pieces[0]
        cos_ref[WIDTH:, cols] = slope.astype(BF16)
        both = dot(wo[...], jnp.concatenate(pieces, axis=0))
        rows = (both[:ROWS] + both[ROWS:]) * jnp.exp(-wide_rate * ramp_ref[:, cols])
        for j in range(span // RADIX):
            base = pl.multiple_of(step * (CHUNK // RADIX * ROWS) + (part * (span // RADIX) + j) * ROWS, ROWS)
            filt[pl.ds(base, ROWS), :] = rows[:, j * RADIX : (j + 1) * RADIX]

    @pl.when(step == SEQLEN // CHUNK - 1)
    def _():
        for o in range(2):
            for pair in range(CHANNELS // 2):
                signal = jnp.concatenate(
                    [filt[pl.ds(2 * (2 * pair + j) + o, HALF_ROWS, stride=ROWS), :] for j in range(2)], axis=1
                ).astype(BF16)
                spec_ref[o, pair * 2 * KROWS : (pair + 1) * 2 * KROWS, :] = forward_pair(
                    signal, left_ref[...], right_ref[...], tc_ref[...], ts_ref[...]
                )


def chain_kernel(
    x_ref, left_ref, back_ref, right_ref, inv_ref, tc_ref, ts_ref, own_ref, rate_ref, ramp_ref,
    spec, act_hbm, cos_hbm, tail_hbm,
    y_ref, out_ref,
    xs, ys, sv, sg2, sz, sg1, conv, dz, dh, act, cos, acc, share, sems,
):
    copies = [
        pltpu.make_async_copy(cos_hbm, cos, sems.at[0]),
        pltpu.make_async_copy(act_hbm, act.at[pl.ds(0, 2 * WIDTH)], sems.at[1]),
        pltpu.make_async_copy(tail_hbm, act.at[pl.ds(2 * WIDTH, PE_BLOCK)], sems.at[2]),
    ]
    for copy in copies:
        copy.start()
    xs[...] = x_ref[...].astype(F32)
    tables_f = (left_ref[...], right_ref[...], tc_ref[...], ts_ref[...])
    tables_i = (back_ref[...], inv_ref[...], tc_ref[...], ts_ref[...])
    pairs = range(CHANNELS // 2)

    def signal(kind, pair):
        return jnp.concatenate(
            [xs[pl.ds(kind * CHANNELS + 2 * pair + j, HALF_ROWS, stride=DATA), :] for j in range(2)], axis=1
        )

    def rows(pair):
        return slice(pair * 2 * KROWS, (pair + 1) * 2 * KROWS)

    def lanes(pair):
        return slice(pair * 2 * RADIX, (pair + 1) * 2 * RADIX)

    def emit(kind, pair, value):
        for j in range(2):
            ys[pl.ds(kind * CHANNELS + 2 * pair + j, HALF_ROWS, stride=SEND), :] = value[
                :, j * RADIX : (j + 1) * RADIX
            ]

    def emit_filter(o, pair, value):
        for j in range(2):
            dh[pl.ds(2 * (2 * pair + j) + o, HALF_ROWS, stride=ROWS), :] = value[:, j * RADIX : (j + 1) * RADIX]

    for p in pairs:
        sv[rows(p), :] = forward_pair(signal(0, p).astype(BF16), *tables_f)
    for p in pairs:
        sg2[rows(p), :] = forward_pair(signal(2, p).astype(BF16), *tables_f)
    for p in pairs:
        conv[:, lanes(p)] = inverse_pair(spectral_product(spec[0, rows(p), :], sv[rows(p), :], 1, 1), *tables_i)
    for p in pairs:
        dz[:, lanes(p)] = inverse_pair(spectral_product(spec[1, rows(p), :], sg2[rows(p), :], -1, 1), *tables_i)
    for p in pairs:
        gated = (signal(1, p) * conv[:, lanes(p)]).astype(BF16)
        sz[rows(p), :] = forward_pair(gated, *tables_f)
    for p in pairs:
        emit(1, p, dz[:, lanes(p)] * conv[:, lanes(p)])
        grad = (dz[:, lanes(p)] * signal(1, p)).astype(BF16)
        sg1[rows(p), :] = forward_pair(grad, *tables_f)
    for p in pairs:
        emit_filter(1, p, inverse_pair(spectral_product(sg2[rows(p), :], sz[rows(p), :], 1, -1), *tables_i))
    for p in pairs:
        emit_filter(0, p, inverse_pair(spectral_product(sg1[rows(p), :], sv[rows(p), :], 1, -1), *tables_i))
    for p in pairs:
        emit(0, p, inverse_pair(spectral_product(spec[1, rows(p), :], sz[rows(p), :], 1, 1), *tables_i))
    for p in pairs:
        emit(2, p, inverse_pair(spectral_product(spec[0, rows(p), :], sg1[rows(p), :], -1, 1), *tables_i))
    for copy in copies:
        copy.wait()

    acc[...] = jnp.zeros_like(acc)
    per = CHUNK // RADIX
    wide_rate = jnp.concatenate([rate_ref[...]] * per, axis=1)
    for step in range(SEQLEN // CHUNK):
        cols = slice(step * CHUNK, (step + 1) * CHUNK)
        wide = jnp.concatenate([dh[(step * per + i) * ROWS : (step * per + i + 1) * ROWS, :] for i in range(per)], axis=1)
        grad = (wide * (jnp.exp(-wide_rate * ramp_ref[:, cols]) * (1.0 / SEQLEN))).astype(BF16)
        low_two = (dot(own_ref[:WIDTH, :ROWS], grad) * cos[WIDTH:, cols].astype(F32)).astype(BF16)
        low_one = (dot(own_ref[WIDTH:, :WIDTH], low_two) * cos[:WIDTH, cols].astype(F32)).astype(BF16)
        acc[...] += dot_last(act[:, cols], jnp.concatenate([low_two, low_one, grad], axis=0))
    out_ref[...] = acc[WIDTH : 2 * WIDTH, 2 * WIDTH :].T
    half = WIDTH // 2
    tail = 2 * WIDTH
    share[:half, :WIDTH] = acc[:half, :WIDTH]
    share[:half, WIDTH:] = acc[half:WIDTH, :WIDTH]
    share[half:, :WIDTH] = acc[tail : tail + 24, WIDTH : 2 * WIDTH]
    share[half : half + 16, WIDTH:] = acc[tail + 24 : tail + 40, WIDTH : 2 * WIDTH]
    share[half + 16 :, WIDTH:] = acc[tail + 32 : tail + 40, :WIDTH]
    for i in range(HALF_ROWS):
        ys[i * SEND + DATA : (i + 1) * SEND, :] = share[...]
    y_ref[...] = ys[...].astype(BF16)


def finish_kernel(back_ref, cot_ref, value_ref, first_ref, second_ref, pos_ref, pos_bias_ref, mid_ref, mid_bias_ref, total):
    step = pl.program_id(0)
    value_ref[...] = back_ref[:, 2 * CHANNELS : DATA, :]
    first_ref[...] = back_ref[:, CHANNELS : 2 * CHANNELS, :]
    second_ref[...] = (cot_ref[...].astype(F32) * back_ref[:, :CHANNELS, :].astype(F32)).astype(BF16)
    part = jnp.sum(back_ref[:, DATA:, :].astype(F32), axis=0)

    @pl.when(step == 0)
    def _():
        total[...] = part

    @pl.when(step > 0)
    def _():
        total[...] += part

    @pl.when(step == pl.num_programs(0) - 1)
    def _():
        half = WIDTH // 2
        mid_ref[...] = jnp.concatenate([total[:half, :WIDTH], total[:half, WIDTH:]], axis=0).T
        pos_ref[:24, :] = total[half:, :WIDTH]
        pos_ref[24:, :] = total[half : half + PE - 24, WIDTH:]
        pos_bias_ref[...] = total[half + PE - 24 : half + PE - 23, WIDTH:]
        mid_bias_ref[...] = total[half + 17 : half + 18, WIDTH:]


def full(shape):
    return pl.BlockSpec(shape, lambda i: (0,) * len(shape))


def params(limit=VMEM_BYTES):
    return pltpu.CompilerParams(vmem_limit_bytes=limit)


def pack(value, first, second, cot):
    anywhere = pl.BlockSpec(memory_space=pltpu.HBM)
    buffer = pltpu.VMEM(value.shape, BF16)
    return pl.pallas_call(
        pack_kernel,
        in_specs=[anywhere] * 4,
        out_specs=anywhere,
        out_shape=jax.ShapeDtypeStruct((value.shape[0], DATA, RADIX), BF16),
        scratch_shapes=[buffer] * 3 + [pltpu.SemaphoreType.DMA((5,))],
        compiler_params=params(),
        cost_estimate=pl.CostEstimate(flops=1 << 17, bytes_accessed=1 << 20, transcendentals=0),
    )(value, first, second, cot)


def network_forward(pos_weight, pos_bias, mid_weight, mid_bias, out_weight, decay_rates, tables, stack, ramp):
    left, back, right, right_inv, twid_cos, twid_sin = tables
    block = pl.BlockSpec((2 * WIDTH, CHUNK), lambda i: (0, i))
    tabs = (left, right, twid_cos, twid_sin)
    args = (pos_weight.T, pos_bias[None, :], mid_weight, mid_bias[None, :], out_weight.T, decay_rates[None, :])
    outs = [
        jax.ShapeDtypeStruct((2 * WIDTH, SEQLEN), BF16),
        jax.ShapeDtypeStruct((2 * WIDTH, SEQLEN), BF16),
        jax.ShapeDtypeStruct((2, CHANNELS * KROWS, 2 * RADIX), F32),
        jax.ShapeDtypeStruct((2 * WIDTH, RADIX), BF16),
        jax.ShapeDtypeStruct((ROWS, RADIX), F32),
    ]
    return pl.pallas_call(
        network_kernel,
        grid=(SEQLEN // CHUNK,),
        in_specs=[block, pl.BlockSpec((1, CHUNK), lambda i: (0, i))]
        + [full(a.shape) for a in tabs]
        + [pl.BlockSpec(memory_space=pltpu.HBM)] * len(args),
        out_specs=[block] * 2 + [full(o.shape) for o in outs[2:]],
        out_shape=outs,
        scratch_shapes=[
            pltpu.VMEM((HALF_ROWS * ROWS, RADIX), F32),
            pltpu.VMEM((RADIX, RADIX), F32),
            pltpu.VMEM((2 * WIDTH, 2 * WIDTH), BF16),
            pltpu.VMEM((2 * WIDTH, 2 * WIDTH), BF16),
            pltpu.VMEM((2 * ROWS, 2 * WIDTH), BF16),
            pltpu.VMEM((WIDTH, RADIX), F32),
            pltpu.VMEM((ROWS, RADIX), F32),
        ]
        + [pltpu.VMEM(a.shape, F32) for a in args]
        + [pltpu.SemaphoreType.DMA((len(args),))],
        compiler_params=params(),
        cost_estimate=pl.CostEstimate(flops=1 << 30, bytes_accessed=10 << 20, transcendentals=1 << 20),
    )(stack, ramp, *tabs, *args)


def chain(x, net, tables, tail, ramp):
    act, cos, spec, own, own_rate = net
    left, back, right, right_inv, twid_cos, twid_sin = tables
    spectrum = pltpu.VMEM((CHANNELS * KROWS, 2 * RADIX), F32)
    wide = pltpu.VMEM((HALF_ROWS, CHANNELS * RADIX), F32)
    tall = 2 * WIDTH + PE_BLOCK
    anywhere = pl.BlockSpec(memory_space=pltpu.HBM)
    within = pl.BlockSpec(memory_space=pltpu.VMEM)
    return pl.pallas_call(
        chain_kernel,
        in_specs=[within] * 11 + [anywhere] * 3,
        out_specs=[within] * 2,
        out_shape=[
            jax.ShapeDtypeStruct((HALF_ROWS * SEND, RADIX), BF16),
            jax.ShapeDtypeStruct((ROWS, WIDTH), F32),
        ],
        scratch_shapes=[pltpu.VMEM(x.shape, F32), pltpu.VMEM((HALF_ROWS * SEND, RADIX), F32)]
        + [spectrum] * 4
        + [wide] * 2
        + [
            pltpu.VMEM((HALF_ROWS * ROWS, RADIX), F32),
            pltpu.VMEM((tall, SEQLEN), BF16),
            pltpu.VMEM((2 * WIDTH, SEQLEN), BF16),
            pltpu.VMEM((tall, 2 * WIDTH + ROWS), F32),
            pltpu.VMEM((SHARE, RADIX), F32),
            pltpu.SemaphoreType.DMA((3,)),
        ],
        compiler_params=params(CHAIN_BYTES),
        cost_estimate=pl.CostEstimate(flops=3 << 30, bytes_accessed=8 << 20, transcendentals=1 << 17),
    )(x, left, back, right, right_inv, twid_cos, twid_sin, own, own_rate, ramp, spec, act, cos, tail)


def finish(back, cot):
    devices = cot.shape[0]
    steps = 4
    data = pl.BlockSpec((devices // steps, CHANNELS, RADIX), lambda i: (i, 0, 0))
    outs = [jax.ShapeDtypeStruct(cot.shape, BF16)] * 3 + [
        jax.ShapeDtypeStruct((PE, WIDTH), F32),
        jax.ShapeDtypeStruct((1, WIDTH), F32),
        jax.ShapeDtypeStruct((WIDTH, WIDTH), F32),
        jax.ShapeDtypeStruct((1, WIDTH), F32),
    ]
    return pl.pallas_call(
        finish_kernel,
        grid=(steps,),
        in_specs=[pl.BlockSpec((devices // steps, SEND, RADIX), lambda i: (i, 0, 0)), data],
        out_specs=[data] * 3 + [full(o.shape) for o in outs[3:]],
        out_shape=outs,
        scratch_shapes=[pltpu.VMEM((SHARE, RADIX), F32)],
        compiler_params=params(),
        cost_estimate=pl.CostEstimate(flops=1 << 20, bytes_accessed=2 << 20, transcendentals=0),
    )(back, cot)


SEQ = ("z", "y", "x")


def on_device(
    value_branch, first_gate, second_gate, out_cotangent,
    pos_weight, pos_bias, mid_weight, mid_bias, out_weight, decay_rates,
):
    devices = lax.axis_size(SEQ)
    tables = dft_tables()
    stack, tail = feature_tables()
    ramp = (np.arange(SEQLEN) / SEQLEN).astype(np.float32)[None, :]
    blocks = (devices, CHANNELS, RADIX)
    cot = out_cotangent.reshape(blocks)
    sent = pack(value_branch.reshape(blocks), first_gate.reshape(blocks), second_gate.reshape(blocks), cot)
    x = lax.all_to_all(sent, SEQ, 0, 0, tiled=True)
    net = network_forward(
        pos_weight, pos_bias, mid_weight, mid_bias, out_weight, decay_rates, tables, stack, ramp
    )
    y, out_weight_grad = chain(x.reshape(HALF_ROWS * DATA, RADIX), net, tables, tail, ramp)
    back = lax.all_to_all(y.reshape(devices, SEND, RADIX), SEQ, 0, 0, tiled=True)
    value_grad, first_grad, second_grad, pos_grad, pos_bias_grad, mid_grad, mid_bias_grad = finish(back, cot)
    shape = value_branch.shape
    return (
        value_grad.reshape(shape),
        first_grad.reshape(shape),
        second_grad.reshape(shape),
        pos_grad.T,
        pos_bias_grad[0],
        mid_grad,
        mid_bias_grad[0],
        out_weight_grad,
    )


def solution(mesh):
    grid = Mesh(mesh.devices.reshape(mesh.shape["dp"], 2, 8, 4), ("dp",) + SEQ)
    part = P(None, ("dp",) + SEQ)
    in_specs = (part,) * 4 + (P(),) * 6
    out_specs = (part,) * 3 + (P("dp", None), P("dp"), P("dp", None), P("dp"), P(SEQ, "dp"))
    return jax.shard_map(on_device, mesh=grid, in_specs=in_specs, out_specs=out_specs, check_vma=False)
```

time: 126 us -> 112 us (0.89); the launches traced: 124 us -> 111 us
  blocking collectives: 0 us -> 49.5 us
  starting transfers between devices: 51.7 us -> 19.1 us
  local copies, waits for them, and re-layouts: 26.6 us -> 0.76 us
  Pallas kernels: 25.7 us -> 37.5 us
  waiting for transfers between devices: 13.6 us -> 3.66 us
  other arithmetic: 5.42 us -> 0 us
    all_to_all x0 -> x1, blocking collectives: none -> 49.5 us  [on_device(): lax.all_to_all(y.reshape(devices, SEND, RADIX), SEQ, 0, 0, tiled=True)]
    all_to_all x2 -> x0, starting transfers between devices: 25.1 us -> none  [the longest x1 15.4 us: on_device(): lax.all_to_all(y.reshape(devices, 3 * CHANNELS, RADIX), SEQ, 0, 0, tiled=...]
    unnamed x50 -> x2, local copies, waits for them, and re-layouts: 20.4 us -> 0.76 us
    pallas_call x3 -> x4, Pallas kernels: 25.7 us -> 37.5 us  [the longest x1 15.5 us: network_forward(): pl.pallas_call(network_kernel, grid=(SEQLEN // CHUNK,), in_specs=[block,...]
    all_to_all x2 -> x0, waiting for transfers between devices: 11.2 us -> none  [the longest x1 11.2 us: on_device(): lax.all_to_all(shares, ('y', 'x'), 0, 0, tiled=True).astype(F32)]
    ppermute x1 -> x0, starting transfers between devices: 7.38 us -> none  [on_device(): inner = inner + lax.ppermute(inner, 'z', [(0, 1), (1, 0)])]
    all_to_all x1, waiting for transfers between devices: 0.01 us -> 3.66 us  [on_device(): x = lax.all_to_all(sent, SEQ, 0, 0, tiled=True)]
    broadcast_in_dim x6 -> x0, local copies, waits for them, and re-layouts: 3.28 us -> none  [the longest x1 0.93 us: on_device(): shares = jnp.broadcast_to(inner.astype(BF16)[None], (peers,) + inner.shape)]
  transfers between devices with their start and end apart: 4 -> 1, of which waited for: 2 -> 1; matrix products, arithmetic and copies ran while one was open for 7% -> 0% of each run, Pallas kernels for 16% -> 14%
where the time goes in v2:
time: 112 us; the launch traced here: 111 us
  blocking collectives  49.5 us (44%)
  Pallas kernels  37.5 us (33%)
  starting transfers between devices  19.1 us (17%)
  waiting for transfers between devices  3.66 us (3%)
    all_to_all x1, blocking collectives, on_device(): lax.all_to_all(y.reshape(devices, SEND, RADIX), SEQ, 0, 0, tiled=True)  49.5 us
    all_to_all x1, starting transfers between devices, on_device(): x = lax.all_to_all(sent, SEQ, 0, 0, tiled=True)  19.1 us
    pallas_call x1, Pallas kernels, network_forward(): pl.pallas_call(network_kernel, grid=(SEQLEN // CHUNK,), in_specs=[block,...  15.5 us
    pallas_call x1, Pallas kernels, chain(): pl.pallas_call(chain_kernel, in_specs=[within] * 11 + [anywhere] * 3, out...  9.39 us
    pallas_call x1, Pallas kernels, pack(): pl.pallas_call(pack_kernel, in_specs=[anywhere] * 4, out_specs=anywhere,...  9.09 us
    all_to_all x1, waiting for transfers between devices, on_device(): x = lax.all_to_all(sent, SEQ, 0, 0, tiled=True)  3.66 us
    pallas_call x1, Pallas kernels, finish(): pl.pallas_call(finish_kernel, grid=(steps,), in_specs=[pl.BlockSpec((devi...  3.55 us
  transfers between devices with their start and end apart: 1, of which 1 were waited for; matrix products, arithmetic and copies ran while one was open for 0% of the time, Pallas kernels for 14%

profile of v2, /device:TPU:6, one launch (start us, length us, event | category | flops | bytes accessed | tf_op | source)
XLA Modules:
  0.0 111.2 jit_solution(2309401750102727839)
XLA Ops:
  0.6 9.1 %shard_map.242 = bf16[64,24,128]{2,1,0:T(8,128)(2,1)} custom-call(bf16[64,8,128]{2,1,0:T(8,128)(2,1)} %bitcast.21, bf16[64,8,128]{2,1,0:T(8,128)(2,1)} %bitcast.22, bf16[64,8,128]{2,1,0:T(8,128)(2,1)} %bitcast.23, bf16[64,8,128]{2,1,0:T(8,128)(2,1)} %bitcast.18), custom_call_target="tpu_custom_call" | custom-call | flops 131072 | bytes 1048576 | tf_op jit(solution)/shard_map/pallas_call | solution.py:388
  9.7 19.1 %all-to-all-start = ((bf16[64,24,128]{2,1,0:T(8,128)(2,1)}), bf16[64,24,128]{2,1,0:T(8,128)(2,1)S(1)}, u32[]{:S(2)}, u32[]{:S(2)}) async-start(bf16[64,24,128]{2,1,0:T(8,128)(2,1)} %shard_map.242), calls=%async_computation | async-start | bytes 786432 | tf_op jit(solution)/shard_map/all_to_all | solution.py:503
  28.8 15.5 %shard_map.243 = (bf16[128,8192]{1,0:T(8,128)(2,1)}, bf16[128,8192]{1,0:T(8,128)(2,1)}, f32[2,640,256]{2,1,0:T(8,128)}, bf16[128,128]{1,0:T(8,128)(2,1)}, f32[16,128]{1,0:T(8,128)}) custom-call(bf16[128,8192]{1,0:T(8,128)(2,1)} %constant.18.clone.pe_ref, f32[1,8192]{1,0:T(1,128)} %constant.19.clone.ramp_ref, bf16[160,64]{1,0:T(8,128)(2,1)} %constant.20.clone.left_ref, ...), custom_call_target="tpu_custom_call" | custom-call | flops 1073741824 | bytes 10485760 | tf_op jit(solution)/shard_map/pallas_call | solution.py:411
  44.3 3.7 %all-to-all-done = bf16[64,24,128]{2,1,0:T(8,128)(2,1)S(1)} async-done(((bf16[64,24,128]{2,1,0:T(8,128)(2,1)}), bf16[64,24,128]{2,1,0:T(8,128)(2,1)S(1)}, u32[]{:S(2)}, u32[]{:S(2)}) %all-to-all-start) | async-done | bytes 393248 | tf_op jit(solution)/shard_map/all_to_all | solution.py:503
  48.0 0.0 copy-start
  48.0 0.8 copy-done
  48.7 9.4 %shard_map.244 = (bf16[5120,128]{1,0:T(8,128)(2,1)}, f32[16,64]{1,0:T(8,128)}) custom-call(bf16[1536,128]{1,0:T(8,128)(2,1)} %bitcast.20, bf16[160,64]{1,0:T(8,128)(2,1)} %constant.20.clone.left_ref, bf16[64,160]{1,0:T(8,128)(2,1)} %constant.24.clone.back_ref, bf16[256,256]{1,0:T(8,128)(2,1)} %constant.21.clone.right_ref, ...), custom_call_target="tpu_custom_call" | custom-call | flops 3221225472 | bytes 8388608 | tf_op jit(solution)/shard_map/pallas_call | solution.py:443
  58.1 49.5 %all_to_all.10.back_ref = bf16[64,80,128]{2,1,0:T(8,128)(2,1)} all-to-all(bf16[64,80,128]{2,1,0:T(8,128)(2,1)} %bitcast.17), channel_id=1, replica_groups=mesh['dp'=8,'z'=2,'y'=8,'x'=4] {'z','y','x'}, dimensions={0} | all-to-all | bytes 2621440 | tf_op jit(solution)/shard_map/all_to_all | solution.py:508
  107.7 3.6 %shard_map.245 = (bf16[64,8,128]{2,1,0:T(8,128)(2,1)}, bf16[64,8,128]{2,1,0:T(8,128)(2,1)}, bf16[64,8,128]{2,1,0:T(8,128)(2,1)}, f32[33,64]{1,0:T(8,128)}, f32[1...) custom-call(bf16[64,80,128]{2,1,0:T(8,128)(2,1)} %all_to_all.10.back_ref, bf16[64,8,128]{2,1,0:T(8,128)(2,1)} %bitcast.19), custom_call_target="tpu_custom_call" | custom-call | flops 1048576 | bytes 2097152 | tf_op jit(solution)/shard_map/pallas_call | solution.py:477
Async XLA Ops:
  9.7 38.2 %all-to-all-start = ((bf16[64,24,128]{2,1,0:T(8,128)(2,1)}), bf16[64,24,128]{2,1,0:T(8,128)(2,1)S(1)}, u32[]{:S(2)}, u32[]{:S(2)}) async-start(bf16[64,24,128]{2,1,0:T(8,128)(2,1)} %shard_map.242), calls=%async_computation | async-start | bytes 786432 | tf_op jit(solution)/shard_map/all_to_all | solution.py:503
  48.0 0.8 copy-start

commit v3 on v2

--- a/solution.py
+++ b/solution.py
@@ -19,9 +19,10 @@
 PE = 33
 PE_BLOCK = 40
 CHUNK = 1024
+NET_CHUNK = 4096
 CHANNELS = 8
 ROWS = 2 * CHANNELS
-SHARE = 56
+SHARE = 8
 DATA = 3 * CHANNELS
 SEND = DATA + SHARE
 VMEM_BYTES = 60 << 20
@@ -162,41 +163,33 @@
     return jnp.concatenate([real.astype(BF16), imag.astype(BF16)], axis=1)
 
 
-def pack_kernel(v_hbm, x1_hbm, x2_hbm, cot_hbm, out_hbm, x2, cot, grad, sems):
-    loads = [pltpu.make_async_copy(cot_hbm, cot, sems.at[0]), pltpu.make_async_copy(x2_hbm, x2, sems.at[1])]
-    moves = [
-        pltpu.make_async_copy(v_hbm, out_hbm.at[:, pl.ds(0, CHANNELS), :], sems.at[2]),
-        pltpu.make_async_copy(x1_hbm, out_hbm.at[:, pl.ds(CHANNELS, CHANNELS), :], sems.at[3]),
+def pack_kernel(v_hbm, x1_hbm, x2_hbm, cot_hbm, out_hbm, v, x1, x2, cot, sent, sems):
+    loads = [
+        pltpu.make_async_copy(src, dst, sems.at[i])
+        for i, (src, dst) in enumerate(((v_hbm, v), (x1_hbm, x1), (x2_hbm, x2), (cot_hbm, cot)))
     ]
-    for copy in loads + moves:
+    for copy in loads:
         copy.start()
     for copy in loads:
         copy.wait()
-    grad[...] = (cot[...].astype(F32) * x2[...].astype(F32)).astype(BF16)
-    last = pltpu.make_async_copy(grad, out_hbm.at[:, pl.ds(2 * CHANNELS, CHANNELS), :], sems.at[4])
+    sent[:, :CHANNELS, :] = v[...]
+    sent[:, CHANNELS : 2 * CHANNELS, :] = x1[...]
+    sent[:, 2 * CHANNELS :, :] = (cot[...].astype(F32) * x2[...].astype(F32)).astype(BF16)
+    last = pltpu.make_async_copy(sent, out_hbm, sems.at[4])
     last.start()
-    for copy in moves + [last]:
-        copy.wait()
+    last.wait()
 
 
 def network_kernel(
     pe_ref, ramp_ref, left_ref, right_ref, tc_ref, ts_ref,
-    pos_hbm, pos_bias_hbm, mid_hbm, mid_bias_hbm, out_hbm, rate_hbm,
+    pos_ref, pos_bias_ref, mid_ref, mid_bias_ref, out_ref, rate_ref,
     act_ref, cos_ref, spec_ref, own_ref, own_rate_ref,
     filt, square, wp, wm, wo, bias, decay,
-    pos_ref, pos_bias_ref, mid_ref, mid_bias_ref, out_ref, rate_ref, sems,
 ):
     step = pl.program_id(0)
 
     @pl.when(step == 0)
     def _():
-        sources = (pos_hbm, pos_bias_hbm, mid_hbm, mid_bias_hbm, out_hbm, rate_hbm)
-        targets = (pos_ref, pos_bias_ref, mid_ref, mid_bias_ref, out_ref, rate_ref)
-        copies = [pltpu.make_async_copy(src, dst, sems.at[i]) for i, (src, dst) in enumerate(zip(sources, targets))]
-        for copy in copies:
-            copy.start()
-        for copy in copies:
-            copy.wait()
         rank = lax.axis_index(SEQ)
         lane = pl.multiple_of(rank // 8 * RADIX, RADIX)
         first = pl.multiple_of(rank % 8 * ROWS, ROWS)
@@ -229,27 +222,39 @@
         own_ref[:WIDTH, :] = square[...].T[:WIDTH, :].astype(BF16)
 
     span = 256
-    parts = [slice(p * span, (p + 1) * span) for p in range(CHUNK // span)]
+    parts = [slice(p * span, (p + 1) * span) for p in range(NET_CHUNK // span)]
     wide_bias = jnp.concatenate([bias[...]] * (span // RADIX), axis=1)
     wide_rate = jnp.concatenate([decay[...]] * (span // RADIX), axis=1)
-    for part, cols in enumerate(parts):
+    pres = []
+    for cols in parts:
         both = dot(wp[...], pe_ref[:, cols])
-        act, slope = sin_cos(both[:WIDTH] + both[WIDTH:])
+        pres.append(both[:WIDTH] + both[WIDTH:])
+    stacks = []
+    for pre, cols in zip(pres, parts):
+        act, slope = sin_cos(pre)
         pieces = split_two(act)
         act_ref[:WIDTH, cols] = pieces[0]
         cos_ref[:WIDTH, cols] = slope.astype(BF16)
-        both = dot(wm[...], jnp.concatenate(pieces, axis=0))
-        act, slope = sin_cos(both[:WIDTH] + both[WIDTH:] + wide_bias)
+        stacks.append(jnp.concatenate(pieces, axis=0))
+    pres = []
+    for stack in stacks:
+        both = dot(wm[...], stack)
+        pres.append(both[:WIDTH] + both[WIDTH:] + wide_bias)
+    stacks = []
+    for pre, cols in zip(pres, parts):
+        act, slope = sin_cos(pre)
         pieces = split_two(act)
         act_ref[WIDTH:, cols] = pieces[0]
         cos_ref[WIDTH:, cols] = slope.astype(BF16)
-        both = dot(wo[...], jnp.concatenate(pieces, axis=0))
+        stacks.append(jnp.concatenate(pieces, axis=0))
+    for part, (stack, cols) in enumerate(zip(stacks, parts)):
+        both = dot(wo[...], stack)
         rows = (both[:ROWS] + both[ROWS:]) * jnp.exp(-wide_rate * ramp_ref[:, cols])
         for j in range(span // RADIX):
-            base = pl.multiple_of(step * (CHUNK // RADIX * ROWS) + (part * (span // RADIX) + j) * ROWS, ROWS)
+            base = pl.multiple_of(step * (NET_CHUNK // RADIX * ROWS) + (part * (span // RADIX) + j) * ROWS, ROWS)
             filt[pl.ds(base, ROWS), :] = rows[:, j * RADIX : (j + 1) * RADIX]
 
-    @pl.when(step == SEQLEN // CHUNK - 1)
+    @pl.when(step == SEQLEN // NET_CHUNK - 1)
     def _():
         for o in range(2):
             for pair in range(CHANNELS // 2):
@@ -337,41 +342,36 @@
         low_one = (dot(own_ref[WIDTH:, :WIDTH], low_two) * cos[:WIDTH, cols].astype(F32)).astype(BF16)
         acc[...] += dot_last(act[:, cols], jnp.concatenate([low_two, low_one, grad], axis=0))
     out_ref[...] = acc[WIDTH : 2 * WIDTH, 2 * WIDTH :].T
-    half = WIDTH // 2
     tail = 2 * WIDTH
-    share[:half, :WIDTH] = acc[:half, :WIDTH]
-    share[:half, WIDTH:] = acc[half:WIDTH, :WIDTH]
-    share[half:, :WIDTH] = acc[tail : tail + 24, WIDTH : 2 * WIDTH]
-    share[half : half + 16, WIDTH:] = acc[tail + 24 : tail + 40, WIDTH : 2 * WIDTH]
-    share[half + 16 :, WIDTH:] = acc[tail + 32 : tail + 40, :WIDTH]
+    share[...] = jnp.zeros_like(share)
+    share[:, :WIDTH] = acc[:WIDTH, :WIDTH]
+    share[:PE_BLOCK, WIDTH:] = acc[tail:, WIDTH : 2 * WIDTH]
+    share[PE_BLOCK : PE_BLOCK + 8, WIDTH:] = acc[tail + 32 :, :WIDTH]
     for i in range(HALF_ROWS):
-        ys[i * SEND + DATA : (i + 1) * SEND, :] = share[...]
+        group = i // 4 % 8
+        ys[i * SEND + DATA : (i + 1) * SEND, :] = share[group * SHARE : (group + 1) * SHARE, :]
     y_ref[...] = ys[...].astype(BF16)
 
 
-def finish_kernel(back_ref, cot_ref, value_ref, first_ref, second_ref, pos_ref, pos_bias_ref, mid_ref, mid_bias_ref, total):
-    step = pl.program_id(0)
+def total_kernel(back_hbm, out_ref, shares, sem):
+    copy = pltpu.make_async_copy(back_hbm.at[:, pl.ds(DATA, SHARE), :], shares, sem)
+    copy.start()
+    copy.wait()
+    total = jnp.sum(shares[...].astype(F32), axis=0)
+    out_ref[...] = jnp.broadcast_to(total[None], out_ref.shape)
+
+
+def finish_kernel(back_ref, cot_ref, value_ref, first_ref, second_ref):
     value_ref[...] = back_ref[:, 2 * CHANNELS : DATA, :]
     first_ref[...] = back_ref[:, CHANNELS : 2 * CHANNELS, :]
     second_ref[...] = (cot_ref[...].astype(F32) * back_ref[:, :CHANNELS, :].astype(F32)).astype(BF16)
-    part = jnp.sum(back_ref[:, DATA:, :].astype(F32), axis=0)
-
-    @pl.when(step == 0)
-    def _():
-        total[...] = part
-
-    @pl.when(step > 0)
-    def _():
-        total[...] += part
-
-    @pl.when(step == pl.num_programs(0) - 1)
-    def _():
-        half = WIDTH // 2
-        mid_ref[...] = jnp.concatenate([total[:half, :WIDTH], total[:half, WIDTH:]], axis=0).T
-        pos_ref[:24, :] = total[half:, :WIDTH]
-        pos_ref[24:, :] = total[half : half + PE - 24, WIDTH:]
-        pos_bias_ref[...] = total[half + PE - 24 : half + PE - 23, WIDTH:]
-        mid_bias_ref[...] = total[half + 17 : half + 18, WIDTH:]
+
+
+def inner_kernel(total_ref, pos_ref, pos_bias_ref, mid_ref, mid_bias_ref):
+    mid_ref[...] = total_ref[...].T[:WIDTH, :]
+    pos_ref[...] = total_ref[:PE, WIDTH:]
+    pos_bias_ref[...] = total_ref[PE : PE + 1, WIDTH:]
+    mid_bias_ref[...] = total_ref[PE_BLOCK + 1 : PE_BLOCK + 2, WIDTH:]
 
 
 def full(shape):
@@ -390,7 +390,7 @@
         in_specs=[anywhere] * 4,
         out_specs=anywhere,
         out_shape=jax.ShapeDtypeStruct((value.shape[0], DATA, RADIX), BF16),
-        scratch_shapes=[buffer] * 3 + [pltpu.SemaphoreType.DMA((5,))],
+        scratch_shapes=[buffer] * 4 + [pltpu.VMEM((value.shape[0], DATA, RADIX), BF16), pltpu.SemaphoreType.DMA((5,))],
         compiler_params=params(),
         cost_estimate=pl.CostEstimate(flops=1 << 17, bytes_accessed=1 << 20, transcendentals=0),
     )(value, first, second, cot)
@@ -398,7 +398,7 @@
 
 def network_forward(pos_weight, pos_bias, mid_weight, mid_bias, out_weight, decay_rates, tables, stack, ramp):
     left, back, right, right_inv, twid_cos, twid_sin = tables
-    block = pl.BlockSpec((2 * WIDTH, CHUNK), lambda i: (0, i))
+    block = pl.BlockSpec((2 * WIDTH, NET_CHUNK), lambda i: (0, i))
     tabs = (left, right, twid_cos, twid_sin)
     args = (pos_weight.T, pos_bias[None, :], mid_weight, mid_bias[None, :], out_weight.T, decay_rates[None, :])
     outs = [
@@ -410,10 +410,10 @@
     ]
     return pl.pallas_call(
         network_kernel,
-        grid=(SEQLEN // CHUNK,),
-        in_specs=[block, pl.BlockSpec((1, CHUNK), lambda i: (0, i))]
+        grid=(SEQLEN // NET_CHUNK,),
+        in_specs=[block, pl.BlockSpec((1, NET_CHUNK), lambda i: (0, i))]
         + [full(a.shape) for a in tabs]
-        + [pl.BlockSpec(memory_space=pltpu.HBM)] * len(args),
+        + [full(a.shape) for a in args],
         out_specs=[block] * 2 + [full(o.shape) for o in outs[2:]],
         out_shape=outs,
         scratch_shapes=[
@@ -424,9 +424,7 @@
             pltpu.VMEM((2 * ROWS, 2 * WIDTH), BF16),
             pltpu.VMEM((WIDTH, RADIX), F32),
             pltpu.VMEM((ROWS, RADIX), F32),
-        ]
-        + [pltpu.VMEM(a.shape, F32) for a in args]
-        + [pltpu.SemaphoreType.DMA((len(args),))],
+        ],
         compiler_params=params(),
         cost_estimate=pl.CostEstimate(flops=1 << 30, bytes_accessed=10 << 20, transcendentals=1 << 20),
     )(stack, ramp, *tabs, *args)
@@ -456,7 +454,7 @@
             pltpu.VMEM((tall, SEQLEN), BF16),
             pltpu.VMEM((2 * WIDTH, SEQLEN), BF16),
             pltpu.VMEM((tall, 2 * WIDTH + ROWS), F32),
-            pltpu.VMEM((SHARE, RADIX), F32),
+            pltpu.VMEM((WIDTH, RADIX), F32),
             pltpu.SemaphoreType.DMA((3,)),
         ],
         compiler_params=params(CHAIN_BYTES),
@@ -464,26 +462,48 @@
     )(x, left, back, right, right_inv, twid_cos, twid_sin, own, own_rate, ramp, spec, act, cos, tail)
 
 
+def share_total(back, peers):
+    return pl.pallas_call(
+        total_kernel,
+        in_specs=[pl.BlockSpec(memory_space=pltpu.HBM)],
+        out_specs=pl.BlockSpec(memory_space=pltpu.VMEM),
+        out_shape=jax.ShapeDtypeStruct((peers, SHARE, RADIX), F32),
+        scratch_shapes=[pltpu.VMEM((back.shape[0], SHARE, RADIX), BF16), pltpu.SemaphoreType.DMA(())],
+        compiler_params=params(),
+        cost_estimate=pl.CostEstimate(flops=1 << 16, bytes_accessed=1 << 17, transcendentals=0),
+    )(back)
+
+
 def finish(back, cot):
     devices = cot.shape[0]
-    steps = 4
+    steps = 2
     data = pl.BlockSpec((devices // steps, CHANNELS, RADIX), lambda i: (i, 0, 0))
-    outs = [jax.ShapeDtypeStruct(cot.shape, BF16)] * 3 + [
-        jax.ShapeDtypeStruct((PE, WIDTH), F32),
-        jax.ShapeDtypeStruct((1, WIDTH), F32),
-        jax.ShapeDtypeStruct((WIDTH, WIDTH), F32),
-        jax.ShapeDtypeStruct((1, WIDTH), F32),
-    ]
     return pl.pallas_call(
         finish_kernel,
         grid=(steps,),
         in_specs=[pl.BlockSpec((devices // steps, SEND, RADIX), lambda i: (i, 0, 0)), data],
-        out_specs=[data] * 3 + [full(o.shape) for o in outs[3:]],
-        out_shape=outs,
-        scratch_shapes=[pltpu.VMEM((SHARE, RADIX), F32)],
+        out_specs=[data] * 3,
+        out_shape=[jax.ShapeDtypeStruct(cot.shape, BF16)] * 3,
         compiler_params=params(),
-        cost_estimate=pl.CostEstimate(flops=1 << 20, bytes_accessed=2 << 20, transcendentals=0),
+        cost_estimate=pl.CostEstimate(flops=1 << 17, bytes_accessed=1 << 20, transcendentals=0),
     )(back, cot)
+
+
+def inner_gradients(total):
+    within = pl.BlockSpec(memory_space=pltpu.VMEM)
+    return pl.pallas_call(
+        inner_kernel,
+        in_specs=[within],
+        out_specs=[within] * 4,
+        out_shape=[
+            jax.ShapeDtypeStruct((PE, WIDTH), F32),
+            jax.ShapeDtypeStruct((1, WIDTH), F32),
+            jax.ShapeDtypeStruct((WIDTH, WIDTH), F32),
+            jax.ShapeDtypeStruct((1, WIDTH), F32),
+        ],
+        compiler_params=params(),
+        cost_estimate=pl.CostEstimate(flops=1 << 13, bytes_accessed=1 << 16, transcendentals=0),
+    )(total)
 
 
 SEQ = ("z", "y", "x")
@@ -506,7 +526,10 @@
     )
     y, out_weight_grad = chain(x.reshape(HALF_ROWS * DATA, RADIX), net, tables, tail, ramp)
     back = lax.all_to_all(y.reshape(devices, SEND, RADIX), SEQ, 0, 0, tiled=True)
-    value_grad, first_grad, second_grad, pos_grad, pos_bias_grad, mid_grad, mid_bias_grad = finish(back, cot)
+    total = share_total(back, lax.axis_size("y"))
+    total = lax.all_to_all(total, "y", 0, 0, tiled=True)
+    value_grad, first_grad, second_grad = finish(back, cot)
+    pos_grad, pos_bias_grad, mid_grad, mid_bias_grad = inner_gradients(total.reshape(WIDTH, RADIX))
     shape = value_branch.shape
     return (
         value_grad.reshape(shape),

time: 112 us -> 93.2 us (0.83)
  blocking collectives: 49.5 us -> 27.1 us
  waiting for transfers between devices: 3.66 us -> 15.8 us
  Pallas kernels: 37.5 us -> 25.4 us
  starting transfers between devices: 19.1 us -> 22.4 us
    all_to_all x1, blocking collectives: 49.5 us -> 27.1 us  [on_device(): lax.all_to_all(y.reshape(devices, SEND, RADIX), SEQ, 0, 0, tiled=True)]
    pallas_call x1, Pallas kernels: 9.09 us -> 1.98 us  [pack(): pl.pallas_call(pack_kernel, in_specs=[anywhere] * 4, out_specs=anywhere,...]
    all_to_all x0 -> x1, waiting for transfers between devices: none -> 6.16 us  [on_device(): total = lax.all_to_all(total, 'y', 0, 0, tiled=True)]
    all_to_all x1, waiting for transfers between devices: 3.66 us -> 9.59 us  [on_device(): x = lax.all_to_all(sent, SEQ, 0, 0, tiled=True)]
    all_to_all x0 -> x1, starting transfers between devices: none -> 3.35 us  [on_device(): total = lax.all_to_all(total, 'y', 0, 0, tiled=True)]
    pallas_call x1 -> x3, Pallas kernels: 15.5 us -> 12.7 us  [the longest x1 9.59 us: network_forward(): pl.pallas_call(network_kernel, grid=(SEQLEN // NET_CHUNK,), in_specs=[blo...]
    pallas_call x1, Pallas kernels: 3.55 us -> 1.78 us  [finish(): pl.pallas_call(finish_kernel, grid=(steps,), in_specs=[pl.BlockSpec((devi...]
  transfers between devices with their start and end apart: 1 -> 2, of which waited for: 1 -> 2; matrix products, arithmetic and copies ran while one was open for 0% -> 0% of each run, Pallas kernels for 14% -> 12%
where the time goes in v3:
time: 93.2 us; the launch traced here: 92.7 us
  blocking collectives  27.1 us (29%)
  Pallas kernels  25.4 us (27%)
  starting transfers between devices  22.4 us (24%)
  waiting for transfers between devices  15.8 us (17%)
  local copies, waits for them, and re-layouts  1.36 us (1%)
    all_to_all x1, blocking collectives, on_device(): lax.all_to_all(y.reshape(devices, SEND, RADIX), SEQ, 0, 0, tiled=True)  27.1 us
    all_to_all x1, starting transfers between devices, on_device(): x = lax.all_to_all(sent, SEQ, 0, 0, tiled=True)  19.1 us
    all_to_all x1, waiting for transfers between devices, on_device(): x = lax.all_to_all(sent, SEQ, 0, 0, tiled=True)  9.59 us
    pallas_call x1, Pallas kernels, network_forward(): pl.pallas_call(network_kernel, grid=(SEQLEN // NET_CHUNK,), in_specs=[blo...  9.59 us
    pallas_call x1, Pallas kernels, chain(): pl.pallas_call(chain_kernel, in_specs=[within] * 11 + [anywhere] * 3, out...  8.99 us
    all_to_all x1, waiting for transfers between devices, on_device(): total = lax.all_to_all(total, 'y', 0, 0, tiled=True)  6.16 us
    all_to_all x1, starting transfers between devices, on_device(): total = lax.all_to_all(total, 'y', 0, 0, tiled=True)  3.35 us
    pallas_call x1, Pallas kernels, pack(): pl.pallas_call(pack_kernel, in_specs=[anywhere] * 4, out_specs=anywhere,...  1.98 us
  transfers between devices with their start and end apart: 2, of which 2 were waited for; matrix products, arithmetic and copies ran while one was open for 0% of the time, Pallas kernels for 12%

profile of v3, /device:TPU:6, one launch (start us, length us, event | category | flops | bytes accessed | tf_op | source)
XLA Modules:
  0.0 92.7 jit_solution(1132044345047266536)
XLA Ops:
  0.6 2.0 %shard_map.242 = bf16[64,24,128]{2,1,0:T(8,128)(2,1)} custom-call(bf16[64,8,128]{2,1,0:T(8,128)(2,1)} %bitcast.22, bf16[64,8,128]{2,1,0:T(8,128)(2,1)} %bitcast.23, bf16[64,8,128]{2,1,0:T(8,128)(2,1)} %bitcast.24, bf16[64,8,128]{2,1,0:T(8,128)(2,1)} %bitcast.18), custom_call_target="tpu_custom_call" | custom-call | flops 131072 | bytes 1048576 | tf_op jit(solution)/shard_map/pallas_call | solution.py:388
  2.6 19.1 %all-to-all-start = ((bf16[64,24,128]{2,1,0:T(8,128)(2,1)}), bf16[64,24,128]{2,1,0:T(8,128)(2,1)S(1)}, u32[]{:S(2)}, u32[]{:S(2)}) async-start(bf16[64,24,128]{2,1,0:T(8,128)(2,1)} %shard_map.242), calls=%async_computation | async-start | bytes 786432 | tf_op jit(solution)/shard_map/all_to_all | solution.py:523
  21.7 9.6 %shard_map.243 = (bf16[128,8192]{1,0:T(8,128)(2,1)}, bf16[128,8192]{1,0:T(8,128)(2,1)}, f32[2,640,256]{2,1,0:T(8,128)}, bf16[128,128]{1,0:T(8,128)(2,1)}, f32[16,128]{1,0:T(8,128)}) custom-call(bf16[128,8192]{1,0:T(8,128)(2,1)} %constant.18.clone.pe_ref, f32[1,8192]{1,0:T(1,128)} %constant.19.clone.ramp_ref, bf16[160,64]{1,0:T(8,128)(2,1)} %constant.20.clone.left_ref, ...), custom_call_target="tpu_custom_call" | custom-call | flops 1073741824 | bytes 10485760 | tf_op jit(solution)/shard_map/pallas_call | solution.py:411
  31.3 9.6 %all-to-all-done = bf16[64,24,128]{2,1,0:T(8,128)(2,1)S(1)} async-done(((bf16[64,24,128]{2,1,0:T(8,128)(2,1)}), bf16[64,24,128]{2,1,0:T(8,128)(2,1)S(1)}, u32[]{:S(2)}, u32[]{:S(2)}) %all-to-all-start) | async-done | bytes 393248 | tf_op jit(solution)/shard_map/all_to_all | solution.py:523
  40.9 0.0 copy-start
  40.9 0.8 copy-done
  41.6 9.0 %shard_map.244 = (bf16[2048,128]{1,0:T(8,128)(2,1)}, f32[16,64]{1,0:T(8,128)}) custom-call(bf16[1536,128]{1,0:T(8,128)(2,1)} %bitcast.21, bf16[160,64]{1,0:T(8,128)(2,1)} %constant.20.clone.left_ref, bf16[64,160]{1,0:T(8,128)(2,1)} %constant.24.clone.back_ref, bf16[256,256]{1,0:T(8,128)(2,1)} %constant.21.clone.right_ref, ...), custom_call_target="tpu_custom_call" | custom-call | flops 3221225472 | bytes 8388608 | tf_op jit(solution)/shard_map/pallas_call | solution.py:441
  50.6 27.1 %all_to_all.15.back_ref.back_hbm = bf16[64,32,128]{2,1,0:T(8,128)(2,1)} all-to-all(bf16[64,32,128]{2,1,0:T(8,128)(2,1)} %bitcast.20), channel_id=1, replica_groups=mesh['dp'=8,'z'=2,'y'=8,'x'=4] {'z','y','x'}, dimensions={0} | all-to-all | bytes 1048576 | tf_op jit(solution)/shard_map/all_to_all | solution.py:528
  77.7 1.6 %shard_map.246 = f32[8,8,128]{2,1,0:T(8,128)} custom-call(bf16[64,32,128]{2,1,0:T(8,128)(2,1)} %all_to_all.15.back_ref.back_hbm), custom_call_target="tpu_custom_call" | custom-call | flops 65536 | bytes 131072 | tf_op jit(solution)/shard_map/pallas_call | solution.py:466
  79.3 3.4 %all-to-all-start.2 = ((f32[8,8,128]{2,1,0:T(8,128)}), f32[8,8,128]{2,1,0:T(8,128)S(1)}, u32[]{:S(2)}, u32[]{:S(2)}) async-start(f32[8,8,128]{2,1,0:T(8,128)} %shard_map.246), calls=%async_computation.2 | async-start | bytes 65536 | tf_op jit(solution)/shard_map/all_to_all | solution.py:530
  82.7 1.8 %shard_map.245 = (bf16[64,8,128]{2,1,0:T(8,128)(2,1)}, bf16[64,8,128]{2,1,0:T(8,128)(2,1)}, bf16[64,8,128]{2,1,0:T(8,128)(2,1)}) custom-call(bf16[64,32,128]{2,1,0:T(8,128)(2,1)} %all_to_all.15.back_ref.back_hbm, bf16[64,8,128]{2,1,0:T(8,128)(2,1)} %bitcast.19), custom_call_target="tpu_custom_call" | custom-call | flops 131072 | bytes 1048576 | tf_op jit(solution)/shard_map/pallas_call | solution.py:481
  84.5 6.2 %all-to-all-done.2 = f32[8,8,128]{2,1,0:T(8,128)S(1)} async-done(((f32[8,8,128]{2,1,0:T(8,128)}), f32[8,8,128]{2,1,0:T(8,128)S(1)}, u32[]{:S(2)}, u32[]{:S(2)}) %all-to-all-start.2) | async-done | bytes 32800 | tf_op jit(solution)/shard_map/all_to_all | solution.py:530
  90.6 0.0 copy-start.1
  90.6 0.6 copy-done.1
  91.2 1.5 %shard_map.247 = (f32[33,64]{1,0:T(8,128)}, f32[1,64]{1,0:T(1,128)}, f32[64,64]{1,0:T(8,128)}, f32[1,64]{1,0:T(1,128)}) custom-call(f32[64,128]{1,0:T(8,128)} %bitcast.25), custom_call_target="tpu_custom_call" | custom-call | flops 8192 | bytes 65536 | tf_op jit(solution)/shard_map/pallas_call | solution.py:494
Async XLA Ops:
  2.6 38.2 %all-to-all-start = ((bf16[64,24,128]{2,1,0:T(8,128)(2,1)}), bf16[64,24,128]{2,1,0:T(8,128)(2,1)S(1)}, u32[]{:S(2)}, u32[]{:S(2)}) async-start(bf16[64,24,128]{2,1,0:T(8,128)(2,1)} %shard_map.242), calls=%async_computation | async-start | bytes 786432 | tf_op jit(solution)/shard_map/all_to_all | solution.py:523
  40.9 0.8 copy-start
  79.3 11.3 %all-to-all-start.2 = ((f32[8,8,128]{2,1,0:T(8,128)}), f32[8,8,128]{2,1,0:T(8,128)S(1)}, u32[]{:S(2)}, u32[]{:S(2)}) async-start(f32[8,8,128]{2,1,0:T(8,128)} %shard_map.246), calls=%async_computation.2 | async-start | bytes 65536 | tf_op jit(solution)/shard_map/all_to_all | solution.py:530
  90.6 0.6 copy-start.1

commit v4 on v3

--- a/solution.py
+++ b/solution.py
@@ -19,14 +19,14 @@
 PE = 33
 PE_BLOCK = 40
 CHUNK = 1024
-NET_CHUNK = 4096
+NET_CHUNK = 2048
 CHANNELS = 8
 ROWS = 2 * CHANNELS
 SHARE = 8
 DATA = 3 * CHANNELS
 SEND = DATA + SHARE
-VMEM_BYTES = 60 << 20
-CHAIN_BYTES = 60 << 20
+VMEM_BYTES = 64 << 20
+CHAIN_BYTES = 64 << 20
 
 
 def dft_tables():
@@ -348,7 +348,7 @@
     share[:PE_BLOCK, WIDTH:] = acc[tail:, WIDTH : 2 * WIDTH]
     share[PE_BLOCK : PE_BLOCK + 8, WIDTH:] = acc[tail + 32 :, :WIDTH]
     for i in range(HALF_ROWS):
-        group = i // 4 % 8
+        group = i % 8
         ys[i * SEND + DATA : (i + 1) * SEND, :] = share[group * SHARE : (group + 1) * SHARE, :]
     y_ref[...] = ys[...].astype(BF16)
 
@@ -501,12 +501,13 @@
             jax.ShapeDtypeStruct((WIDTH, WIDTH), F32),
             jax.ShapeDtypeStruct((1, WIDTH), F32),
         ],
-        compiler_params=params(),
+        compiler_params=params(2 << 20),
         cost_estimate=pl.CostEstimate(flops=1 << 13, bytes_accessed=1 << 16, transcendentals=0),
     )(total)
 
 
-SEQ = ("z", "y", "x")
+SEQ = ("z", "yhi", "ylo", "x")
+NEAR = ("ylo", "x")
 
 
 def on_device(
@@ -526,8 +527,8 @@
     )
     y, out_weight_grad = chain(x.reshape(HALF_ROWS * DATA, RADIX), net, tables, tail, ramp)
     back = lax.all_to_all(y.reshape(devices, SEND, RADIX), SEQ, 0, 0, tiled=True)
-    total = share_total(back, lax.axis_size("y"))
-    total = lax.all_to_all(total, "y", 0, 0, tiled=True)
+    total = share_total(back, lax.axis_size(NEAR))
+    total = lax.all_to_all(total, NEAR, 0, 0, tiled=True)
     value_grad, first_grad, second_grad = finish(back, cot)
     pos_grad, pos_bias_grad, mid_grad, mid_bias_grad = inner_gradients(total.reshape(WIDTH, RADIX))
     shape = value_branch.shape
@@ -544,7 +545,7 @@
 
 
 def solution(mesh):
-    grid = Mesh(mesh.devices.reshape(mesh.shape["dp"], 2, 8, 4), ("dp",) + SEQ)
+    grid = Mesh(mesh.devices.reshape(mesh.shape["dp"], 2, 4, 2, 4), ("dp",) + SEQ)
     part = P(None, ("dp",) + SEQ)
     in_specs = (part,) * 4 + (P(),) * 6
     out_specs = (part,) * 3 + (P("dp", None), P("dp"), P("dp", None), P("dp"), P(SEQ, "dp"))

time: 93.2 us -> 90.5 us (0.971)
  waiting for transfers between devices: 15.8 us -> 12.2 us
  starting transfers between devices: 22.4 us -> 24.2 us
  local copies, waits for them, and re-layouts: 1.36 us -> 0 us
    all_to_all x1, waiting for transfers between devices: 6.16 us -> 2.53 us  [on_device(): total = lax.all_to_all(total, NEAR, 0, 0, tiled=True)]
    all_to_all x1, starting transfers between devices: 3.35 us -> 4.94 us  [on_device(): total = lax.all_to_all(total, NEAR, 0, 0, tiled=True)]
    unnamed x4 -> x0, local copies, waits for them, and re-layouts: 1.36 us -> none
  transfers between devices with their start and end apart: 2 -> 2, of which waited for: 2 -> 2; matrix products, arithmetic and copies ran while one was open for 0% -> 0% of each run, Pallas kernels for 12% -> 13%
where the time goes in v4:
time: 90.5 us; the launch traced here: 89.3 us
  blocking collectives  27.1 us (30%)
  Pallas kernels  25.3 us (28%)
  starting transfers between devices  24.2 us (27%)
  waiting for transfers between devices  12.2 us (13%)
    all_to_all x1, blocking collectives, on_device(): lax.all_to_all(y.reshape(devices, SEND, RADIX), SEQ, 0, 0, tiled=True)  27.1 us
    all_to_all x1, starting transfers between devices, on_device(): x = lax.all_to_all(sent, SEQ, 0, 0, tiled=True)  19.2 us
    all_to_all x1, waiting for transfers between devices, on_device(): x = lax.all_to_all(sent, SEQ, 0, 0, tiled=True)  9.64 us
    pallas_call x1, Pallas kernels, network_forward(): pl.pallas_call(network_kernel, grid=(SEQLEN // NET_CHUNK,), in_specs=[blo...  9.47 us
    pallas_call x1, Pallas kernels, chain(): pl.pallas_call(chain_kernel, in_specs=[within] * 11 + [anywhere] * 3, out...  8.99 us
    all_to_all x1, starting transfers between devices, on_device(): total = lax.all_to_all(total, NEAR, 0, 0, tiled=True)  4.94 us
    all_to_all x1, waiting for transfers between devices, on_device(): total = lax.all_to_all(total, NEAR, 0, 0, tiled=True)  2.53 us
    pallas_call x1, Pallas kernels, pack(): pl.pallas_call(pack_kernel, in_specs=[anywhere] * 4, out_specs=anywhere,...  1.98 us
  transfers between devices with their start and end apart: 2, of which 2 were waited for; matrix products, arithmetic and copies ran while one was open for 0% of the time, Pallas kernels for 13%

profile of v4, /device:TPU:6, one launch (start us, length us, event | category | flops | bytes accessed | tf_op | source)
XLA Modules:
  0.0 89.3 jit_solution(10978564502411301249)
XLA Ops:
  0.6 2.0 %shard_map.242 = bf16[64,24,128]{2,1,0:T(8,128)(2,1)} custom-call(bf16[64,8,128]{2,1,0:T(8,128)(2,1)} %bitcast.21, bf16[64,8,128]{2,1,0:T(8,128)(2,1)} %bitcast.22, bf16[64,8,128]{2,1,0:T(8,128)(2,1)} %bitcast.23, bf16[64,8,128]{2,1,0:T(8,128)(2,1)} %bitcast.18), custom_call_target="tpu_custom_call" | custom-call | flops 131072 | bytes 1048576 | tf_op jit(solution)/shard_map/pallas_call | solution.py:388
  2.6 19.2 %all-to-all-start = ((bf16[64,24,128]{2,1,0:T(8,128)(2,1)}), bf16[64,24,128]{2,1,0:T(8,128)(2,1)}, u32[]{:S(2)}, u32[]{:S(2)}) async-start(bf16[64,24,128]{2,1,0:T(8,128)(2,1)} %shard_map.242), calls=%async_computation | async-start | bytes 786432 | tf_op jit(solution)/shard_map/all_to_all | solution.py:524
  21.8 9.5 %shard_map.243 = (bf16[128,8192]{1,0:T(8,128)(2,1)}, bf16[128,8192]{1,0:T(8,128)(2,1)}, f32[2,640,256]{2,1,0:T(8,128)}, bf16[128,128]{1,0:T(8,128)(2,1)}, f32[16,128]{1,0:T(8,128)}) custom-call(bf16[128,8192]{1,0:T(8,128)(2,1)} %constant.18.clone.pe_ref, f32[1,8192]{1,0:T(1,128)} %constant.19.clone.ramp_ref, bf16[160,64]{1,0:T(8,128)(2,1)} %constant.20.clone.left_ref, ...), custom_call_target="tpu_custom_call" | custom-call | flops 1073741824 | bytes 10485760 | tf_op jit(solution)/shard_map/pallas_call | solution.py:411
  31.3 9.6 %all-to-all-done = bf16[64,24,128]{2,1,0:T(8,128)(2,1)} async-done(((bf16[64,24,128]{2,1,0:T(8,128)(2,1)}), bf16[64,24,128]{2,1,0:T(8,128)(2,1)}, u32[]{:S(2)}, u32[]{:S(2)}) %all-to-all-start) | async-done | bytes 393248 | tf_op jit(solution)/shard_map/all_to_all | solution.py:524
  41.0 9.0 %shard_map.244 = (bf16[2048,128]{1,0:T(8,128)(2,1)}, f32[16,64]{1,0:T(8,128)}) custom-call(bf16[1536,128]{1,0:T(8,128)(2,1)} %bitcast.4.x_ref, bf16[160,64]{1,0:T(8,128)(2,1)} %constant.20.clone.left_ref, bf16[64,160]{1,0:T(8,128)(2,1)} %constant.24.clone.back_ref, bf16[256,256]{1,0:T(8,128)(2,1)} %constant.21.clone.right_ref, ...), custom_call_target="tpu_custom_call" | custom-call | flops 3221225472 | bytes 8388608 | tf_op jit(solution)/shard_map/pallas_call | solution.py:441
  50.0 27.1 %all_to_all.15.back_ref.back_hbm = bf16[64,32,128]{2,1,0:T(8,128)(2,1)} all-to-all(bf16[64,32,128]{2,1,0:T(8,128)(2,1)} %bitcast.20), channel_id=1, replica_groups=mesh['dp'=8,'z'=2,'yhi'=4,'ylo'=2,'x'=4] {'z','yhi','ylo','x'}, dimensions={0} | all-to-all | bytes 1048576 | tf_op jit(solution)/shard_map/all_to_all | solution.py:529
  77.0 1.6 %shard_map.246 = f32[8,8,128]{2,1,0:T(8,128)} custom-call(bf16[64,32,128]{2,1,0:T(8,128)(2,1)} %all_to_all.15.back_ref.back_hbm), custom_call_target="tpu_custom_call" | custom-call | flops 65536 | bytes 131072 | tf_op jit(solution)/shard_map/pallas_call | solution.py:466
  78.6 4.9 %all-to-all-start.2 = ((f32[8,8,128]{2,1,0:T(8,128)}), f32[8,8,128]{2,1,0:T(8,128)}, u32[]{:S(2)}, u32[]{:S(2)}) async-start(f32[8,8,128]{2,1,0:T(8,128)} %shard_map.246), calls=%async_computation.2 | async-start | bytes 65536 | tf_op jit(solution)/shard_map/all_to_all | solution.py:531
  83.6 1.8 %shard_map.245 = (bf16[64,8,128]{2,1,0:T(8,128)(2,1)}, bf16[64,8,128]{2,1,0:T(8,128)(2,1)}, bf16[64,8,128]{2,1,0:T(8,128)(2,1)}) custom-call(bf16[64,32,128]{2,1,0:T(8,128)(2,1)} %all_to_all.15.back_ref.back_hbm, bf16[64,8,128]{2,1,0:T(8,128)(2,1)} %bitcast.19), custom_call_target="tpu_custom_call" | custom-call | flops 131072 | bytes 1048576 | tf_op jit(solution)/shard_map/pallas_call | solution.py:481
  85.3 2.5 %all-to-all-done.2 = f32[8,8,128]{2,1,0:T(8,128)} async-done(((f32[8,8,128]{2,1,0:T(8,128)}), f32[8,8,128]{2,1,0:T(8,128)}, u32[]{:S(2)}, u32[]{:S(2)}) %all-to-all-start.2) | async-done | bytes 32800 | tf_op jit(solution)/shard_map/all_to_all | solution.py:531
  87.9 1.5 %shard_map.247 = (f32[33,64]{1,0:T(8,128)}, f32[1,64]{1,0:T(1,128)}, f32[64,64]{1,0:T(8,128)}, f32[1,64]{1,0:T(1,128)}) custom-call(f32[64,128]{1,0:T(8,128)} %bitcast.14.total_ref), custom_call_target="tpu_custom_call" | custom-call | flops 8192 | bytes 65536 | tf_op jit(solution)/shard_map/pallas_call | solution.py:494
Async XLA Ops:
  2.6 38.3 %all-to-all-start = ((bf16[64,24,128]{2,1,0:T(8,128)(2,1)}), bf16[64,24,128]{2,1,0:T(8,128)(2,1)}, u32[]{:S(2)}, u32[]{:S(2)}) async-start(bf16[64,24,128]{2,1,0:T(8,128)(2,1)} %shard_map.242), calls=%async_computation | async-start | bytes 786432 | tf_op jit(solution)/shard_map/all_to_all | solution.py:524
  78.6 9.2 %all-to-all-start.2 = ((f32[8,8,128]{2,1,0:T(8,128)}), f32[8,8,128]{2,1,0:T(8,128)}, u32[]{:S(2)}, u32[]{:S(2)}) async-start(f32[8,8,128]{2,1,0:T(8,128)} %shard_map.246), calls=%async_computation.2 | async-start | bytes 65536 | tf_op jit(solution)/shard_map/all_to_all | solution.py:531

commit v5 on v4

--- a/solution.py
+++ b/solution.py
@@ -14,17 +14,17 @@
 RADIX = 128
 HALF_ROWS = 64
 SEQLEN = HALF_ROWS * RADIX
-KROWS = 80
+KROWS = 72
 WIDTH = 64
 PE = 33
 PE_BLOCK = 40
-CHUNK = 1024
 NET_CHUNK = 2048
 CHANNELS = 8
 ROWS = 2 * CHANNELS
 SHARE = 8
 DATA = 3 * CHANNELS
 SEND = DATA + SHARE
+PACK_PARTS = 2
 VMEM_BYTES = 64 << 20
 CHAIN_BYTES = 64 << 20
 
@@ -132,10 +132,10 @@
     for j in range(2):
         cols = slice(j * RADIX, (j + 1) * RADIX)
         real_a, imag_a = stacked[:KROWS, cols], stacked[KROWS:, cols]
-        real_b = (real_a * twid_cos + imag_a * twid_sin).astype(BF16)
-        imag_b = (imag_a * twid_cos - real_a * twid_sin).astype(BF16)
+        real_b = real_a * twid_cos + imag_a * twid_sin
+        imag_b = imag_a * twid_cos - real_a * twid_sin
         rows.append(jnp.concatenate([real_b, imag_b], axis=1))
-    return dot(jnp.concatenate(rows, axis=0), right)
+    return dot(jnp.concatenate(rows, axis=0).astype(BF16), right)
 
 
 def inverse_pair(product, back, right_inv, twid_cos, twid_sin):
@@ -144,10 +144,10 @@
     for j in range(2):
         real_q = section[j * KROWS : (j + 1) * KROWS, :RADIX]
         imag_q = section[j * KROWS : (j + 1) * KROWS, RADIX:]
-        real_r = (real_q * twid_cos - imag_q * twid_sin).astype(BF16)
-        imag_r = (imag_q * twid_cos + real_q * twid_sin).astype(BF16)
+        real_r = real_q * twid_cos - imag_q * twid_sin
+        imag_r = imag_q * twid_cos + real_q * twid_sin
         cols.append(jnp.concatenate([real_r, imag_r], axis=0))
-    return dot(back, jnp.concatenate(cols, axis=1))
+    return dot(back, jnp.concatenate(cols, axis=1).astype(BF16))
 
 
 def spectral_product(left, right, sign_left, sign_right):
@@ -163,21 +163,28 @@
     return jnp.concatenate([real.astype(BF16), imag.astype(BF16)], axis=1)
 
 
-def pack_kernel(v_hbm, x1_hbm, x2_hbm, cot_hbm, out_hbm, v, x1, x2, cot, sent, sems):
-    loads = [
-        pltpu.make_async_copy(src, dst, sems.at[i])
-        for i, (src, dst) in enumerate(((v_hbm, v), (x1_hbm, x1), (x2_hbm, x2), (cot_hbm, cot)))
-    ]
-    for copy in loads:
-        copy.start()
-    for copy in loads:
+def pack_kernel(v_hbm, x1_hbm, x2_hbm, cot_hbm, out_hbm, x2, cot, sent, sems):
+    size = x2.shape[0] // PACK_PARTS
+    spans = [pl.ds(i * size, size) for i in range(PACK_PARTS)]
+    loads, stores = [], []
+    for i, span in enumerate(spans):
+        moves = (
+            (v_hbm.at[span], sent.at[span, pl.ds(0, CHANNELS)]),
+            (x1_hbm.at[span], sent.at[span, pl.ds(CHANNELS, CHANNELS)]),
+            (x2_hbm.at[span], x2.at[span]),
+            (cot_hbm.at[span], cot.at[span]),
+        )
+        loads.append([pltpu.make_async_copy(src, dst, sems.at[5 * i + j]) for j, (src, dst) in enumerate(moves)])
+        for copy in loads[-1]:
+            copy.start()
+    for i, span in enumerate(spans):
+        for copy in loads[i]:
+            copy.wait()
+        sent[span, 2 * CHANNELS :, :] = (cot[span].astype(F32) * x2[span].astype(F32)).astype(BF16)
+        stores.append(pltpu.make_async_copy(sent.at[span], out_hbm.at[span], sems.at[5 * i + 4]))
+        stores[-1].start()
+    for copy in stores:
         copy.wait()
-    sent[:, :CHANNELS, :] = v[...]
-    sent[:, CHANNELS : 2 * CHANNELS, :] = x1[...]
-    sent[:, 2 * CHANNELS :, :] = (cot[...].astype(F32) * x2[...].astype(F32)).astype(BF16)
-    last = pltpu.make_async_copy(sent, out_hbm, sems.at[4])
-    last.start()
-    last.wait()
 
 
 def network_kernel(
@@ -267,21 +274,30 @@
 
 
 def chain_kernel(
+    x_hbm, left_hbm, back_hbm, right_hbm, inv_hbm, tc_hbm, ts_hbm, own_hbm, rate_hbm, ramp_hbm,
+    spec_hbm, act_hbm, cos_hbm, tail_hbm,
+    y_hbm, out_ref,
     x_ref, left_ref, back_ref, right_ref, inv_ref, tc_ref, ts_ref, own_ref, rate_ref, ramp_ref,
-    spec, act_hbm, cos_hbm, tail_hbm,
-    y_ref, out_ref,
-    xs, ys, sv, sg2, sz, sg1, conv, dz, dh, act, cos, acc, share, sems,
+    xs, ys, sv, sg2, sz, sg1, conv, dz, dh, spec, act, cos, stat, acc, share, data, parts, sems,
 ):
-    copies = [
-        pltpu.make_async_copy(cos_hbm, cos, sems.at[0]),
-        pltpu.make_async_copy(act_hbm, act.at[pl.ds(0, 2 * WIDTH)], sems.at[1]),
-        pltpu.make_async_copy(tail_hbm, act.at[pl.ds(2 * WIDTH, PE_BLOCK)], sems.at[2]),
+    sources = (x_hbm, left_hbm, right_hbm, tc_hbm, ts_hbm, back_hbm, inv_hbm, own_hbm, rate_hbm, ramp_hbm)
+    targets = (x_ref, left_ref, right_ref, tc_ref, ts_ref, back_ref, inv_ref, own_ref, rate_ref, ramp_ref)
+    small = [pltpu.make_async_copy(s, d, sems.at[6 + i]) for i, (s, d) in enumerate(zip(sources, targets))]
+    for copy in small:
+        copy.start()
+    first_load = pltpu.make_async_copy(spec_hbm, spec, sems.at[0])
+    loads = [
+        pltpu.make_async_copy(cos_hbm, cos, sems.at[1]),
+        pltpu.make_async_copy(act_hbm, act.at[pl.ds(0, 2 * WIDTH)], sems.at[2]),
+        pltpu.make_async_copy(tail_hbm, act.at[pl.ds(2 * WIDTH, PE_BLOCK)], sems.at[3]),
     ]
-    for copy in copies:
+    first_load.start()
+    for copy in loads:
         copy.start()
+    for copy in small[:5]:
+        copy.wait()
     xs[...] = x_ref[...].astype(F32)
     tables_f = (left_ref[...], right_ref[...], tc_ref[...], ts_ref[...])
-    tables_i = (back_ref[...], inv_ref[...], tc_ref[...], ts_ref[...])
     pairs = range(CHANNELS // 2)
 
     def signal(kind, pair):
@@ -297,7 +313,7 @@
 
     def emit(kind, pair, value):
         for j in range(2):
-            ys[pl.ds(kind * CHANNELS + 2 * pair + j, HALF_ROWS, stride=SEND), :] = value[
+            ys[pl.ds(kind * CHANNELS + 2 * pair + j, HALF_ROWS, stride=DATA), :] = value[
                 :, j * RADIX : (j + 1) * RADIX
             ]
 
@@ -309,6 +325,10 @@
         sv[rows(p), :] = forward_pair(signal(0, p).astype(BF16), *tables_f)
     for p in pairs:
         sg2[rows(p), :] = forward_pair(signal(2, p).astype(BF16), *tables_f)
+    first_load.wait()
+    for copy in small[5:]:
+        copy.wait()
+    tables_i = (back_ref[...], inv_ref[...], tc_ref[...], ts_ref[...])
     for p in pairs:
         conv[:, lanes(p)] = inverse_pair(spectral_product(spec[0, rows(p), :], sv[rows(p), :], 1, 1), *tables_i)
     for p in pairs:
@@ -328,19 +348,28 @@
         emit(0, p, inverse_pair(spectral_product(spec[1, rows(p), :], sz[rows(p), :], 1, 1), *tables_i))
     for p in pairs:
         emit(2, p, inverse_pair(spectral_product(spec[0, rows(p), :], sg1[rows(p), :], -1, 1), *tables_i))
-    for copy in copies:
+    for i in range(HALF_ROWS):
+        data[i] = ys[i * DATA : (i + 1) * DATA, :].astype(BF16)
+    stores = [pltpu.make_async_copy(data, y_hbm.at[:, pl.ds(0, DATA), :], sems.at[4])]
+    stores[0].start()
+
+    span = 256
+    columns = [slice(i * span, (i + 1) * span) for i in range(SEQLEN // span)]
+    wide_rate = jnp.concatenate([rate_ref[...]] * (span // RADIX), axis=1)
+    for cols in columns:
+        first = cols.start // RADIX
+        wide = jnp.concatenate([dh[(first + i) * ROWS : (first + i + 1) * ROWS, :] for i in range(span // RADIX)], axis=1)
+        grad = wide * (jnp.exp(-wide_rate * ramp_ref[:, cols]) * (1.0 / SEQLEN))
+        stat[2 * WIDTH :, cols] = grad.astype(BF16)
+    for copy in loads:
         copy.wait()
-
-    acc[...] = jnp.zeros_like(acc)
-    per = CHUNK // RADIX
-    wide_rate = jnp.concatenate([rate_ref[...]] * per, axis=1)
-    for step in range(SEQLEN // CHUNK):
-        cols = slice(step * CHUNK, (step + 1) * CHUNK)
-        wide = jnp.concatenate([dh[(step * per + i) * ROWS : (step * per + i + 1) * ROWS, :] for i in range(per)], axis=1)
-        grad = (wide * (jnp.exp(-wide_rate * ramp_ref[:, cols]) * (1.0 / SEQLEN))).astype(BF16)
-        low_two = (dot(own_ref[:WIDTH, :ROWS], grad) * cos[WIDTH:, cols].astype(F32)).astype(BF16)
-        low_one = (dot(own_ref[WIDTH:, :WIDTH], low_two) * cos[:WIDTH, cols].astype(F32)).astype(BF16)
-        acc[...] += dot_last(act[:, cols], jnp.concatenate([low_two, low_one, grad], axis=0))
+    for cols in columns:
+        stat[:WIDTH, cols] = (dot(own_ref[:WIDTH, :ROWS], stat[2 * WIDTH :, cols]) * cos[WIDTH:, cols].astype(F32)).astype(BF16)
+    for cols in columns:
+        stat[WIDTH : 2 * WIDTH, cols] = (
+            dot(own_ref[WIDTH:, :WIDTH], stat[:WIDTH, cols]) * cos[:WIDTH, cols].astype(F32)
+        ).astype(BF16)
+    acc[...] = dot_last(act[...], stat[...])
     out_ref[...] = acc[WIDTH : 2 * WIDTH, 2 * WIDTH :].T
     tail = 2 * WIDTH
     share[...] = jnp.zeros_like(share)
@@ -349,8 +378,11 @@
     share[PE_BLOCK : PE_BLOCK + 8, WIDTH:] = acc[tail + 32 :, :WIDTH]
     for i in range(HALF_ROWS):
         group = i % 8
-        ys[i * SEND + DATA : (i + 1) * SEND, :] = share[group * SHARE : (group + 1) * SHARE, :]
-    y_ref[...] = ys[...].astype(BF16)
+        parts[i] = share[group * SHARE : (group + 1) * SHARE, :].astype(BF16)
+    stores.append(pltpu.make_async_copy(parts, y_hbm.at[:, pl.ds(DATA, SHARE), :], sems.at[5]))
+    stores[1].start()
+    for copy in stores:
+        copy.wait()
 
 
 def total_kernel(back_hbm, out_ref, shares, sem):
@@ -390,7 +422,8 @@
         in_specs=[anywhere] * 4,
         out_specs=anywhere,
         out_shape=jax.ShapeDtypeStruct((value.shape[0], DATA, RADIX), BF16),
-        scratch_shapes=[buffer] * 4 + [pltpu.VMEM((value.shape[0], DATA, RADIX), BF16), pltpu.SemaphoreType.DMA((5,))],
+        scratch_shapes=[buffer] * 2
+        + [pltpu.VMEM((value.shape[0], DATA, RADIX), BF16), pltpu.SemaphoreType.DMA((5 * PACK_PARTS,))],
         compiler_params=params(),
         cost_estimate=pl.CostEstimate(flops=1 << 17, bytes_accessed=1 << 20, transcendentals=0),
     )(value, first, second, cot)
@@ -436,30 +469,36 @@
     spectrum = pltpu.VMEM((CHANNELS * KROWS, 2 * RADIX), F32)
     wide = pltpu.VMEM((HALF_ROWS, CHANNELS * RADIX), F32)
     tall = 2 * WIDTH + PE_BLOCK
+    small = (x, left, back, right, right_inv, twid_cos, twid_sin, own, own_rate, ramp)
     anywhere = pl.BlockSpec(memory_space=pltpu.HBM)
     within = pl.BlockSpec(memory_space=pltpu.VMEM)
     return pl.pallas_call(
         chain_kernel,
-        in_specs=[within] * 11 + [anywhere] * 3,
-        out_specs=[within] * 2,
+        in_specs=[anywhere] * 14,
+        out_specs=[anywhere, within],
         out_shape=[
-            jax.ShapeDtypeStruct((HALF_ROWS * SEND, RADIX), BF16),
+            jax.ShapeDtypeStruct((HALF_ROWS, SEND, RADIX), BF16),
             jax.ShapeDtypeStruct((ROWS, WIDTH), F32),
         ],
-        scratch_shapes=[pltpu.VMEM(x.shape, F32), pltpu.VMEM((HALF_ROWS * SEND, RADIX), F32)]
+        scratch_shapes=[pltpu.VMEM(a.shape, a.dtype) for a in small]
+        + [pltpu.VMEM(x.shape, F32)] * 2
         + [spectrum] * 4
         + [wide] * 2
         + [
             pltpu.VMEM((HALF_ROWS * ROWS, RADIX), F32),
+            pltpu.VMEM(spec.shape, F32),
             pltpu.VMEM((tall, SEQLEN), BF16),
             pltpu.VMEM((2 * WIDTH, SEQLEN), BF16),
+            pltpu.VMEM((2 * WIDTH + ROWS, SEQLEN), BF16),
             pltpu.VMEM((tall, 2 * WIDTH + ROWS), F32),
             pltpu.VMEM((WIDTH, RADIX), F32),
-            pltpu.SemaphoreType.DMA((3,)),
+            pltpu.VMEM((HALF_ROWS, DATA, RADIX), BF16),
+            pltpu.VMEM((HALF_ROWS, SHARE, RADIX), BF16),
+            pltpu.SemaphoreType.DMA((6 + len(small),)),
         ],
         compiler_params=params(CHAIN_BYTES),
         cost_estimate=pl.CostEstimate(flops=3 << 30, bytes_accessed=8 << 20, transcendentals=1 << 17),
-    )(x, left, back, right, right_inv, twid_cos, twid_sin, own, own_rate, ramp, spec, act, cos, tail)
+    )(*small, spec, act, cos, tail)
 
 
 def share_total(back, peers):
@@ -526,7 +565,7 @@
         pos_weight, pos_bias, mid_weight, mid_bias, out_weight, decay_rates, tables, stack, ramp
     )
     y, out_weight_grad = chain(x.reshape(HALF_ROWS * DATA, RADIX), net, tables, tail, ramp)
-    back = lax.all_to_all(y.reshape(devices, SEND, RADIX), SEQ, 0, 0, tiled=True)
+    back = lax.all_to_all(y, SEQ, 0, 0, tiled=True)
     total = share_total(back, lax.axis_size(NEAR))
     total = lax.all_to_all(total, NEAR, 0, 0, tiled=True)
     value_grad, first_grad, second_grad = finish(back, cot)

time: 90.5 us -> 89.6 us (0.990)
  Pallas kernels: 25.3 us -> 24.3 us
where the time goes in v5:
time: 89.6 us; the launch traced here: 88.3 us
  blocking collectives  27 us (30%)
  Pallas kernels  24.3 us (27%)
  starting transfers between devices  24.1 us (27%)
  waiting for transfers between devices  12.3 us (14%)
    all_to_all x1, blocking collectives, on_device(): back = lax.all_to_all(y, SEQ, 0, 0, tiled=True)  27 us
    all_to_all x1, starting transfers between devices, on_device(): x = lax.all_to_all(sent, SEQ, 0, 0, tiled=True)  19.2 us
    all_to_all x1, waiting for transfers between devices, on_device(): x = lax.all_to_all(sent, SEQ, 0, 0, tiled=True)  9.73 us
    pallas_call x1, Pallas kernels, network_forward(): pl.pallas_call(network_kernel, grid=(SEQLEN // NET_CHUNK,), in_specs=[blo...  9.39 us
    pallas_call x1, Pallas kernels, chain(): pl.pallas_call(chain_kernel, in_specs=[anywhere] * 14, out_specs=[anywher...  8.22 us
    all_to_all x1, starting transfers between devices, on_device(): total = lax.all_to_all(total, NEAR, 0, 0, tiled=True)  4.93 us
    all_to_all x1, waiting for transfers between devices, on_device(): total = lax.all_to_all(total, NEAR, 0, 0, tiled=True)  2.53 us
    pallas_call x1, Pallas kernels, pack(): pl.pallas_call(pack_kernel, in_specs=[anywhere] * 4, out_specs=anywhere,...  1.85 us
  transfers between devices with their start and end apart: 2, of which 2 were waited for; matrix products, arithmetic and copies ran while one was open for 0% of the time, Pallas kernels for 13%

profile of v5, /device:TPU:6, one launch (start us, length us, event | category | flops | bytes accessed | tf_op | source)
XLA Modules:
  0.0 88.3 jit_solution(18039344014214619236)
XLA Ops:
  0.6 1.8 %shard_map.242 = bf16[64,24,128]{2,1,0:T(8,128)(2,1)} custom-call(bf16[64,8,128]{2,1,0:T(8,128)(2,1)} %bitcast.19, bf16[64,8,128]{2,1,0:T(8,128)(2,1)} %bitcast.20, bf16[64,8,128]{2,1,0:T(8,128)(2,1)} %bitcast.21, bf16[64,8,128]{2,1,0:T(8,128)(2,1)} %bitcast.17), custom_call_target="tpu_custom_call" | custom-call | flops 131072 | bytes 1048576 | tf_op jit(solution)/shard_map/pallas_call | solution.py:420
  2.5 19.2 %all-to-all-start = ((bf16[64,24,128]{2,1,0:T(8,128)(2,1)}), bf16[64,24,128]{2,1,0:T(8,128)(2,1)}, u32[]{:S(2)}, u32[]{:S(2)}) async-start(bf16[64,24,128]{2,1,0:T(8,128)(2,1)} %shard_map.242), calls=%async_computation | async-start | bytes 786432 | tf_op jit(solution)/shard_map/all_to_all | solution.py:563
  21.7 9.4 %shard_map.243 = (bf16[128,8192]{1,0:T(8,128)(2,1)}, bf16[128,8192]{1,0:T(8,128)(2,1)}, f32[2,576,256]{2,1,0:T(8,128)}, bf16[128,128]{1,0:T(8,128)(2,1)}, f32[16,128]{1,0:T(8,128)}) custom-call(bf16[128,8192]{1,0:T(8,128)(2,1)} %constant.18.clone.pe_ref, f32[1,8192]{1,0:T(1,128)} %constant.19.clone.ramp_ref.ramp_hbm, ...), custom_call_target="tpu_custom_call" | custom-call | flops 1073741824 | bytes 10485760 | tf_op jit(solution)/shard_map/pallas_call | solution.py:444
  31.1 9.7 %all-to-all-done = bf16[64,24,128]{2,1,0:T(8,128)(2,1)} async-done(((bf16[64,24,128]{2,1,0:T(8,128)(2,1)}), bf16[64,24,128]{2,1,0:T(8,128)(2,1)}, u32[]{:S(2)}, u32[]{:S(2)}) %all-to-all-start) | async-done | bytes 393248 | tf_op jit(solution)/shard_map/all_to_all | solution.py:563
  40.8 8.2 %shard_map.244 = (bf16[64,32,128]{2,1,0:T(8,128)(2,1)}, f32[16,64]{1,0:T(8,128)}) custom-call(bf16[1536,128]{1,0:T(8,128)(2,1)} %bitcast.4.x_hbm, bf16[144,64]{1,0:T(8,128)(2,1)} %constant.20.clone.left_ref.left_hbm, bf16[64,144]{1,0:T(8,128)(2,1)} %constant.24.clone.back_hbm, bf16[256,256]{1,0:T(8,128)(2,1)} %constant.21.clone.right_ref.right_hbm, ...), custom_call_target="tpu_custom_call" | custom-call | flops 3221225472 | bytes 8388608 | tf_op jit(solution)/shard_map/pallas_call | solution.py:475
  49.1 27.0 %all_to_all.15.back_ref.back_hbm = bf16[64,32,128]{2,1,0:T(8,128)(2,1)} all-to-all(bf16[64,32,128]{2,1,0:T(8,128)(2,1)} %get-tuple-element.27), channel_id=1, replica_groups=mesh['dp'=8,'z'=2,'yhi'=4,'ylo'=2,'x'=4] {'z','yhi','ylo','x'}, dimensions={0} | all-to-all | bytes 1048576 | tf_op jit(solution)/shard_map/all_to_all | solution.py:568
  76.0 1.6 %shard_map.246 = f32[8,8,128]{2,1,0:T(8,128)} custom-call(bf16[64,32,128]{2,1,0:T(8,128)(2,1)} %all_to_all.15.back_ref.back_hbm), custom_call_target="tpu_custom_call" | custom-call | flops 65536 | bytes 131072 | tf_op jit(solution)/shard_map/pallas_call | solution.py:505
  77.6 4.9 %all-to-all-start.2 = ((f32[8,8,128]{2,1,0:T(8,128)}), f32[8,8,128]{2,1,0:T(8,128)}, u32[]{:S(2)}, u32[]{:S(2)}) async-start(f32[8,8,128]{2,1,0:T(8,128)} %shard_map.246), calls=%async_computation.2 | async-start | bytes 65536 | tf_op jit(solution)/shard_map/all_to_all | solution.py:570
  82.6 1.8 %shard_map.245 = (bf16[64,8,128]{2,1,0:T(8,128)(2,1)}, bf16[64,8,128]{2,1,0:T(8,128)(2,1)}, bf16[64,8,128]{2,1,0:T(8,128)(2,1)}) custom-call(bf16[64,32,128]{2,1,0:T(8,128)(2,1)} %all_to_all.15.back_ref.back_hbm, bf16[64,8,128]{2,1,0:T(8,128)(2,1)} %bitcast.18), custom_call_target="tpu_custom_call" | custom-call | flops 131072 | bytes 1048576 | tf_op jit(solution)/shard_map/pallas_call | solution.py:520
  84.3 2.5 %all-to-all-done.2 = f32[8,8,128]{2,1,0:T(8,128)} async-done(((f32[8,8,128]{2,1,0:T(8,128)}), f32[8,8,128]{2,1,0:T(8,128)}, u32[]{:S(2)}, u32[]{:S(2)}) %all-to-all-start.2) | async-done | bytes 32800 | tf_op jit(solution)/shard_map/all_to_all | solution.py:570
  86.9 1.5 %shard_map.247 = (f32[33,64]{1,0:T(8,128)}, f32[1,64]{1,0:T(1,128)}, f32[64,64]{1,0:T(8,128)}, f32[1,64]{1,0:T(1,128)}) custom-call(f32[64,128]{1,0:T(8,128)} %bitcast.13.total_ref), custom_call_target="tpu_custom_call" | custom-call | flops 8192 | bytes 65536 | tf_op jit(solution)/shard_map/pallas_call | solution.py:533
Async XLA Ops:
  2.5 38.3 %all-to-all-start = ((bf16[64,24,128]{2,1,0:T(8,128)(2,1)}), bf16[64,24,128]{2,1,0:T(8,128)(2,1)}, u32[]{:S(2)}, u32[]{:S(2)}) async-start(bf16[64,24,128]{2,1,0:T(8,128)(2,1)} %shard_map.242), calls=%async_computation | async-start | bytes 786432 | tf_op jit(solution)/shard_map/all_to_all | solution.py:563
  77.6 9.2 %all-to-all-start.2 = ((f32[8,8,128]{2,1,0:T(8,128)}), f32[8,8,128]{2,1,0:T(8,128)}, u32[]{:S(2)}, u32[]{:S(2)}) async-start(f32[8,8,128]{2,1,0:T(8,128)} %shard_map.246), calls=%async_computation.2 | async-start | bytes 65536 | tf_op jit(solution)/shard_map/all_to_all | solution.py:570

commit v6 on v5

--- a/solution.py
+++ b/solution.py
@@ -24,6 +24,7 @@
 SHARE = 8
 DATA = 3 * CHANNELS
 SEND = DATA + SHARE
+PEERS = 8
 PACK_PARTS = 2
 VMEM_BYTES = 64 << 20
 CHAIN_BYTES = 64 << 20
@@ -276,13 +277,13 @@
 def chain_kernel(
     x_hbm, left_hbm, back_hbm, right_hbm, inv_hbm, tc_hbm, ts_hbm, own_hbm, rate_hbm, ramp_hbm,
     spec_hbm, act_hbm, cos_hbm, tail_hbm,
-    y_hbm, out_ref,
+    share_ref, out_ref, sz_hbm, sg1_hbm, prod_hbm,
     x_ref, left_ref, back_ref, right_ref, inv_ref, tc_ref, ts_ref, own_ref, rate_ref, ramp_ref,
-    xs, ys, sv, sg2, sz, sg1, conv, dz, dh, spec, act, cos, stat, acc, share, data, parts, sems,
+    xs, sv, sg2, sz, sg1, conv, dz, prod, dh, spec, act, cos, stat, acc, sems,
 ):
     sources = (x_hbm, left_hbm, right_hbm, tc_hbm, ts_hbm, back_hbm, inv_hbm, own_hbm, rate_hbm, ramp_hbm)
     targets = (x_ref, left_ref, right_ref, tc_ref, ts_ref, back_ref, inv_ref, own_ref, rate_ref, ramp_ref)
-    small = [pltpu.make_async_copy(s, d, sems.at[6 + i]) for i, (s, d) in enumerate(zip(sources, targets))]
+    small = [pltpu.make_async_copy(s, d, sems.at[7 + i]) for i, (s, d) in enumerate(zip(sources, targets))]
     for copy in small:
         copy.start()
     first_load = pltpu.make_async_copy(spec_hbm, spec, sems.at[0])
@@ -311,12 +312,6 @@
     def lanes(pair):
         return slice(pair * 2 * RADIX, (pair + 1) * 2 * RADIX)
 
-    def emit(kind, pair, value):
-        for j in range(2):
-            ys[pl.ds(kind * CHANNELS + 2 * pair + j, HALF_ROWS, stride=DATA), :] = value[
-                :, j * RADIX : (j + 1) * RADIX
-            ]
-
     def emit_filter(o, pair, value):
         for j in range(2):
             dh[pl.ds(2 * (2 * pair + j) + o, HALF_ROWS, stride=ROWS), :] = value[:, j * RADIX : (j + 1) * RADIX]
@@ -337,21 +332,20 @@
         gated = (signal(1, p) * conv[:, lanes(p)]).astype(BF16)
         sz[rows(p), :] = forward_pair(gated, *tables_f)
     for p in pairs:
-        emit(1, p, dz[:, lanes(p)] * conv[:, lanes(p)])
+        prod[:, lanes(p)] = (dz[:, lanes(p)] * conv[:, lanes(p)]).astype(BF16)
         grad = (dz[:, lanes(p)] * signal(1, p)).astype(BF16)
         sg1[rows(p), :] = forward_pair(grad, *tables_f)
+    stores = [
+        pltpu.make_async_copy(sz, sz_hbm, sems.at[4]),
+        pltpu.make_async_copy(sg1, sg1_hbm, sems.at[5]),
+        pltpu.make_async_copy(prod, prod_hbm, sems.at[6]),
+    ]
+    for copy in stores:
+        copy.start()
     for p in pairs:
         emit_filter(1, p, inverse_pair(spectral_product(sg2[rows(p), :], sz[rows(p), :], 1, -1), *tables_i))
     for p in pairs:
         emit_filter(0, p, inverse_pair(spectral_product(sg1[rows(p), :], sv[rows(p), :], 1, -1), *tables_i))
-    for p in pairs:
-        emit(0, p, inverse_pair(spectral_product(spec[1, rows(p), :], sz[rows(p), :], 1, 1), *tables_i))
-    for p in pairs:
-        emit(2, p, inverse_pair(spectral_product(spec[0, rows(p), :], sg1[rows(p), :], -1, 1), *tables_i))
-    for i in range(HALF_ROWS):
-        data[i] = ys[i * DATA : (i + 1) * DATA, :].astype(BF16)
-    stores = [pltpu.make_async_copy(data, y_hbm.at[:, pl.ds(0, DATA), :], sems.at[4])]
-    stores[0].start()
 
     span = 256
     columns = [slice(i * span, (i + 1) * span) for i in range(SEQLEN // span)]
@@ -372,38 +366,80 @@
     acc[...] = dot_last(act[...], stat[...])
     out_ref[...] = acc[WIDTH : 2 * WIDTH, 2 * WIDTH :].T
     tail = 2 * WIDTH
-    share[...] = jnp.zeros_like(share)
-    share[:, :WIDTH] = acc[:WIDTH, :WIDTH]
-    share[:PE_BLOCK, WIDTH:] = acc[tail:, WIDTH : 2 * WIDTH]
-    share[PE_BLOCK : PE_BLOCK + 8, WIDTH:] = acc[tail + 32 :, :WIDTH]
-    for i in range(HALF_ROWS):
-        group = i % 8
-        parts[i] = share[group * SHARE : (group + 1) * SHARE, :].astype(BF16)
-    stores.append(pltpu.make_async_copy(parts, y_hbm.at[:, pl.ds(DATA, SHARE), :], sems.at[5]))
-    stores[1].start()
+    share_ref[...] = jnp.zeros_like(share_ref)
+    share_ref[:, :WIDTH] = acc[:WIDTH, :WIDTH]
+    share_ref[:PE_BLOCK, WIDTH:] = acc[tail:, WIDTH : 2 * WIDTH]
+    share_ref[PE_BLOCK : PE_BLOCK + 8, WIDTH:] = acc[tail + 32 :, :WIDTH]
     for copy in stores:
         copy.wait()
 
 
-def total_kernel(back_hbm, out_ref, shares, sem):
-    copy = pltpu.make_async_copy(back_hbm.at[:, pl.ds(DATA, SHARE), :], shares, sem)
+def output_kernel(
+    spec_hbm, sz_hbm, sg1_hbm, prod_hbm, back_hbm, inv_hbm, tc_hbm, ts_hbm,
+    y_hbm,
+    spec, sz, sg1, prod, back_ref, inv_ref, tc_ref, ts_ref, ys, data, sems,
+):
+    sources = (spec_hbm, sz_hbm, sg1_hbm, prod_hbm, back_hbm, inv_hbm, tc_hbm, ts_hbm)
+    targets = (spec, sz, sg1, prod, back_ref, inv_ref, tc_ref, ts_ref)
+    loads = [pltpu.make_async_copy(s, d, sems.at[i]) for i, (s, d) in enumerate(zip(sources, targets))]
+    for copy in loads:
+        copy.start()
+    for copy in loads:
+        copy.wait()
+    tables_i = (back_ref[...], inv_ref[...], tc_ref[...], ts_ref[...])
+
+    def emit(kind, pair, value):
+        for j in range(2):
+            ys[pl.ds(kind * CHANNELS + 2 * pair + j, HALF_ROWS, stride=DATA), :] = value[
+                :, j * RADIX : (j + 1) * RADIX
+            ]
+
+    for p in range(CHANNELS // 2):
+        rows = slice(p * 2 * KROWS, (p + 1) * 2 * KROWS)
+        emit(0, p, inverse_pair(spectral_product(spec[1, rows, :], sz[rows, :], 1, 1), *tables_i))
+    for p in range(CHANNELS // 2):
+        rows = slice(p * 2 * KROWS, (p + 1) * 2 * KROWS)
+        emit(2, p, inverse_pair(spectral_product(spec[0, rows, :], sg1[rows, :], -1, 1), *tables_i))
+        emit(1, p, prod[:, p * 2 * RADIX : (p + 1) * 2 * RADIX].astype(F32))
+    for i in range(HALF_ROWS):
+        data[i] = ys[i * DATA : (i + 1) * DATA, :].astype(BF16)
+    last = pltpu.make_async_copy(data, y_hbm.at[:, pl.ds(0, DATA), :], sems.at[8])
+    last.start()
+    last.wait()
+
+
+def total_kernel(y_in, near_ref, y_out, parts, sem):
+    total = jnp.sum(near_ref[...], axis=0).astype(BF16)
+    parts[...] = jnp.broadcast_to(total[None], parts.shape)
+    copy = pltpu.make_async_copy(parts, y_out.at[:, pl.ds(DATA, SHARE), :], sem)
     copy.start()
     copy.wait()
-    total = jnp.sum(shares[...].astype(F32), axis=0)
-    out_ref[...] = jnp.broadcast_to(total[None], out_ref.shape)
-
-
-def finish_kernel(back_ref, cot_ref, value_ref, first_ref, second_ref):
+
+
+def finish_kernel(back_ref, cot_ref, value_ref, first_ref, second_ref, pos_ref, pos_bias_ref, mid_ref, mid_bias_ref, total):
+    step = pl.program_id(0)
     value_ref[...] = back_ref[:, 2 * CHANNELS : DATA, :]
     first_ref[...] = back_ref[:, CHANNELS : 2 * CHANNELS, :]
     second_ref[...] = (cot_ref[...].astype(F32) * back_ref[:, :CHANNELS, :].astype(F32)).astype(BF16)
-
-
-def inner_kernel(total_ref, pos_ref, pos_bias_ref, mid_ref, mid_bias_ref):
-    mid_ref[...] = total_ref[...].T[:WIDTH, :]
-    pos_ref[...] = total_ref[:PE, WIDTH:]
-    pos_bias_ref[...] = total_ref[PE : PE + 1, WIDTH:]
-    mid_bias_ref[...] = total_ref[PE_BLOCK + 1 : PE_BLOCK + 2, WIDTH:]
+    part = jnp.zeros(total.shape, F32)
+    for i in range(back_ref.shape[0] // PEERS):
+        part = part + back_ref[i * PEERS : (i + 1) * PEERS, DATA:, :].astype(F32)
+
+    @pl.when(step == 0)
+    def _():
+        total[...] = part
+
+    @pl.when(step > 0)
+    def _():
+        total[...] += part
+
+    @pl.when(step == pl.num_programs(0) - 1)
+    def _():
+        whole = jnp.concatenate([total[j] for j in range(PEERS)], axis=0)
+        mid_ref[...] = whole.T[:WIDTH, :]
+        pos_ref[...] = whole[:PE, WIDTH:]
+        pos_bias_ref[...] = whole[PE : PE + 1, WIDTH:]
+        mid_bias_ref[...] = whole[PE_BLOCK + 1 : PE_BLOCK + 2, WIDTH:]
 
 
 def full(shape):
@@ -475,74 +511,87 @@
     return pl.pallas_call(
         chain_kernel,
         in_specs=[anywhere] * 14,
-        out_specs=[anywhere, within],
+        out_specs=[within] * 2 + [anywhere] * 3,
         out_shape=[
-            jax.ShapeDtypeStruct((HALF_ROWS, SEND, RADIX), BF16),
+            jax.ShapeDtypeStruct((WIDTH, RADIX), F32),
             jax.ShapeDtypeStruct((ROWS, WIDTH), F32),
+            jax.ShapeDtypeStruct((CHANNELS * KROWS, 2 * RADIX), F32),
+            jax.ShapeDtypeStruct((CHANNELS * KROWS, 2 * RADIX), F32),
+            jax.ShapeDtypeStruct((HALF_ROWS, CHANNELS * RADIX), BF16),
         ],
         scratch_shapes=[pltpu.VMEM(a.shape, a.dtype) for a in small]
-        + [pltpu.VMEM(x.shape, F32)] * 2
+        + [pltpu.VMEM(x.shape, F32)]
         + [spectrum] * 4
         + [wide] * 2
         + [
+            pltpu.VMEM((HALF_ROWS, CHANNELS * RADIX), BF16),
             pltpu.VMEM((HALF_ROWS * ROWS, RADIX), F32),
             pltpu.VMEM(spec.shape, F32),
             pltpu.VMEM((tall, SEQLEN), BF16),
             pltpu.VMEM((2 * WIDTH, SEQLEN), BF16),
             pltpu.VMEM((2 * WIDTH + ROWS, SEQLEN), BF16),
             pltpu.VMEM((tall, 2 * WIDTH + ROWS), F32),
-            pltpu.VMEM((WIDTH, RADIX), F32),
-            pltpu.VMEM((HALF_ROWS, DATA, RADIX), BF16),
-            pltpu.VMEM((HALF_ROWS, SHARE, RADIX), BF16),
-            pltpu.SemaphoreType.DMA((6 + len(small),)),
+            pltpu.SemaphoreType.DMA((7 + len(small),)),
         ],
         compiler_params=params(CHAIN_BYTES),
         cost_estimate=pl.CostEstimate(flops=3 << 30, bytes_accessed=8 << 20, transcendentals=1 << 17),
     )(*small, spec, act, cos, tail)
 
 
-def share_total(back, peers):
+def outputs(spec, sz, sg1, prod, tables):
+    left, back, right, right_inv, twid_cos, twid_sin = tables
+    anywhere = pl.BlockSpec(memory_space=pltpu.HBM)
+    args = (spec, sz, sg1, prod, back, right_inv, twid_cos, twid_sin)
+    return pl.pallas_call(
+        output_kernel,
+        in_specs=[anywhere] * len(args),
+        out_specs=anywhere,
+        out_shape=jax.ShapeDtypeStruct((HALF_ROWS, SEND, RADIX), BF16),
+        scratch_shapes=[pltpu.VMEM(a.shape, a.dtype) for a in args]
+        + [
+            pltpu.VMEM((HALF_ROWS * DATA, RADIX), F32),
+            pltpu.VMEM((HALF_ROWS, DATA, RADIX), BF16),
+            pltpu.SemaphoreType.DMA((len(args) + 1,)),
+        ],
+        compiler_params=params(),
+        cost_estimate=pl.CostEstimate(flops=1 << 29, bytes_accessed=4 << 20, transcendentals=0),
+    )(*args)
+
+
+def add_total(y, near):
+    anywhere = pl.BlockSpec(memory_space=pltpu.HBM)
     return pl.pallas_call(
         total_kernel,
-        in_specs=[pl.BlockSpec(memory_space=pltpu.HBM)],
-        out_specs=pl.BlockSpec(memory_space=pltpu.VMEM),
-        out_shape=jax.ShapeDtypeStruct((peers, SHARE, RADIX), F32),
-        scratch_shapes=[pltpu.VMEM((back.shape[0], SHARE, RADIX), BF16), pltpu.SemaphoreType.DMA(())],
+        in_specs=[anywhere, pl.BlockSpec(memory_space=pltpu.VMEM)],
+        out_specs=anywhere,
+        out_shape=jax.ShapeDtypeStruct(y.shape, BF16),
+        input_output_aliases={0: 0},
+        scratch_shapes=[pltpu.VMEM((y.shape[0], SHARE, RADIX), BF16), pltpu.SemaphoreType.DMA(())],
         compiler_params=params(),
         cost_estimate=pl.CostEstimate(flops=1 << 16, bytes_accessed=1 << 17, transcendentals=0),
-    )(back)
+    )(y, near)
 
 
 def finish(back, cot):
     devices = cot.shape[0]
     steps = 2
     data = pl.BlockSpec((devices // steps, CHANNELS, RADIX), lambda i: (i, 0, 0))
+    outs = [jax.ShapeDtypeStruct(cot.shape, BF16)] * 3 + [
+        jax.ShapeDtypeStruct((PE, WIDTH), F32),
+        jax.ShapeDtypeStruct((1, WIDTH), F32),
+        jax.ShapeDtypeStruct((WIDTH, WIDTH), F32),
+        jax.ShapeDtypeStruct((1, WIDTH), F32),
+    ]
     return pl.pallas_call(
         finish_kernel,
         grid=(steps,),
         in_specs=[pl.BlockSpec((devices // steps, SEND, RADIX), lambda i: (i, 0, 0)), data],
-        out_specs=[data] * 3,
-        out_shape=[jax.ShapeDtypeStruct(cot.shape, BF16)] * 3,
+        out_specs=[data] * 3 + [full(o.shape) for o in outs[3:]],
+        out_shape=outs,
+        scratch_shapes=[pltpu.VMEM((PEERS, SHARE, RADIX), F32)],
         compiler_params=params(),
-        cost_estimate=pl.CostEstimate(flops=1 << 17, bytes_accessed=1 << 20, transcendentals=0),
+        cost_estimate=pl.CostEstimate(flops=1 << 20, bytes_accessed=1 << 20, transcendentals=0),
     )(back, cot)
-
-
-def inner_gradients(total):
-    within = pl.BlockSpec(memory_space=pltpu.VMEM)
-    return pl.pallas_call(
-        inner_kernel,
-        in_specs=[within],
-        out_specs=[within] * 4,
-        out_shape=[
-            jax.ShapeDtypeStruct((PE, WIDTH), F32),
-            jax.ShapeDtypeStruct((1, WIDTH), F32),
-            jax.ShapeDtypeStruct((WIDTH, WIDTH), F32),
-            jax.ShapeDtypeStruct((1, WIDTH), F32),
-        ],
-        compiler_params=params(2 << 20),
-        cost_estimate=pl.CostEstimate(flops=1 << 13, bytes_accessed=1 << 16, transcendentals=0),
-    )(total)
 
 
 SEQ = ("z", "yhi", "ylo", "x")
@@ -564,12 +613,11 @@
     net = network_forward(
         pos_weight, pos_bias, mid_weight, mid_bias, out_weight, decay_rates, tables, stack, ramp
     )
-    y, out_weight_grad = chain(x.reshape(HALF_ROWS * DATA, RADIX), net, tables, tail, ramp)
-    back = lax.all_to_all(y, SEQ, 0, 0, tiled=True)
-    total = share_total(back, lax.axis_size(NEAR))
-    total = lax.all_to_all(total, NEAR, 0, 0, tiled=True)
-    value_grad, first_grad, second_grad = finish(back, cot)
-    pos_grad, pos_bias_grad, mid_grad, mid_bias_grad = inner_gradients(total.reshape(WIDTH, RADIX))
+    share, out_weight_grad, sz, sg1, prod = chain(x.reshape(HALF_ROWS * DATA, RADIX), net, tables, tail, ramp)
+    near = lax.all_to_all(share.reshape(PEERS, SHARE, RADIX), NEAR, 0, 0, tiled=True)
+    y = outputs(net[2], sz, sg1, prod, tables)
+    back = lax.all_to_all(add_total(y, near), SEQ, 0, 0, tiled=True)
+    value_grad, first_grad, second_grad, pos_grad, pos_bias_grad, mid_grad, mid_bias_grad = finish(back, cot)
     shape = value_branch.shape
     return (
         value_grad.reshape(shape),

time: 89.6 us -> 88.4 us (0.987)
  waiting for transfers between devices: 12.3 us -> 10.2 us
    all_to_all x1, waiting for transfers between devices: 2.53 us -> 0.47 us  [on_device(): lax.all_to_all(share.reshape(PEERS, SHARE, RADIX), NEAR, 0, 0, tiled=True)]
  transfers between devices with their start and end apart: 2 -> 2, of which waited for: 2 -> 2; matrix products, arithmetic and copies ran while one was open for 0% -> 0% of each run, Pallas kernels for 13% -> 15%
where the time goes in v6:
time: 88.4 us; the launch traced here: 87.6 us
  blocking collectives  27.6 us (31%)
  Pallas kernels  25 us (28%)
  starting transfers between devices  24.1 us (27%)
  waiting for transfers between devices  10.2 us (12%)
    all_to_all x1, blocking collectives, on_device(): back = lax.all_to_all(add_total(y, near), SEQ, 0, 0, tiled=True)  27.6 us
    all_to_all x1, starting transfers between devices, on_device(): x = lax.all_to_all(sent, SEQ, 0, 0, tiled=True)  19.2 us
    all_to_all x1, waiting for transfers between devices, on_device(): x = lax.all_to_all(sent, SEQ, 0, 0, tiled=True)  9.73 us
    pallas_call x1, Pallas kernels, network_forward(): pl.pallas_call(network_kernel, grid=(SEQLEN // NET_CHUNK,), in_specs=[blo...  9.38 us
    pallas_call x1, Pallas kernels, chain(): pl.pallas_call(chain_kernel, in_specs=[anywhere] * 14, out_specs=[within]...  6.57 us
    all_to_all x1, starting transfers between devices, on_device(): lax.all_to_all(share.reshape(PEERS, SHARE, RADIX), NEAR, 0, 0, tiled=True)  4.89 us
    pallas_call x1, Pallas kernels, outputs(): pl.pallas_call(output_kernel, in_specs=[anywhere] * len(args), out_specs=...  3.82 us
    pallas_call x1, Pallas kernels, finish(): pl.pallas_call(finish_kernel, grid=(steps,), in_specs=[pl.BlockSpec((devi...  1.92 us
  transfers between devices with their start and end apart: 2, of which 2 were waited for; matrix products, arithmetic and copies ran while one was open for 0% of the time, Pallas kernels for 15%

profile of v6, /device:TPU:6, one launch (start us, length us, event | category | flops | bytes accessed | tf_op | source)
XLA Modules:
  0.0 87.6 jit_solution(17918703848282777101)
XLA Ops:
  0.6 1.9 %shard_map.243 = bf16[64,24,128]{2,1,0:T(8,128)(2,1)} custom-call(bf16[64,8,128]{2,1,0:T(8,128)(2,1)} %bitcast.19, bf16[64,8,128]{2,1,0:T(8,128)(2,1)} %bitcast.20, bf16[64,8,128]{2,1,0:T(8,128)(2,1)} %bitcast.21, bf16[64,8,128]{2,1,0:T(8,128)(2,1)} %bitcast.17), custom_call_target="tpu_custom_call" | custom-call | flops 131072 | bytes 1048576 | tf_op jit(solution)/shard_map/pallas_call | solution.py:456
  2.5 19.2 %all-to-all-start = ((bf16[64,24,128]{2,1,0:T(8,128)(2,1)}), bf16[64,24,128]{2,1,0:T(8,128)(2,1)}, u32[]{:S(2)}, u32[]{:S(2)}) async-start(bf16[64,24,128]{2,1,0:T(8,128)(2,1)} %shard_map.243), calls=%async_computation | async-start | bytes 786432 | tf_op jit(solution)/shard_map/all_to_all | solution.py:612
  21.7 9.4 %shard_map.242 = (bf16[128,8192]{1,0:T(8,128)(2,1)}, bf16[128,8192]{1,0:T(8,128)(2,1)}, f32[2,576,256]{2,1,0:T(8,128)}, bf16[128,128]{1,0:T(8,128)(2,1)}, f32[16,128]{1,0:T(8,128)}) custom-call(bf16[128,8192]{1,0:T(8,128)(2,1)} %constant.18.clone.pe_ref, f32[1,8192]{1,0:T(1,128)} %constant.19.clone.ramp_ref.ramp_hbm, ...), custom_call_target="tpu_custom_call" | custom-call | flops 1073741824 | bytes 10485760 | tf_op jit(solution)/shard_map/pallas_call | solution.py:480
  31.1 9.7 %all-to-all-done = bf16[64,24,128]{2,1,0:T(8,128)(2,1)} async-done(((bf16[64,24,128]{2,1,0:T(8,128)(2,1)}), bf16[64,24,128]{2,1,0:T(8,128)(2,1)}, u32[]{:S(2)}, u32[]{:S(2)}) %all-to-all-start) | async-done | bytes 393248 | tf_op jit(solution)/shard_map/all_to_all | solution.py:612
  40.8 6.6 %shard_map.244 = (f32[64,128]{1,0:T(8,128)}, f32[16,64]{1,0:T(8,128)}, f32[576,256]{1,0:T(8,128)}, f32[576,256]{1,0:T(8,128)}, bf16[64,1024]{1,0:T(8,128)(2,1)}) custom-call(bf16[1536,128]{1,0:T(8,128)(2,1)} %bitcast.9.x_hbm, bf16[144,64]{1,0:T(8,128)(2,1)} %constant.20.clone.left_ref.left_hbm, bf16[64,144]{1,0:T(8,128)(2,1)} %constant.24.clone.back_hbm, ...), custom_call_target="tpu_custom_call" | custom-call | flops 3221225472 | bytes 8388608 | tf_op jit(solution)/shard_map/pallas_call | solution.py:511
  47.4 4.9 %all-to-all-start.1 = ((f32[8,8,128]{2,1,0:T(8,128)}), f32[8,8,128]{2,1,0:T(8,128)}, u32[]{:S(2)}, u32[]{:S(2)}) async-start(f32[8,8,128]{2,1,0:T(8,128)} %bitcast.22), calls=%async_computation.1 | async-start | bytes 65536 | tf_op jit(solution)/shard_map/all_to_all | solution.py:617
  52.3 3.8 %shard_map.245.y_in = bf16[64,32,128]{2,1,0:T(8,128)(2,1)} custom-call(f32[2,576,256]{2,1,0:T(8,128)} %get-tuple-element.25.spec_hbm, f32[576,256]{1,0:T(8,128)} %get-tuple-element.30.sz_hbm, f32[576,256]{1,0:T(8,128)} %get-tuple-element.31.sg1_hbm, bf16[64,1024]{1,0:T(8,128)(2,1)} %get-tuple-element.32.prod_hbm, bf16[64,144]{1,0:T(8,128)(2,1)} %constant.24.clone.back_hbm, ...), custom_call_target="tpu_custom_call" | custom-call | flops 536870912 | bytes 4194304 | tf_op jit(solution)/shard_map/pallas_call | solution.py:545
  56.1 0.5 all-to-all-done.1.near_ref
  56.6 1.4 %shard_map.246 = bf16[64,32,128]{2,1,0:T(8,128)(2,1)} custom-call(bf16[64,32,128]{2,1,0:T(8,128)(2,1)} %shard_map.245.y_in, f32[8,8,128]{2,1,0:T(8,128)} %all-to-all-done.1.near_ref), custom_call_target="tpu_custom_call", output_to_operand_aliasing={{}: (0, {})} | custom-call | flops 65536 | bytes 131072 | tf_op jit(solution)/shard_map/pallas_call | solution.py:563
  58.0 27.6 %all_to_all.15.back_ref = bf16[64,32,128]{2,1,0:T(8,128)(2,1)} all-to-all(bf16[64,32,128]{2,1,0:T(8,128)(2,1)} %shard_map.246), channel_id=1, replica_groups=mesh['dp'=8,'z'=2,'yhi'=4,'ylo'=2,'x'=4] {'z','yhi','ylo','x'}, dimensions={0} | all-to-all | bytes 1048576 | tf_op jit(solution)/shard_map/all_to_all | solution.py:619
  85.7 1.9 %shard_map.247 = (bf16[64,8,128]{2,1,0:T(8,128)(2,1)}, bf16[64,8,128]{2,1,0:T(8,128)(2,1)}, bf16[64,8,128]{2,1,0:T(8,128)(2,1)}, f32[33,64]{1,0:T(8,128)}, f32[1...) custom-call(bf16[64,32,128]{2,1,0:T(8,128)(2,1)} %all_to_all.15.back_ref, bf16[64,8,128]{2,1,0:T(8,128)(2,1)} %bitcast.18), custom_call_target="tpu_custom_call" | custom-call | flops 1048576 | bytes 1048576 | tf_op jit(solution)/shard_map/pallas_call | solution.py:585
Async XLA Ops:
  2.5 38.3 %all-to-all-start = ((bf16[64,24,128]{2,1,0:T(8,128)(2,1)}), bf16[64,24,128]{2,1,0:T(8,128)(2,1)}, u32[]{:S(2)}, u32[]{:S(2)}) async-start(bf16[64,24,128]{2,1,0:T(8,128)(2,1)} %shard_map.243), calls=%async_computation | async-start | bytes 786432 | tf_op jit(solution)/shard_map/all_to_all | solution.py:612
  47.4 9.2 %all-to-all-start.1 = ((f32[8,8,128]{2,1,0:T(8,128)}), f32[8,8,128]{2,1,0:T(8,128)}, u32[]{:S(2)}, u32[]{:S(2)}) async-start(f32[8,8,128]{2,1,0:T(8,128)} %bitcast.22), calls=%async_computation.1 | async-start | bytes 65536 | tf_op jit(solution)/shard_map/all_to_all | solution.py:617

commit v7 on v6

--- a/solution.py
+++ b/solution.py
@@ -18,7 +18,7 @@
 WIDTH = 64
 PE = 33
 PE_BLOCK = 40
-NET_CHUNK = 2048
+NET_CHUNK = 8192
 CHANNELS = 8
 ROWS = 2 * CHANNELS
 SHARE = 8
@@ -26,6 +26,8 @@
 SEND = DATA + SHARE
 PEERS = 8
 PACK_PARTS = 2
+ADD_BYTES = 64 << 20
+FIN_BYTES = 64 << 20
 VMEM_BYTES = 64 << 20
 CHAIN_BYTES = 64 << 20
 
@@ -379,12 +381,12 @@
     y_hbm,
     spec, sz, sg1, prod, back_ref, inv_ref, tc_ref, ts_ref, ys, data, sems,
 ):
-    sources = (spec_hbm, sz_hbm, sg1_hbm, prod_hbm, back_hbm, inv_hbm, tc_hbm, ts_hbm)
-    targets = (spec, sz, sg1, prod, back_ref, inv_ref, tc_ref, ts_ref)
+    sources = (spec_hbm.at[1], sz_hbm, inv_hbm, tc_hbm, ts_hbm, back_hbm, spec_hbm.at[0], sg1_hbm, prod_hbm)
+    targets = (spec.at[1], sz, inv_ref, tc_ref, ts_ref, back_ref, spec.at[0], sg1, prod)
     loads = [pltpu.make_async_copy(s, d, sems.at[i]) for i, (s, d) in enumerate(zip(sources, targets))]
     for copy in loads:
         copy.start()
-    for copy in loads:
+    for copy in loads[:6]:
         copy.wait()
     tables_i = (back_ref[...], inv_ref[...], tc_ref[...], ts_ref[...])
 
@@ -397,13 +399,15 @@
     for p in range(CHANNELS // 2):
         rows = slice(p * 2 * KROWS, (p + 1) * 2 * KROWS)
         emit(0, p, inverse_pair(spectral_product(spec[1, rows, :], sz[rows, :], 1, 1), *tables_i))
+    for copy in loads[6:]:
+        copy.wait()
     for p in range(CHANNELS // 2):
         rows = slice(p * 2 * KROWS, (p + 1) * 2 * KROWS)
         emit(2, p, inverse_pair(spectral_product(spec[0, rows, :], sg1[rows, :], -1, 1), *tables_i))
         emit(1, p, prod[:, p * 2 * RADIX : (p + 1) * 2 * RADIX].astype(F32))
     for i in range(HALF_ROWS):
         data[i] = ys[i * DATA : (i + 1) * DATA, :].astype(BF16)
-    last = pltpu.make_async_copy(data, y_hbm.at[:, pl.ds(0, DATA), :], sems.at[8])
+    last = pltpu.make_async_copy(data, y_hbm.at[:, pl.ds(0, DATA), :], sems.at[9])
     last.start()
     last.wait()
 
@@ -551,7 +555,7 @@
         + [
             pltpu.VMEM((HALF_ROWS * DATA, RADIX), F32),
             pltpu.VMEM((HALF_ROWS, DATA, RADIX), BF16),
-            pltpu.SemaphoreType.DMA((len(args) + 1,)),
+            pltpu.SemaphoreType.DMA((len(args) + 2,)),
         ],
         compiler_params=params(),
         cost_estimate=pl.CostEstimate(flops=1 << 29, bytes_accessed=4 << 20, transcendentals=0),
@@ -567,7 +571,7 @@
         out_shape=jax.ShapeDtypeStruct(y.shape, BF16),
         input_output_aliases={0: 0},
         scratch_shapes=[pltpu.VMEM((y.shape[0], SHARE, RADIX), BF16), pltpu.SemaphoreType.DMA(())],
-        compiler_params=params(),
+        compiler_params=params(ADD_BYTES),
         cost_estimate=pl.CostEstimate(flops=1 << 16, bytes_accessed=1 << 17, transcendentals=0),
     )(y, near)
 
@@ -589,7 +593,7 @@
         out_specs=[data] * 3 + [full(o.shape) for o in outs[3:]],
         out_shape=outs,
         scratch_shapes=[pltpu.VMEM((PEERS, SHARE, RADIX), F32)],
-        compiler_params=params(),
+        compiler_params=params(FIN_BYTES),
         cost_estimate=pl.CostEstimate(flops=1 << 20, bytes_accessed=1 << 20, transcendentals=0),
     )(back, cot)
 

time: 88.4 us -> 88.3 us (level)
  no operation moved by 1% of the time
where the time goes in v7:
time: 88.3 us; the launch traced here: 87.5 us
  blocking collectives  27.5 us (31%)
  Pallas kernels  24.5 us (28%)
  starting transfers between devices  24.1 us (27%)
  waiting for transfers between devices  10.6 us (12%)
    all_to_all x1, blocking collectives, on_device(): back = lax.all_to_all(add_total(y, near), SEQ, 0, 0, tiled=True)  27.5 us
    all_to_all x1, starting transfers between devices, on_device(): x = lax.all_to_all(sent, SEQ, 0, 0, tiled=True)  19.2 us
    all_to_all x1, waiting for transfers between devices, on_device(): x = lax.all_to_all(sent, SEQ, 0, 0, tiled=True)  10 us
    pallas_call x1, Pallas kernels, network_forward(): pl.pallas_call(network_kernel, grid=(SEQLEN // NET_CHUNK,), in_specs=[blo...  9.07 us
    pallas_call x1, Pallas kernels, chain(): pl.pallas_call(chain_kernel, in_specs=[anywhere] * 14, out_specs=[within]...  6.57 us
    all_to_all x1, starting transfers between devices, on_device(): lax.all_to_all(share.reshape(PEERS, SHARE, RADIX), NEAR, 0, 0, tiled=True)  4.89 us
    pallas_call x1, Pallas kernels, outputs(): pl.pallas_call(output_kernel, in_specs=[anywhere] * len(args), out_specs=...  3.7 us
    pallas_call x1, Pallas kernels, finish(): pl.pallas_call(finish_kernel, grid=(steps,), in_specs=[pl.BlockSpec((devi...  1.92 us
  transfers between devices with their start and end apart: 2, of which 2 were waited for; matrix products, arithmetic and copies ran while one was open for 0% of the time, Pallas kernels for 15%

profile of v7, /device:TPU:6, one launch (start us, length us, event | category | flops | bytes accessed | tf_op | source)
XLA Modules:
  0.0 87.5 jit_solution(9758277099137134067)
XLA Ops:
  0.6 1.9 %shard_map.243 = bf16[64,24,128]{2,1,0:T(8,128)(2,1)} custom-call(bf16[64,8,128]{2,1,0:T(8,128)(2,1)} %bitcast.19, bf16[64,8,128]{2,1,0:T(8,128)(2,1)} %bitcast.20, bf16[64,8,128]{2,1,0:T(8,128)(2,1)} %bitcast.21, bf16[64,8,128]{2,1,0:T(8,128)(2,1)} %bitcast.17), custom_call_target="tpu_custom_call" | custom-call | flops 131072 | bytes 1048576 | tf_op jit(solution)/shard_map/pallas_call | solution.py:460
  2.5 19.2 %all-to-all-start = ((bf16[64,24,128]{2,1,0:T(8,128)(2,1)}), bf16[64,24,128]{2,1,0:T(8,128)(2,1)}, u32[]{:S(2)}, u32[]{:S(2)}) async-start(bf16[64,24,128]{2,1,0:T(8,128)(2,1)} %shard_map.243), calls=%async_computation | async-start | bytes 786432 | tf_op jit(solution)/shard_map/all_to_all | solution.py:616
  21.7 9.1 %shard_map.242 = (bf16[128,8192]{1,0:T(8,128)(2,1)}, bf16[128,8192]{1,0:T(8,128)(2,1)}, f32[2,576,256]{2,1,0:T(8,128)}, bf16[128,128]{1,0:T(8,128)(2,1)}, f32[16,128]{1,0:T(8,128)}) custom-call(bf16[128,8192]{1,0:T(8,128)(2,1)} %constant.18.clone.pe_ref, f32[1,8192]{1,0:T(1,128)} %constant.19.clone.ramp_ref.ramp_hbm, ...), custom_call_target="tpu_custom_call" | custom-call | flops 1073741824 | bytes 10485760 | tf_op jit(solution)/shard_map/pallas_call | solution.py:484
  30.8 10.0 %all-to-all-done = bf16[64,24,128]{2,1,0:T(8,128)(2,1)} async-done(((bf16[64,24,128]{2,1,0:T(8,128)(2,1)}), bf16[64,24,128]{2,1,0:T(8,128)(2,1)}, u32[]{:S(2)}, u32[]{:S(2)}) %all-to-all-start) | async-done | bytes 393248 | tf_op jit(solution)/shard_map/all_to_all | solution.py:616
  40.8 6.6 %shard_map.244 = (f32[64,128]{1,0:T(8,128)}, f32[16,64]{1,0:T(8,128)}, f32[576,256]{1,0:T(8,128)}, f32[576,256]{1,0:T(8,128)}, bf16[64,1024]{1,0:T(8,128)(2,1)}) custom-call(bf16[1536,128]{1,0:T(8,128)(2,1)} %bitcast.9.x_hbm, bf16[144,64]{1,0:T(8,128)(2,1)} %constant.20.clone.left_ref.left_hbm, bf16[64,144]{1,0:T(8,128)(2,1)} %constant.24.clone.back_hbm, ...), custom_call_target="tpu_custom_call" | custom-call | flops 3221225472 | bytes 8388608 | tf_op jit(solution)/shard_map/pallas_call | solution.py:515
  47.4 4.9 %all-to-all-start.1 = ((f32[8,8,128]{2,1,0:T(8,128)}), f32[8,8,128]{2,1,0:T(8,128)}, u32[]{:S(2)}, u32[]{:S(2)}) async-start(f32[8,8,128]{2,1,0:T(8,128)} %bitcast.22), calls=%async_computation.1 | async-start | bytes 65536 | tf_op jit(solution)/shard_map/all_to_all | solution.py:621
  52.3 3.7 %shard_map.245.y_in = bf16[64,32,128]{2,1,0:T(8,128)(2,1)} custom-call(f32[2,576,256]{2,1,0:T(8,128)} %get-tuple-element.25.spec_hbm, f32[576,256]{1,0:T(8,128)} %get-tuple-element.30.sz_hbm, f32[576,256]{1,0:T(8,128)} %get-tuple-element.31.sg1_hbm, bf16[64,1024]{1,0:T(8,128)(2,1)} %get-tuple-element.32.prod_hbm, bf16[64,144]{1,0:T(8,128)(2,1)} %constant.24.clone.back_hbm, ...), custom_call_target="tpu_custom_call" | custom-call | flops 536870912 | bytes 4194304 | tf_op jit(solution)/shard_map/pallas_call | solution.py:549
  56.0 0.6 all-to-all-done.1.near_ref
  56.6 1.4 %shard_map.246 = bf16[64,32,128]{2,1,0:T(8,128)(2,1)} custom-call(bf16[64,32,128]{2,1,0:T(8,128)(2,1)} %shard_map.245.y_in, f32[8,8,128]{2,1,0:T(8,128)} %all-to-all-done.1.near_ref), custom_call_target="tpu_custom_call", output_to_operand_aliasing={{}: (0, {})} | custom-call | flops 65536 | bytes 131072 | tf_op jit(solution)/shard_map/pallas_call | solution.py:567
  58.0 27.5 %all_to_all.15.back_ref = bf16[64,32,128]{2,1,0:T(8,128)(2,1)} all-to-all(bf16[64,32,128]{2,1,0:T(8,128)(2,1)} %shard_map.246), channel_id=1, replica_groups=mesh['dp'=8,'z'=2,'yhi'=4,'ylo'=2,'x'=4] {'z','yhi','ylo','x'}, dimensions={0} | all-to-all | bytes 1048576 | tf_op jit(solution)/shard_map/all_to_all | solution.py:623
  85.5 1.9 %shard_map.247 = (bf16[64,8,128]{2,1,0:T(8,128)(2,1)}, bf16[64,8,128]{2,1,0:T(8,128)(2,1)}, bf16[64,8,128]{2,1,0:T(8,128)(2,1)}, f32[33,64]{1,0:T(8,128)}, f32[1...) custom-call(bf16[64,32,128]{2,1,0:T(8,128)(2,1)} %all_to_all.15.back_ref, bf16[64,8,128]{2,1,0:T(8,128)(2,1)} %bitcast.18), custom_call_target="tpu_custom_call" | custom-call | flops 1048576 | bytes 1048576 | tf_op jit(solution)/shard_map/pallas_call | solution.py:589
Async XLA Ops:
  2.5 38.3 %all-to-all-start = ((bf16[64,24,128]{2,1,0:T(8,128)(2,1)}), bf16[64,24,128]{2,1,0:T(8,128)(2,1)}, u32[]{:S(2)}, u32[]{:S(2)}) async-start(bf16[64,24,128]{2,1,0:T(8,128)(2,1)} %shard_map.243), calls=%async_computation | async-start | bytes 786432 | tf_op jit(solution)/shard_map/all_to_all | solution.py:616
  47.4 9.2 %all-to-all-start.1 = ((f32[8,8,128]{2,1,0:T(8,128)}), f32[8,8,128]{2,1,0:T(8,128)}, u32[]{:S(2)}, u32[]{:S(2)}) async-start(f32[8,8,128]{2,1,0:T(8,128)} %bitcast.22), calls=%async_computation.1 | async-start | bytes 65536 | tf_op jit(solution)/shard_map/all_to_all | solution.py:621

commit v8 on v7

--- a/solution.py
+++ b/solution.py
@@ -578,7 +578,7 @@
 
 def finish(back, cot):
     devices = cot.shape[0]
-    steps = 2
+    steps = 1
     data = pl.BlockSpec((devices // steps, CHANNELS, RADIX), lambda i: (i, 0, 0))
     outs = [jax.ShapeDtypeStruct(cot.shape, BF16)] * 3 + [
         jax.ShapeDtypeStruct((PE, WIDTH), F32),

time: 88.3 us -> 88.3 us (level)
  no operation moved by 1% of the time
where the time goes in v8:
time: 88.3 us; the launch traced here: 87.4 us
  blocking collectives  27.5 us (31%)
  Pallas kernels  24.5 us (28%)
  starting transfers between devices  24.1 us (27%)
  waiting for transfers between devices  10.6 us (12%)
    all_to_all x1, blocking collectives, on_device(): back = lax.all_to_all(add_total(y, near), SEQ, 0, 0, tiled=True)  27.5 us
    all_to_all x1, starting transfers between devices, on_device(): x = lax.all_to_all(sent, SEQ, 0, 0, tiled=True)  19.2 us
    all_to_all x1, waiting for transfers between devices, on_device(): x = lax.all_to_all(sent, SEQ, 0, 0, tiled=True)  10 us
    pallas_call x1, Pallas kernels, network_forward(): pl.pallas_call(network_kernel, grid=(SEQLEN // NET_CHUNK,), in_specs=[blo...  9.07 us
    pallas_call x1, Pallas kernels, chain(): pl.pallas_call(chain_kernel, in_specs=[anywhere] * 14, out_specs=[within]...  6.57 us
    all_to_all x1, starting transfers between devices, on_device(): lax.all_to_all(share.reshape(PEERS, SHARE, RADIX), NEAR, 0, 0, tiled=True)  4.89 us
    pallas_call x1, Pallas kernels, outputs(): pl.pallas_call(output_kernel, in_specs=[anywhere] * len(args), out_specs=...  3.7 us
    pallas_call x1, Pallas kernels, finish(): pl.pallas_call(finish_kernel, grid=(steps,), in_specs=[pl.BlockSpec((devi...  1.86 us
  transfers between devices with their start and end apart: 2, of which 2 were waited for; matrix products, arithmetic and copies ran while one was open for 0% of the time, Pallas kernels for 15%

profile of v8, /device:TPU:6, one launch (start us, length us, event | category | flops | bytes accessed | tf_op | source)
XLA Modules:
  0.0 87.4 jit_solution(5143837457999862413)
XLA Ops:
  0.6 1.9 %shard_map.243 = bf16[64,24,128]{2,1,0:T(8,128)(2,1)} custom-call(bf16[64,8,128]{2,1,0:T(8,128)(2,1)} %bitcast.19, bf16[64,8,128]{2,1,0:T(8,128)(2,1)} %bitcast.20, bf16[64,8,128]{2,1,0:T(8,128)(2,1)} %bitcast.21, bf16[64,8,128]{2,1,0:T(8,128)(2,1)} %bitcast.17), custom_call_target="tpu_custom_call" | custom-call | flops 131072 | bytes 1048576 | tf_op jit(solution)/shard_map/pallas_call | solution.py:460
  2.5 19.2 %all-to-all-start = ((bf16[64,24,128]{2,1,0:T(8,128)(2,1)}), bf16[64,24,128]{2,1,0:T(8,128)(2,1)}, u32[]{:S(2)}, u32[]{:S(2)}) async-start(bf16[64,24,128]{2,1,0:T(8,128)(2,1)} %shard_map.243), calls=%async_computation | async-start | bytes 786432 | tf_op jit(solution)/shard_map/all_to_all | solution.py:616
  21.7 9.1 %shard_map.242 = (bf16[128,8192]{1,0:T(8,128)(2,1)}, bf16[128,8192]{1,0:T(8,128)(2,1)}, f32[2,576,256]{2,1,0:T(8,128)}, bf16[128,128]{1,0:T(8,128)(2,1)}, f32[16,128]{1,0:T(8,128)}) custom-call(bf16[128,8192]{1,0:T(8,128)(2,1)} %constant.18.clone.pe_ref, f32[1,8192]{1,0:T(1,128)} %constant.19.clone.ramp_ref.ramp_hbm, ...), custom_call_target="tpu_custom_call" | custom-call | flops 1073741824 | bytes 10485760 | tf_op jit(solution)/shard_map/pallas_call | solution.py:484
  30.8 10.0 %all-to-all-done = bf16[64,24,128]{2,1,0:T(8,128)(2,1)} async-done(((bf16[64,24,128]{2,1,0:T(8,128)(2,1)}), bf16[64,24,128]{2,1,0:T(8,128)(2,1)}, u32[]{:S(2)}, u32[]{:S(2)}) %all-to-all-start) | async-done | bytes 393248 | tf_op jit(solution)/shard_map/all_to_all | solution.py:616
  40.8 6.6 %shard_map.244 = (f32[64,128]{1,0:T(8,128)}, f32[16,64]{1,0:T(8,128)}, f32[576,256]{1,0:T(8,128)}, f32[576,256]{1,0:T(8,128)}, bf16[64,1024]{1,0:T(8,128)(2,1)}) custom-call(bf16[1536,128]{1,0:T(8,128)(2,1)} %bitcast.9.x_hbm, bf16[144,64]{1,0:T(8,128)(2,1)} %constant.20.clone.left_ref.left_hbm, bf16[64,144]{1,0:T(8,128)(2,1)} %constant.24.clone.back_hbm, ...), custom_call_target="tpu_custom_call" | custom-call | flops 3221225472 | bytes 8388608 | tf_op jit(solution)/shard_map/pallas_call | solution.py:515
  47.4 4.9 %all-to-all-start.1 = ((f32[8,8,128]{2,1,0:T(8,128)}), f32[8,8,128]{2,1,0:T(8,128)}, u32[]{:S(2)}, u32[]{:S(2)}) async-start(f32[8,8,128]{2,1,0:T(8,128)} %bitcast.22), calls=%async_computation.1 | async-start | bytes 65536 | tf_op jit(solution)/shard_map/all_to_all | solution.py:621
  52.3 3.7 %shard_map.245.y_in = bf16[64,32,128]{2,1,0:T(8,128)(2,1)} custom-call(f32[2,576,256]{2,1,0:T(8,128)} %get-tuple-element.25.spec_hbm, f32[576,256]{1,0:T(8,128)} %get-tuple-element.30.sz_hbm, f32[576,256]{1,0:T(8,128)} %get-tuple-element.31.sg1_hbm, bf16[64,1024]{1,0:T(8,128)(2,1)} %get-tuple-element.32.prod_hbm, bf16[64,144]{1,0:T(8,128)(2,1)} %constant.24.clone.back_hbm, ...), custom_call_target="tpu_custom_call" | custom-call | flops 536870912 | bytes 4194304 | tf_op jit(solution)/shard_map/pallas_call | solution.py:549
  56.0 0.6 all-to-all-done.1.near_ref
  56.6 1.4 %shard_map.246 = bf16[64,32,128]{2,1,0:T(8,128)(2,1)} custom-call(bf16[64,32,128]{2,1,0:T(8,128)(2,1)} %shard_map.245.y_in, f32[8,8,128]{2,1,0:T(8,128)} %all-to-all-done.1.near_ref), custom_call_target="tpu_custom_call", output_to_operand_aliasing={{}: (0, {})} | custom-call | flops 65536 | bytes 131072 | tf_op jit(solution)/shard_map/pallas_call | solution.py:567
  58.0 27.5 %all_to_all.15.back_ref = bf16[64,32,128]{2,1,0:T(8,128)(2,1)} all-to-all(bf16[64,32,128]{2,1,0:T(8,128)(2,1)} %shard_map.246), channel_id=1, replica_groups=mesh['dp'=8,'z'=2,'yhi'=4,'ylo'=2,'x'=4] {'z','yhi','ylo','x'}, dimensions={0} | all-to-all | bytes 1048576 | tf_op jit(solution)/shard_map/all_to_all | solution.py:623
  85.5 1.9 %shard_map.247 = (bf16[64,8,128]{2,1,0:T(8,128)(2,1)}, bf16[64,8,128]{2,1,0:T(8,128)(2,1)}, bf16[64,8,128]{2,1,0:T(8,128)(2,1)}, f32[33,64]{1,0:T(8,128)}, f32[1...) custom-call(bf16[64,32,128]{2,1,0:T(8,128)(2,1)} %all_to_all.15.back_ref, bf16[64,8,128]{2,1,0:T(8,128)(2,1)} %bitcast.18), custom_call_target="tpu_custom_call" | custom-call | flops 1048576 | bytes 1048576 | tf_op jit(solution)/shard_map/pallas_call | solution.py:589
Async XLA Ops:
  2.5 38.3 %all-to-all-start = ((bf16[64,24,128]{2,1,0:T(8,128)(2,1)}), bf16[64,24,128]{2,1,0:T(8,128)(2,1)}, u32[]{:S(2)}, u32[]{:S(2)}) async-start(bf16[64,24,128]{2,1,0:T(8,128)(2,1)} %shard_map.243), calls=%async_computation | async-start | bytes 786432 | tf_op jit(solution)/shard_map/all_to_all | solution.py:616
  47.4 9.2 %all-to-all-start.1 = ((f32[8,8,128]{2,1,0:T(8,128)}), f32[8,8,128]{2,1,0:T(8,128)}, u32[]{:S(2)}, u32[]{:S(2)}) async-start(f32[8,8,128]{2,1,0:T(8,128)} %bitcast.22), calls=%async_computation.1 | async-start | bytes 65536 | tf_op jit(solution)/shard_map/all_to_all | solution.py:621
